TPU v7x, 32 devices: a whole 2x2x4 slice. The times are simulated.
32 devices in a mesh: dp: 4 (over y, core), tm: 8 (over z, x).
Axes of the slice: x: 2, y: 2, z: 4, core: 2. Of those that a mesh axis runs over, the one named last changes fastest.
Arguments:
- query_input: bfloat16 [4, 2048, 512], P('dp', 'tm'), may hold values from -6 to 6
- key_input: bfloat16 [4, 2048, 512], P('dp', 'tm'), may hold values from -6 to 6
- value_input: bfloat16 [4, 2048, 512], P('dp', 'tm'), may hold values from -6 to 6
- query_conv: float32 [4, 512], replicated, may hold values from -3 to 3
- key_conv: float32 [4, 512], replicated, may hold values from -3 to 3
- value_conv: float32 [4, 512], replicated, may hold values from -12 to 12
- log_decay: float32 [4, 2048, 4], P('dp', 'tm'), may hold values from -1 to 0
- write_strength: float32 [4, 2048, 4], P('dp', 'tm'), may hold values from 0.002 to 1
- out_cotangent: bfloat16 [4, 2048, 512], P('dp', 'tm'), may hold values from -6 to 6
Outputs:
- mixed_out: bfloat16 [4, 2048, 512], P('dp', 'tm')
- grad_query_input: bfloat16 [4, 2048, 512], P('dp', 'tm')
- grad_key_input: bfloat16 [4, 2048, 512], P('dp', 'tm')
- grad_value_input: bfloat16 [4, 2048, 512], P('dp', 'tm')
- grad_query_conv: float32 [4, 512], replicated
- grad_key_conv: float32 [4, 512], replicated
- grad_value_conv: float32 [4, 512], replicated
- grad_log_decay: float32 [4, 2048, 4], P('dp', 'tm')
- grad_write_strength: float32 [4, 2048, 4], P('dp', 'tm')
All inputs are finite; a program needn't handle non-finite values.
Results may differ from a plain program's by a relative error of at most 0.001.
Values may be sent and summed in bfloat16 or wider, within the bound.
No kernel may reach another device: no remote copies, remote signals or barrier semaphores. Data moves between devices by JAX's collectives and lax.ppermute only.
A program may use at most 128 MiB of HBM per device.

v0:
```python
import jax
import jax.numpy as jnp
from jax import lax
from jax.sharding import PartitionSpec as P

block_len = 64
highest = lax.Precision.HIGHEST


def from_behind(value, axis, steps):
    count = lax.axis_size(axis)
    first, last = (max(0, -steps), min(count, count - steps))
    return lax.ppermute(value, axis, [(source, source + steps) for source in range(first, last)])


def prefix(value, axis, join, neutral):
    count, mine = (lax.axis_size(axis), lax.axis_index(axis))
    pieces = jax.tree.map(lambda part: lax.all_gather(part, axis), value)
    pieces = jax.tree.map(lambda part: part[::-1], pieces)
    mine = count - 1 - mine
    so_far = jax.tree.map(
        lambda part, zero: jnp.full_like(part, 0) + jnp.asarray(zero, part.dtype), value, neutral
    )

    def lap(position, so_far):
        longer = join(so_far, jax.tree.map(lambda part: part[position], pieces))
        return jax.tree.map(lambda new, old: jnp.where(position < mine, new, old), longer, so_far)

    return lax.fori_loop(0, count - 1, lap, so_far)


def block_step(state, pieces):
    queries, keys_now, values_now, decays, betas = pieces
    block_size = decays.shape[1]
    running = jnp.cumsum(decays, axis=1)
    row_ids = lax.broadcasted_iota(jnp.int32, (block_size, block_size), 0)
    col_ids = lax.broadcasted_iota(jnp.int32, (block_size, block_size), 1)
    strictly = row_ids > col_ids
    inclusive = row_ids >= col_ids
    spread_log = running[:, :, None] - running[:, None, :]
    ratios = jnp.where(inclusive, jnp.exp(jnp.where(inclusive, spread_log, 0.0)), 0.0)
    key_gram = jnp.einsum("hrd,hsd->hrs", keys_now, keys_now, precision=highest)
    lower_part = jnp.where(strictly, betas[:, :, None] * ratios * key_gram, 0.0)
    system_matrix = lower_part + jnp.eye(block_size, dtype=jnp.float32)
    starting = jnp.exp(running)
    recalled = jnp.einsum("hrk,hvk->hrv", keys_now, state, precision=highest)
    targets = betas[:, :, None] * (values_now - starting[:, :, None] * recalled)
    updates = lax.linalg.triangular_solve(
        system_matrix, targets, left_side=True, lower=True, unit_diagonal=True
    )
    query_gram = jnp.einsum("hrd,hsd->hrs", queries, keys_now, precision=highest)
    mixed = starting[:, :, None] * jnp.einsum("hrk,hvk->hrv", queries, state, precision=highest)
    mixed = mixed + jnp.einsum("hrs,hsv->hrv", ratios * query_gram, updates, precision=highest)
    tail_decay = jnp.exp(running[:, -1:] - running)
    carried = jnp.exp(running[:, -1])[:, None, None] * state
    carried = carried + jnp.einsum(
        "hsv,hsk->hvk", updates, tail_decay[:, :, None] * keys_now, precision=highest
    )
    return (carried, mixed)


def to_blocks(array):
    block_count = array.shape[0] // block_len
    reshaped = array.reshape((block_count, block_len) + array.shape[1:])
    return jnp.moveaxis(reshaped, 2, 1)


def mix_sequence(queries, keys_now, values_now, decays, betas, initial):
    frame_count = queries.shape[0]
    head_count = queries.shape[1]
    final_state, outputs = lax.scan(
        block_step,
        initial,
        (
            to_blocks(queries),
            to_blocks(keys_now),
            to_blocks(values_now),
            to_blocks(decays),
            to_blocks(betas),
        ),
    )
    outputs = jnp.moveaxis(outputs, 1, 2).reshape(frame_count, head_count, -1)
    return (outputs, final_state)


def convolve(padded, weights):
    frame_count = padded.shape[0] - 3
    summed = weights[0] * padded[0:frame_count]
    for offset in range(1, 4):
        summed = summed + weights[offset] * padded[offset : offset + frame_count]
    return jax.nn.silu(summed)


def normalize(features, head_count):
    shaped = features.reshape(features.shape[0], head_count, -1)
    return shaped * lax.rsqrt(jnp.sum(shaped * shaped, axis=-1, keepdims=True) + 1e-06)


def layer_forward(
    initial, padded_q, padded_k, padded_v, query_conv, key_conv, value_conv, decays, betas
):
    head_count = decays.shape[1]
    queries = normalize(convolve(padded_q, query_conv), head_count)
    keys_now = normalize(convolve(padded_k, key_conv), head_count)
    values_now = convolve(padded_v, value_conv).reshape(padded_v.shape[0] - 3, head_count, -1)
    outputs, final_state = mix_sequence(queries, keys_now, values_now, decays, betas, initial)
    return (outputs.reshape(outputs.shape[0], -1), final_state)


def local_maps(padded_q, padded_k, padded_v, query_conv, key_conv, value_conv, decays, betas):
    head_count = decays.shape[1]
    queries = normalize(convolve(padded_q, query_conv), head_count)
    keys_now = normalize(convolve(padded_k, key_conv), head_count)
    values_now = convolve(padded_v, value_conv).reshape(padded_v.shape[0] - 3, head_count, -1)
    per_head_width = keys_now.shape[2]
    value_width = values_now.shape[2]
    extended = jnp.concatenate(
        [values_now, jnp.zeros((values_now.shape[0], head_count, per_head_width), jnp.float32)],
        axis=2,
    )
    identity_rows = jnp.broadcast_to(
        jnp.eye(per_head_width, dtype=jnp.float32), (head_count, per_head_width, per_head_width)
    )
    initial = jnp.concatenate(
        [jnp.zeros((head_count, value_width, per_head_width), jnp.float32), identity_rows], axis=1
    )
    outputs, final_state = mix_sequence(queries, keys_now, extended, decays, betas, initial)
    return (final_state[:, :value_width], final_state[:, value_width:])


def compose(earlier, later):
    joined = jnp.einsum("hij,hjk->hik", earlier[0], later[0], precision=highest)
    offset_part = jnp.einsum("hvj,hjk->hvk", earlier[1], later[0], precision=highest) + later[1]
    return (joined, offset_part)


def body(
    query_input,
    key_input,
    value_input,
    query_conv,
    key_conv,
    value_conv,
    log_decay,
    write_strength,
    out_cotangent,
):
    raw_q = query_input[0]
    raw_k = key_input[0]
    raw_v = value_input[0]
    decays = log_decay[0]
    betas = write_strength[0]
    cotangent = out_cotangent[0].astype(jnp.float32)
    history = from_behind((raw_q[-3:], raw_k[-3:], raw_v[-3:]), "tm", 1)
    padded_q = jnp.concatenate([history[0], raw_q], axis=0).astype(jnp.float32)
    padded_k = jnp.concatenate([history[1], raw_k], axis=0).astype(jnp.float32)
    padded_v = jnp.concatenate([history[2], raw_v], axis=0).astype(jnp.float32)
    offset_state, transit = local_maps(
        padded_q, padded_k, padded_v, query_conv, key_conv, value_conv, decays, betas
    )
    zero_state = jnp.zeros_like(offset_state)
    identity_maps = (
        jnp.broadcast_to(jnp.eye(transit.shape[1], dtype=jnp.float32), transit.shape),
        zero_state,
    )

    def relay(step_index, carried):
        arriving = from_behind(carried[1], "tm", 1)
        leaving = jnp.einsum("hvk,hkj->hvj", arriving, transit, precision=highest) + offset_state
        return (arriving, leaving)

    incoming, unused_state = lax.fori_loop(
        0, lax.axis_size("tm"), relay, (zero_state, offset_state)
    )
    (outputs, final_state), pullback = jax.vjp(
        layer_forward,
        incoming,
        padded_q,
        padded_k,
        padded_v,
        query_conv,
        key_conv,
        value_conv,
        decays,
        betas,
    )
    unused_pair, zero_pullback = jax.vjp(
        layer_forward,
        zero_state,
        padded_q,
        padded_k,
        padded_v,
        query_conv,
        key_conv,
        value_conv,
        decays,
        betas,
    )
    seed_state = zero_pullback((cotangent, zero_state))[0]
    transposed = jnp.swapaxes(transit, 1, 2)
    unused_back, returning = prefix((transposed, seed_state), "tm", compose, identity_maps)
    grads = pullback((cotangent, returning))
    rim_back = from_behind((grads[1][:3], grads[2][:3], grads[3][:3]), "tm", -1)
    grad_q = jnp.concatenate([grads[1][3:-3], grads[1][-3:] + rim_back[0]], axis=0)
    grad_k = jnp.concatenate([grads[2][3:-3], grads[2][-3:] + rim_back[1]], axis=0)
    value_gradient = jnp.concatenate([grads[3][3:-3], grads[3][-3:] + rim_back[2]], axis=0)
    conv_totals = lax.psum((grads[4], grads[5], grads[6]), ("dp", "tm"))
    return (
        outputs.astype(jnp.bfloat16)[None],
        grad_q.astype(jnp.bfloat16)[None],
        grad_k.astype(jnp.bfloat16)[None],
        value_gradient.astype(jnp.bfloat16)[None],
        conv_totals[0],
        conv_totals[1],
        conv_totals[2],
        grads[7][None],
        grads[8][None],
    )


def solution(mesh):
    in_specs = (
        P("dp", "tm", None),
        P("dp", "tm", None),
        P("dp", "tm", None),
        P(),
        P(),
        P(),
        P("dp", "tm", None),
        P("dp", "tm", None),
        P("dp", "tm", None),
    )
    out_specs = (
        P("dp", "tm", None),
        P("dp", "tm", None),
        P("dp", "tm", None),
        P("dp", "tm", None),
        P(),
        P(),
        P(),
        P("dp", "tm", None),
        P("dp", "tm", None),
    )
    return jax.shard_map(body, mesh=mesh, in_specs=in_specs, out_specs=out_specs, check_vma=False)
```

profile of v0, /device:TPU:0, one launch (start us, length us, event | category | flops | bytes accessed | tf_op | source)
XLA Modules:
  0.0 931.4 jit_solution(10559180824961694907)
XLA Ops:
  41.6 106.4 %while.165 = (s32[]{:T(128)}, f32[4,256,128]{2,1,0:T(8,128)S(1)}, f32[4,4,64]{2,1,0:T(4,128)}, f32[4,4,64]{2,1,0:T(4,128)}, f32[4,4,64,128]{3,2,1,0:T(8,128)S(1)...) while((s32[]{:T(128)}, f32[4,256,128]{2,1,0:T(8,128)S(1)}, f32[4,4,64]{2,1,0:T(4,128)}, ...), condition=%wide.region_3.4_spmd, body=%wide.region_1.3_spmd.sunk | while | flops 277508160 | bytes 3565849 | solution.py:71
  45.5 19.7 %custom-call.41 = f32[4,1,64,64]{2,3,1,0:T(8,128)S(1)} custom-call(f32[4,1,64,64]{3,2,1,0:T(8,128)S(1)} %fusion.372), custom_call_target="InvertDiagBlocksLowerTriangular" | custom-call | tf_op jit(solution)/shard_map/while/body/eval_jaxpr/triangular_solve | solution.py:48
  72.1 19.7 %custom-call.41 = f32[4,1,64,64]{2,3,1,0:T(8,128)S(1)} custom-call(f32[4,1,64,64]{3,2,1,0:T(8,128)S(1)} %fusion.372), custom_call_target="InvertDiagBlocksLowerTriangular" | custom-call | tf_op jit(solution)/shard_map/while/body/eval_jaxpr/triangular_solve | solution.py:48
  98.7 19.7 %custom-call.41 = f32[4,1,64,64]{2,3,1,0:T(8,128)S(1)} custom-call(f32[4,1,64,64]{3,2,1,0:T(8,128)S(1)} %fusion.372), custom_call_target="InvertDiagBlocksLowerTriangular" | custom-call | tf_op jit(solution)/shard_map/while/body/eval_jaxpr/triangular_solve | solution.py:48
  125.3 19.7 %custom-call.41 = f32[4,1,64,64]{2,3,1,0:T(8,128)S(1)} custom-call(f32[4,1,64,64]{3,2,1,0:T(8,128)S(1)} %fusion.372), custom_call_target="InvertDiagBlocksLowerTriangular" | custom-call | tf_op jit(solution)/shard_map/while/body/eval_jaxpr/triangular_solve | solution.py:48
  163.2 25.9 %while.168 = (s32[]{:T(128)}, f32[4,4,64,1]{2,1,3,0:T(4,128)}, f32[4,4,64,1]{2,1,3,0:T(4,128)}, f32[4,4,64,64]{3,2,1,0:T(8,128)}, f32[4,4,64,64]{3,2,1,0:T(8,128...) while((s32[]{:T(128)}, f32[4,4,64,1]{2,1,3,0:T(4,128)}, ...), condition=%wide.region_12.13_spmd.clone.clone, body=%wide.region_10.12_spmd.clone.clone.sunk | while | flops 50569216 | bytes 1021181 | solution.py:71
  189.1 110.9 %while.170 = (s32[]{:T(128)}, f32[4,128,128]{2,1,0:T(8,128)S(1)}, f32[4,4,1,1]{1,3,2,0:T(1,128)}, f32[4,4,64,1]{2,1,3,0:T(4,128)}, f32[4,4,64,128]{3,2,1,0:T(8,1...) while((s32[]{:T(128)}, f32[4,128,128]{2,1,0:T(8,128)S(1)}, ...), condition=%wide.region_14.16_spmd.clone, body=%wide.region_13.15_spmd.clone.sunk | while | flops 201863232 | bytes 3137267 | solution.py:71
  195.5 19.7 %custom-call.45 = f32[4,1,64,64]{2,3,1,0:T(8,128)S(1)} custom-call(f32[4,1,64,64]{3,2,1,0:T(8,128)S(1)} %fusion.447), custom_call_target="InvertDiagBlocksLowerTriangular" | custom-call | tf_op jit(solution)/shard_map/transpose(jvp())/while/body/eval_jaxpr/triangular_solve/custom-call.2 | solution.py:48
  223.2 19.7 %custom-call.45 = f32[4,1,64,64]{2,3,1,0:T(8,128)S(1)} custom-call(f32[4,1,64,64]{3,2,1,0:T(8,128)S(1)} %fusion.447), custom_call_target="InvertDiagBlocksLowerTriangular" | custom-call | tf_op jit(solution)/shard_map/transpose(jvp())/while/body/eval_jaxpr/triangular_solve/custom-call.2 | solution.py:48
  251.0 19.7 %custom-call.45 = f32[4,1,64,64]{2,3,1,0:T(8,128)S(1)} custom-call(f32[4,1,64,64]{3,2,1,0:T(8,128)S(1)} %fusion.447), custom_call_target="InvertDiagBlocksLowerTriangular" | custom-call | tf_op jit(solution)/shard_map/transpose(jvp())/while/body/eval_jaxpr/triangular_solve/custom-call.2 | solution.py:48
  278.7 19.7 %custom-call.45 = f32[4,1,64,64]{2,3,1,0:T(8,128)S(1)} custom-call(f32[4,1,64,64]{3,2,1,0:T(8,128)S(1)} %fusion.447), custom_call_target="InvertDiagBlocksLowerTriangular" | custom-call | tf_op jit(solution)/shard_map/transpose(jvp())/while/body/eval_jaxpr/triangular_solve/custom-call.2 | solution.py:48
  305.3 93.6 %while.166 = (s32[]{:T(128)}, f32[4,128,128]{2,1,0:T(8,128)}, f32[4,128,128]{2,1,0:T(8,128)S(1)}, f32[4,128,128]{2,1,0:T(8,128)S(1)}, f32[4,128,128]{2,1,0:T(8,128)S(1)}, /*index=5*/s32[]{:T(128)}) while((s32[]{:T(128)}, f32[4,128,128]{2,1,0:T(8,128)}, f32[4,128,128]{2,1,0:T(8,128)S(1)}, f32[4,128,128]{2,1,0:T(8,128)S(1)}, ...), condition=%wide.region_5.6_spmd, body=%wide.region_4.5_spmd.sunk | while | flops 100728832 | bytes 3145865 | solution.py:172
  322.7 9.1 collective-permute-start
  331.8 9.8 %collective-permute-done = f32[4,128,128]{2,1,0:T(8,128)S(1)} collective-permute-done((f32[4,128,128]{2,1,0:T(8,128)S(1)}, f32[4,128,128]{2,1,0:T(8,128)S(1)}, u32[]{:S(2)}, u32[]{:S(2)}) %collective-permute-start) | collective-permute-done | bytes 262176 | tf_op jit(solution)/shard_map/while/body/eval_jaxpr/ppermute | solution.py:13
  342.3 6.2 collective-permute-start
  353.8 10.9 %collective-permute-start = (f32[4,128,128]{2,1,0:T(8,128)S(1)}, f32[4,128,128]{2,1,0:T(8,128)S(1)}, u32[]{:S(2)}, u32[]{:S(2)}) collective-permute-start(f32[4,128,128]{2,1,0:T(8,128)S(1)} %get-tuple-element.3811), channel_id=1, source_target_pairs={{0,1},{1,2},{2,3},{3,4},{4,5},{5,6},{6,7},{8,9},{9,10},{10,11},{11... | collective-permute-start | bytes 786440 | tf_op jit(solution)/shard_map/while/body/eval_jaxpr/ppermute | solution.py:13
  410.4 135.1 %while.167 = (s32[]{:T(128)}, f32[4,128,128]{2,1,0:T(8,128)S(1)}, bf16[4,4,64,128]{3,2,1,0:T(8,128)(2,1)}, f32[4,4,64,64]{3,2,1,0:T(8,128)}, f32[4,4,64,64]{3,2,...) while((s32[]{:T(128)}, f32[4,128,128]{2,1,0:T(8,128)S(1)}, ...), condition=%wide.region_9.10_spmd.clone.clone, body=%wide.region_7.9_spmd.clone.clone.sunk | while | flops 252531264 | bytes 8529445 | solution.py:71
  417.1 19.7 %custom-call.42 = f32[4,1,64,64]{2,3,1,0:T(8,128)S(1)} custom-call(f32[4,1,64,64]{3,2,1,0:T(8,128)S(1)} %add_bitcast_fusion.4), custom_call_target="InvertDiagBlocksLowerTriangular" | custom-call | tf_op jit(solution)/shard_map/jvp()/while/body/eval_jaxpr/triangular_solve | solution.py:48
  450.9 19.7 %custom-call.42 = f32[4,1,64,64]{2,3,1,0:T(8,128)S(1)} custom-call(f32[4,1,64,64]{3,2,1,0:T(8,128)S(1)} %add_bitcast_fusion.4), custom_call_target="InvertDiagBlocksLowerTriangular" | custom-call | tf_op jit(solution)/shard_map/jvp()/while/body/eval_jaxpr/triangular_solve | solution.py:48
  484.7 19.7 %custom-call.42 = f32[4,1,64,64]{2,3,1,0:T(8,128)S(1)} custom-call(f32[4,1,64,64]{3,2,1,0:T(8,128)S(1)} %add_bitcast_fusion.4), custom_call_target="InvertDiagBlocksLowerTriangular" | custom-call | tf_op jit(solution)/shard_map/jvp()/while/body/eval_jaxpr/triangular_solve | solution.py:48
  518.5 19.7 %custom-call.42 = f32[4,1,64,64]{2,3,1,0:T(8,128)S(1)} custom-call(f32[4,1,64,64]{3,2,1,0:T(8,128)S(1)} %add_bitcast_fusion.4), custom_call_target="InvertDiagBlocksLowerTriangular" | custom-call | tf_op jit(solution)/shard_map/jvp()/while/body/eval_jaxpr/triangular_solve | solution.py:48
  559.7 10.4 %while.171 = (s32[]{:T(128)}, f32[4,128,128]{1,2,0:T(8,128)S(1)}, s32[]{:T(128)}, f32[8,4,128,128]{2,3,1,0:T(8,128)}, f32[8,4,128,128]{2,3,1,0:T(8,128)}, /*index=5*/s32[]{:T(128)}, s32[]{:T(128)}) while((s32[]{:T(128)}, f32[4,128,128]{1,2,0:T(8,128)S(1)}, s32[]{:T(128)}, f32[8,4,128,128]{2,3,1,0:T(8,128)}, ...), condition=%wide.region_16.18_spmd.clone, body=%wide.region_15.17_spmd.clone.sunk | while | flops 100925440 | bytes 1837671 | solution.py:29
  574.0 270.3 %while.169 = (s32[]{:T(128)}, f32[4,128,128]{2,1,0:T(8,128)S(1)}, f32[4,4,64,128]{3,2,1,0:T(8,128)}, f32[4,4,64,128]{3,2,1,0:T(8,128)}, f32[4,4,64,128]{3,2,1,0:...) while((s32[]{:T(128)}, f32[4,128,128]{2,1,0:T(8,128)S(1)}, ...), condition=%wide.region_28.30_spmd.clone.clone, body=%wide.region_17.29_spmd.clone.clone.sunk | while | flops 517469504 | bytes 10423457 | solution.py:71
  581.8 19.7 %custom-call.43 = f32[4,1,64,64]{2,3,1,0:T(8,128)S(1)} custom-call(f32[4,1,64,64]{3,2,1,0:T(8,128)S(1)} %fusion.419), custom_call_target="InvertDiagBlocksLowerTriangular" | custom-call | tf_op jit(solution)/shard_map/transpose(jvp())/while/body/eval_jaxpr/triangular_solve/custom-call.2 | solution.py:48
  609.7 19.7 %custom-call.44 = f32[4,1,64,64]{2,3,1,0:T(8,128)S(1)} custom-call(f32[4,1,64,64]{3,2,1,0:T(8,128)S(1)} %add_bitcast_fusion.5), custom_call_target="InvertDiagBlocksLowerTriangular" | custom-call | tf_op jit(solution)/shard_map/transpose(jvp())/while/body/eval_jaxpr/triangular_solve | solution.py:48
  649.3 19.7 %custom-call.43 = f32[4,1,64,64]{2,3,1,0:T(8,128)S(1)} custom-call(f32[4,1,64,64]{3,2,1,0:T(8,128)S(1)} %fusion.419), custom_call_target="InvertDiagBlocksLowerTriangular" | custom-call | tf_op jit(solution)/shard_map/transpose(jvp())/while/body/eval_jaxpr/triangular_solve/custom-call.2 | solution.py:48
  677.2 19.7 %custom-call.44 = f32[4,1,64,64]{2,3,1,0:T(8,128)S(1)} custom-call(f32[4,1,64,64]{3,2,1,0:T(8,128)S(1)} %add_bitcast_fusion.5), custom_call_target="InvertDiagBlocksLowerTriangular" | custom-call | tf_op jit(solution)/shard_map/transpose(jvp())/while/body/eval_jaxpr/triangular_solve | solution.py:48
  716.8 19.7 %custom-call.43 = f32[4,1,64,64]{2,3,1,0:T(8,128)S(1)} custom-call(f32[4,1,64,64]{3,2,1,0:T(8,128)S(1)} %fusion.419), custom_call_target="InvertDiagBlocksLowerTriangular" | custom-call | tf_op jit(solution)/shard_map/transpose(jvp())/while/body/eval_jaxpr/triangular_solve/custom-call.2 | solution.py:48
  744.6 19.7 %custom-call.44 = f32[4,1,64,64]{2,3,1,0:T(8,128)S(1)} custom-call(f32[4,1,64,64]{3,2,1,0:T(8,128)S(1)} %add_bitcast_fusion.5), custom_call_target="InvertDiagBlocksLowerTriangular" | custom-call | tf_op jit(solution)/shard_map/transpose(jvp())/while/body/eval_jaxpr/triangular_solve | solution.py:48
  784.2 19.7 %custom-call.43 = f32[4,1,64,64]{2,3,1,0:T(8,128)S(1)} custom-call(f32[4,1,64,64]{3,2,1,0:T(8,128)S(1)} %fusion.419), custom_call_target="InvertDiagBlocksLowerTriangular" | custom-call | tf_op jit(solution)/shard_map/transpose(jvp())/while/body/eval_jaxpr/triangular_solve/custom-call.2 | solution.py:48
  812.1 19.7 %custom-call.44 = f32[4,1,64,64]{2,3,1,0:T(8,128)S(1)} custom-call(f32[4,1,64,64]{3,2,1,0:T(8,128)S(1)} %add_bitcast_fusion.5), custom_call_target="InvertDiagBlocksLowerTriangular" | custom-call | tf_op jit(solution)/shard_map/transpose(jvp())/while/body/eval_jaxpr/triangular_solve | solution.py:48
  866.8 52.5 %all-reduce.28 = (f32[4,512]{1,0:T(4,128)}, f32[4,512]{1,0:T(4,128)}, f32[4,512]{1,0:T(4,128)}) all-reduce(f32[4,512]{1,0:T(4,128)S(1)} %pad_add_fusion.5, f32[4,512]{1,0:T(4,128)S(1)} %pad_add_fusion.4, f32[4,512]{1,0:T(4,128)S(1)} %pad_add_fusion.3), channel_id=1, replica_groups=mesh['dp'=4,'tm'=8] {'dp','tm'}, use_global_device_ids=true, to_apply=%region_35.37 | all-reduce | flops 6144 | bytes 49152 | tf_op jit(solution)/shard_map/psum | solution.py:207
  (731 shorter events, 431.7 us)
Async XLA Ops:
  7.2 18.2 %copy-start.59 = (f32[4,512]{1,0:T(4,128)S(1)}, f32[4,512]{1,0:T(4,128)}, u32[]{:S(2)}) copy-start(f32[4,512]{1,0:T(4,128)} %param.29) | copy-start | bytes 24580
  7.2 18.2 %copy-start.60 = (f32[4,512]{1,0:T(4,128)S(1)}, f32[4,512]{1,0:T(4,128)}, u32[]{:S(2)}) copy-start(f32[4,512]{1,0:T(4,128)} %param.30) | copy-start | bytes 24580
  7.2 18.8 %copy-start.61 = (f32[4,512]{1,0:T(4,128)S(1)}, f32[4,512]{1,0:T(4,128)}, u32[]{:S(2)}) copy-start(f32[4,512]{1,0:T(4,128)} %param.28) | copy-start | bytes 24580
  7.2 20.2 %copy-start.62 = (f32[1,256,4]{1,2,0:T(4,128)S(1)}, f32[1,256,4]{1,2,0:T(4,128)}, u32[]{:S(2)}) copy-start(f32[1,256,4]{1,2,0:T(4,128)} %param.31) | copy-start | bytes 12292
  7.2 20.9 %copy-start.63 = (f32[1,256,4]{1,2,0:T(4,128)S(1)}, f32[1,256,4]{1,2,0:T(4,128)}, u32[]{:S(2)}) copy-start(f32[1,256,4]{1,2,0:T(4,128)} %param.32) | copy-start | bytes 12292
  7.2 21.6 %copy-start.24 = (bf16[1,256,512]{2,1,0:T(8,128)(2,1)S(1)}, bf16[1,256,512]{2,1,0:T(8,128)(2,1)}, u32[]{:S(2)}) copy-start(bf16[1,256,512]{2,1,0:T(8,128)(2,1)} %param.33) | copy-start | bytes 786436
  7.2 540.2 %all-gather.5.cloned.1.call-start = ((), (), s32[]{:S(2)}) async-start(), calls=%async_computation | async-start | bytes 2359296 | tf_op jit(solution)/shard_map/all_gather | solution.py:18
  8.5 20.6 %collective-permute-start.1 = (bf16[3,512]{0,1:T(8,128)(2,1)S(1)}, bf16[3,512]{0,1:T(8,128)(2,1)S(1)}, u32[]{:S(2)}, u32[]{:S(2)}) collective-permute-start(bf16[3,512]{0,1:T(8,128)(2,1)S(1)} %slice_bitcast_fusion.2), channel_id=1, source_target_pairs={{0,1},{1,2},{2,3},{3,4},{4,5},{5,6},{6,7},{8,9},{9,10},{10,11},{11... | collective-permute-start | bytes 9224 | tf_op jit(solution)/shard_map/ppermute | solution.py:13
  14.5 14.3 %copy-start.17 = (bf16[1,256,512]{1,2,0:T(8,128)(2,1)}, bf16[1,256,512]{1,2,0:T(8,128)(2,1)S(1)}, u32[]{:S(2)}) copy-start(bf16[1,256,512]{1,2,0:T(8,128)(2,1)S(1)} %copy.204) | copy-start | bytes 786436
  15.3 19.1 %collective-permute-start.2 = (bf16[3,512]{0,1:T(8,128)(2,1)}, bf16[3,512]{0,1:T(8,128)(2,1)}, u32[]{:S(2)}, u32[]{:S(2)}) collective-permute-start(bf16[3,512]{0,1:T(8,128)(2,1)} %slice_bitcast_fusion.1), channel_id=1, source_target_pairs={{0,1},{1,2},{2,3},{3,4},{4,5},{5,6},{6,7},{8,9},{9,10},{10,11},{11... | collective-permute-start | bytes 9224 | tf_op jit(solution)/shard_map/ppermute | solution.py:13
  21.2 127.9 %collective-permute-start.3 = (bf16[3,512]{0,1:T(8,128)(2,1)}, bf16[3,512]{0,1:T(8,128)(2,1)}, u32[]{:S(2)}, u32[]{:S(2)}) collective-permute-start(bf16[3,512]{0,1:T(8,128)(2,1)} %slice_bitcast_fusion), channel_id=1, source_target_pairs={{0,1},{1,2},{2,3},{3,4},{4,5},{5,6},{6,7},{8,9},{9,10},{10,11},{11... | collective-permute-start | bytes 9224 | tf_op jit(solution)/shard_map/ppermute | solution.py:13
  151.9 5.0 copy-start.31
  151.9 5.2 copy-start.10
  157.0 6.2 copy-start.29
  158.6 395.0 %all-gather.7.cloned.1.call-start = ((), (), s32[]{:S(2)}) async-start(), calls=%async_computation.1 | async-start | bytes 2359296 | tf_op jit(solution)/shard_map/all_gather | solution.py:18
  299.9 5.3 copy-start.2
  305.3 7.8 collective-permute-start
  313.8 8.3 collective-permute-start
  322.7 18.9 %collective-permute-start = (f32[4,128,128]{2,1,0:T(8,128)S(1)}, f32[4,128,128]{2,1,0:T(8,128)S(1)}, u32[]{:S(2)}, u32[]{:S(2)}) collective-permute-start(f32[4,128,128]{2,1,0:T(8,128)S(1)} %get-tuple-element.3811), channel_id=1, source_target_pairs={{0,1},{1,2},{2,3},{3,4},{4,5},{5,6},{6,7},{8,9},{9,10},{10,11},{11... | collective-permute-start | bytes 786440 | tf_op jit(solution)/shard_map/while/body/eval_jaxpr/ppermute | solution.py:13
  342.3 10.8 %collective-permute-start = (f32[4,128,128]{2,1,0:T(8,128)S(1)}, f32[4,128,128]{2,1,0:T(8,128)S(1)}, u32[]{:S(2)}, u32[]{:S(2)}) collective-permute-start(f32[4,128,128]{2,1,0:T(8,128)S(1)} %get-tuple-element.3811), channel_id=1, source_target_pairs={{0,1},{1,2},{2,3},{3,4},{4,5},{5,6},{6,7},{8,9},{9,10},{10,11},{11... | collective-permute-start | bytes 786440 | tf_op jit(solution)/shard_map/while/body/eval_jaxpr/ppermute | solution.py:13
  353.8 14.8 %collective-permute-start = (f32[4,128,128]{2,1,0:T(8,128)S(1)}, f32[4,128,128]{2,1,0:T(8,128)S(1)}, u32[]{:S(2)}, u32[]{:S(2)}) collective-permute-start(f32[4,128,128]{2,1,0:T(8,128)S(1)} %get-tuple-element.3811), channel_id=1, source_target_pairs={{0,1},{1,2},{2,3},{3,4},{4,5},{5,6},{6,7},{8,9},{9,10},{10,11},{11... | collective-permute-start | bytes 786440 | tf_op jit(solution)/shard_map/while/body/eval_jaxpr/ppermute | solution.py:13
  369.3 9.1 collective-permute-start
  379.1 9.2 collective-permute-start
  389.0 9.2 collective-permute-start
  402.9 7.6 copy-start.1
  570.0 3.9 copy-start.23
  860.5 4.9 copy-start.33
  860.5 5.6 copy-start.34
  860.5 59.7 %copy-start.21 = (bf16[1,253,512]{1,2,0:T(8,128)(2,1)S(1)}, bf16[1,253,512]{1,2,0:T(8,128)(2,1)}, u32[]{:S(2)}) copy-start(bf16[1,253,512]{1,2,0:T(8,128)(2,1)} %fusion.243) | copy-start | bytes 777220
  861.4 57.8 %collective-permute-start.4 = (f32[3,512]{0,1:T(8,128)}, f32[3,512]{0,1:T(8,128)S(1)}, u32[]{:S(2)}, u32[]{:S(2)}) collective-permute-start(f32[3,512]{0,1:T(8,128)} %slice.265), channel_id=1, source_target_pairs={{1,0},{2,1},{3,2},{4,3},{5,4},{6,5},{7,6},{9,8},{10,9},{11,10},{12... | collective-permute-start | bytes 18440 | tf_op jit(solution)/shard_map/ppermute | solution.py:13
  862.7 57.7 %collective-permute-start.5 = (f32[3,512]{0,1:T(8,128)}, f32[3,512]{0,1:T(8,128)}, u32[]{:S(2)}, u32[]{:S(2)}) collective-permute-start(f32[3,512]{0,1:T(8,128)} %slice.268), channel_id=1, source_target_pairs={{1,0},{2,1},{3,2},{4,3},{5,4},{6,5},{7,6},{9,8},{10,9},{11,10},{12... | collective-permute-start | bytes 18440 | tf_op jit(solution)/shard_map/ppermute | solution.py:13
  864.0 59.2 %collective-permute-start.6 = (f32[3,512]{0,1:T(8,128)S(1)}, f32[3,512]{0,1:T(8,128)S(1)}, u32[]{:S(2)}, u32[]{:S(2)}) collective-permute-start(f32[3,512]{0,1:T(8,128)S(1)} %slice.271), channel_id=1, source_target_pairs={{1,0},{2,1},{3,2},{4,3},{5,4},{6,5},{7,6},{9,8},{10,9},{11,10},{12... | collective-permute-start | bytes 18440 | tf_op jit(solution)/shard_map/ppermute | solution.py:13
  (67 other events, 134.7 us)
Sparse Core Ops, SparseCore 0:
  158.7 48.1 all-gather.4
  305.4 56.1 all-gather.6
where the time goes:
time: 943 us; the launch traced here: 931 us
  other arithmetic  461 us (49%)
  matrix products  162 us (17%)
  local copies, waits for them, and re-layouts  134 us (14%)
  starting transfers between devices  65.8 us (7%)
  blocking collectives  52.5 us (6%)
  waiting for transfers between devices  38.6 us (4%)
  between operations  15.7 us (2%)
    another operation x76, other arithmetic, block_step(): lax.linalg.triangular_solve(system_matrix, targets, left_side=True, lower...  406 us
    ppermute x14, starting transfers between devices, from_behind(): lax.ppermute(value, axis, [(source, source + steps) for source in range(f...  65.6 us
    psum x1, blocking collectives, body(): conv_totals = lax.psum((grads[4], grads[5], grads[6]), ('dp', 'tm'))  52.5 us
    ppermute x14, waiting for transfers between devices, from_behind(): lax.ppermute(value, axis, [(source, source + steps) for source in range(f...  38.6 us
    dot_general x20, matrix products, block_step(): jnp.einsum('hsv,hsk->hvk', updates, tail_decay[:, :, None] * keys_now, pr...  28.1 us
    dot_general x20, matrix products, block_step(): recalled = jnp.einsum('hrk,hvk->hrv', keys_now, state, precision=highest)  25.1 us
    another operation x20, matrix products, block_step(): lax.linalg.triangular_solve(system_matrix, targets, left_side=True, lower...  20.1 us
    dynamic_update_slice x24, local copies, waits for them, and re-layouts, mix_sequence(): lax.scan(block_step, initial, (to_blocks(queries), to_blocks(keys_now), t...  19.8 us
  transfers between devices with their start and end apart: 16, of which 8 were waited for; matrix products, arithmetic and copies ran while one was open for 47% of the time, Pallas kernels for 0%

commit v1 on v0

v1 whole, which is shorter than its diff:
```python
import functools

import jax
import jax.numpy as jnp
from jax import lax
from jax.experimental import pallas as pl
from jax.experimental.pallas import tpu as pltpu
from jax.sharding import PartitionSpec as P

F32 = jnp.float32
BF16 = jnp.bfloat16
CHUNK = 128
ANY = pl.BlockSpec(memory_space=pl.ANY)
VMEM = pl.BlockSpec(memory_space=pltpu.VMEM)
SMEM = pl.BlockSpec(memory_space=pltpu.SMEM)


def params(**more):
    return pltpu.CompilerParams(vmem_limit_bytes=56 * 1024 * 1024, **more)


def split(x):
    high = x.astype(BF16)
    return high, (x - high.astype(F32)).astype(BF16)


def nn(a, b):
    left = jnp.concatenate([a[0], a[0], a[1]], axis=1)
    right = jnp.concatenate([b[0], b[1], b[0]], axis=0)
    return jnp.dot(left, right, preferred_element_type=F32)


def nt(a, b):
    left = jnp.concatenate([a[0], a[0], a[1]], axis=1)
    right = jnp.concatenate([b[0], b[1], b[0]], axis=1)
    return lax.dot_general(left, right, (((1,), (1,)), ((), ())), preferred_element_type=F32)


def rows_of(*pairs):
    return tuple(jnp.concatenate(parts, axis=0) for parts in zip(*pairs))


def columns_of(*pairs):
    return tuple(jnp.concatenate(parts, axis=1) for parts in zip(*pairs))


def grid_ids():
    rows = lax.broadcasted_iota(jnp.int32, (CHUNK, CHUNK), 0)
    columns = lax.broadcasted_iota(jnp.int32, (CHUNK, CHUNK), 1)
    return rows, columns


def as_column(row, rows, columns):
    return jnp.sum(jnp.where(rows == columns, row, 0.0), axis=1, keepdims=True)


def as_row(column, rows, columns):
    return jnp.sum(jnp.where(rows == columns, column, 0.0), axis=0, keepdims=True)


def decay_forms(decay_row, rows, columns):
    g_column = jnp.sum(jnp.where(columns <= rows, decay_row, 0.0), axis=1, keepdims=True)
    g_row = as_row(g_column, rows, columns)
    g_last = jnp.sum(decay_row, axis=1, keepdims=True)
    return g_column, g_row, g_last


def place_in_group(axis, heads):
    index = lax.axis_index(axis)
    return lax.rem(index, heads), lax.div(index, heads)


def peer(me, heads, step):
    return me ^ step if heads & (heads - 1) == 0 else lax.rem(heads - me + step, heads)


def aligned(index, size):
    return pl.ds(pl.multiple_of(index * size, size), size)


def three_rows(values):
    high = values.astype(BF16).astype(F32)
    middle = (values - high).astype(BF16).astype(F32)
    return high, middle, values - high - middle


def pack_kernel(heads, axis, *refs):
    (q_ref, k_ref, v_ref, o_ref, rates), refs = refs[:5], refs[5:]
    key_outs, rest_outs, tails, lines = refs[:heads], refs[heads : 2 * heads], refs[2 * heads : 3 * heads], refs[-1]
    me, _ = place_in_group(axis, heads)
    frames, width = q_ref.shape[0], q_ref.shape[1] // heads
    per = frames // CHUNK
    lines[...] = jnp.zeros_like(lines)
    for step in range(heads):
        target = peer(me, heads, step)
        lanes = aligned(target, width)
        key_outs[step][0:frames, :] = k_ref[:, lanes]
        for place, ref in enumerate((v_ref, q_ref, o_ref)):
            rest_outs[step][place] = ref[:, lanes]
        for kind in range(2):
            for part, line in enumerate(three_rows(rates[pl.ds(kind * heads + target, 1), :])):
                for c in range(per):
                    at = (part * 2 + kind) * per + c
                    lines[at : at + 1, :] = line[:, c * CHUNK : (c + 1) * CHUNK]
        key_outs[step][frames:, :] = lines[...].astype(BF16)
    for head in range(heads):
        for place, ref in enumerate((k_ref, v_ref, q_ref)):
            tails[head][place] = ref[frames - 8 : frames, head * width : (head + 1) * width]


def line_rows(frames):
    return -(-6 * (frames // CHUNK) // 16) * 16


def pack(heads, axis, q, k, v, o, rates):
    frames, features = q.shape
    width = features // heads
    out_shape = [jax.ShapeDtypeStruct((frames + line_rows(frames), width), BF16)] * heads
    out_shape += [jax.ShapeDtypeStruct((3, frames, width), BF16)] * heads
    out_shape += [jax.ShapeDtypeStruct((3, 8, width), BF16)] * heads
    outs = pl.pallas_call(
        functools.partial(pack_kernel, heads, axis),
        out_shape=out_shape,
        in_specs=[VMEM] * 5,
        out_specs=[VMEM] * len(out_shape),
        scratch_shapes=[pltpu.VMEM((line_rows(frames), CHUNK), F32)],
        compiler_params=params(),
        name="pack",
    )(q, k, v, o, rates)
    return outs[:heads], outs[heads : 2 * heads], outs[2 * heads :]


def unpack_kernel(heads, axis, *refs):
    mixed, grads, taps, refs = refs[:heads], refs[heads : 2 * heads], refs[2 * heads : 3 * heads], refs[3 * heads :]
    outs, decay_out, beta_out, tap_outs = refs[:4], refs[4], refs[5], refs[6:9]
    me, _ = place_in_group(axis, heads)
    frames, width = mixed[0].shape
    per = frames // CHUNK
    line_ids = lax.broadcasted_iota(jnp.int32, (heads, CHUNK), 0)
    for step in range(heads):
        source = peer(me, heads, step)
        lanes = aligned(source, width)
        outs[0][:, lanes] = mixed[step][...]
        for place in range(3):
            outs[1 + place][:, lanes] = grads[step][place * frames : (place + 1) * frames, :]
            tap_outs[place][:, lanes] = taps[step][4 * place : 4 * place + 4, :]
        lines = grads[step][3 * frames :, :].astype(F32)
        for kind, out in enumerate((decay_out, beta_out)):
            for c in range(per):
                line = sum(
                    lines[(part * 2 + kind) * per + c : (part * 2 + kind) * per + c + 1, :]
                    for part in range(3)
                )
                at = slice(c * CHUNK, (c + 1) * CHUNK)
                out[:, at] = jnp.where(line_ids == source, line, 0.0 if step == 0 else out[:, at])


def unpack(heads, axis, mixed, grads, taps):
    frames, width = mixed[0].shape
    features = heads * width
    out_shape = [jax.ShapeDtypeStruct((frames, features), BF16)] * 4
    out_shape += [jax.ShapeDtypeStruct((heads, frames), F32)] * 2
    out_shape += [jax.ShapeDtypeStruct((4, features), F32)] * 3
    return pl.pallas_call(
        functools.partial(unpack_kernel, heads, axis),
        out_shape=out_shape,
        in_specs=[VMEM] * (3 * heads),
        out_specs=[VMEM] * 9,
        compiler_params=params(),
        name="unpack",
    )(*mixed, *grads, *taps)


def convolve(padded_ref, place, start, taps):
    total = taps[0:1] * padded_ref[place, 5 + start : 5 + start + CHUNK, :]
    for offset in range(1, 4):
        at = 5 + start + offset
        total = total + taps[offset : offset + 1] * padded_ref[place, at : at + CHUNK, :]
    return total


def tail_of(tails, place):
    tail = tails[0][place].astype(F32)
    for other in tails[1:]:
        tail = tail + other[place].astype(F32)
    return tail


def activated(c_value, unit):
    y = c_value * jax.nn.sigmoid(c_value)
    if unit:
        y = y * lax.rsqrt(jnp.sum(y * y, axis=1, keepdims=True) + 1e-06)
    return y


def ratio_forms(g_column, g_row, rows, columns):
    inclusive, above = columns <= rows, columns >= rows
    ratio = jnp.where(inclusive, jnp.exp(jnp.where(inclusive, g_column - g_row, 0.0)), 0.0)
    ratio_t = jnp.where(above, jnp.exp(jnp.where(above, g_row - g_column, 0.0)), 0.0)
    return ratio, ratio_t


def key_kernel(heads, axis, *refs):
    received, tails, tap_ref, refs = refs[:heads], refs[heads : 2 * heads], refs[2 * heads], refs[2 * heads + 1 :]
    raw_out, rate_out, k_out, inverse, padded, lower_high, lower_low = refs
    me, _ = place_in_group(axis, heads)
    length, width = k_out.shape
    frames = length // heads
    per = frames // CHUNK
    chunk_count = length // CHUNK
    padded[0, 0:8, :] = tail_of(tails, 0)
    for step in range(heads):
        source = peer(me, heads, step)
        block = received[step][0:frames, :]
        raw_out[aligned(source, frames), :] = block
        padded[0, pl.ds(pl.multiple_of(source * frames + 8, 8), frames), :] = block.astype(F32)
        lines = received[step][frames:, :].astype(F32)
        for kind in range(2):
            for c in range(per):
                at = kind * per + c
                line = lines[at : at + 1] + lines[at + 2 * per : at + 2 * per + 1]
                line = line + lines[at + 4 * per : at + 4 * per + 1]
                rate_out[kind, pl.ds(source * per + c, 1), :] = line
    rows, columns = grid_ids()
    eye = jnp.where(rows == columns, 1.0, 0.0)
    masks = []
    for level in range(CHUNK.bit_length() - 1):
        masks.append(
            ((rows >> (level + 1)) == (columns >> (level + 1)))
            & ((rows >> level) != (columns >> level))
            & (rows > columns)
        )
    taps = tap_ref[:, aligned(me, width)]
    for c in range(chunk_count):
        at = pl.ds(c * CHUNK, CHUNK)
        g_column, g_row, g_last = decay_forms(rate_out[0, c : c + 1, :], rows, columns)
        beta_column = as_column(rate_out[1, c : c + 1, :], rows, columns)
        keys = activated(convolve(padded, 0, c * CHUNK, taps), True)
        k_out[at, :] = keys
        k_pair = split(keys)
        below = columns < rows
        ratio = jnp.exp(jnp.where(below, g_column - g_row, 0.0))
        lower = jnp.where(below, beta_column * ratio * nt(k_pair, k_pair), 0.0)
        high, low = split(lower)
        lower_high[at, :] = high
        lower_low[at, :] = low
        inverse[at, :] = eye - jnp.where(masks[0], lower, 0.0)
    zero = jnp.zeros((CHUNK, CHUNK), BF16)
    for level in range(1, len(masks)):
        halfway = []
        for c in range(chunk_count):
            at = pl.ds(c * CHUNK, CHUNK)
            off = (
                jnp.where(masks[level], lower_high[at, :], zero),
                jnp.where(masks[level], lower_low[at, :], zero),
            )
            halfway.append(nn(off, split(inverse[at, :])))
        for c in range(chunk_count):
            at = pl.ds(c * CHUNK, CHUNK)
            t_value = inverse[at, :]
            inverse[at, :] = t_value - nn(split(t_value), split(halfway[c]))


def key_part(heads, axis, frames, received, tails, k_taps):
    width = received[0].shape[1]
    length = heads * frames
    out_shape = [
        jax.ShapeDtypeStruct((length, width), BF16),
        jax.ShapeDtypeStruct((2, length // CHUNK, CHUNK), F32),
        jax.ShapeDtypeStruct((length, width), F32),
        jax.ShapeDtypeStruct((length, CHUNK), F32),
    ]
    return pl.pallas_call(
        functools.partial(key_kernel, heads, axis),
        out_shape=out_shape,
        in_specs=[VMEM] * (2 * heads + 1),
        out_specs=[VMEM] * 4,
        scratch_shapes=[
            pltpu.VMEM((1, length + 8, width), F32),
            pltpu.VMEM((length, CHUNK), BF16),
            pltpu.VMEM((length, CHUNK), BF16),
        ],
        compiler_params=params(),
        name="key_part",
    )(*received, *tails, k_taps)


def local_kernel(heads, axis, *refs):
    received, tails, refs = refs[:heads], refs[heads : 2 * heads], refs[2 * heads :]
    rate, k_in, inverse, v_taps, q_taps = refs[:5]
    (raw, q_out, v_out, p_out, u_out, w_out, x_out, y_out) = refs[5:13]
    (mt_out, bt_out, ct_out, state_out, back_out, padded) = refs[13:]
    me, group = place_in_group(axis, heads)
    length, width = k_in.shape
    frames = length // heads
    chunk_count = length // CHUNK
    for place in range(2):
        padded[place, 0:8, :] = tail_of(tails, 1 + place)
    for step in range(heads):
        source = peer(me, heads, step)
        for place in range(3):
            block = received[step][place]
            raw[place, aligned(source, frames), :] = block
            if place < 2:
                rows = pl.ds(pl.multiple_of(source * frames + 8, 8), frames)
                padded[place, rows, :] = block.astype(F32)
    rows, columns = grid_ids()
    eye = jnp.where(rows == columns, 1.0, 0.0)
    taps = [ref[:, aligned(me, width)] for ref in (v_taps, q_taps)]
    for c in range(chunk_count):
        at = pl.ds(c * CHUNK, CHUNK)
        beta_row = rate[1, c : c + 1, :]
        g_column, g_row, g_last = decay_forms(rate[0, c : c + 1, :], rows, columns)
        beta_column = as_column(beta_row, rows, columns)
        ratio, ratio_t = ratio_forms(g_column, g_row, rows, columns)
        start_column, start_row = jnp.exp(g_column), jnp.exp(g_row)
        tail_column, tail_row = jnp.exp(g_last - g_column), jnp.exp(g_last - g_row)
        values = activated(convolve(padded, 0, c * CHUNK, taps[0]), False)
        queries = activated(convolve(padded, 1, c * CHUNK, taps[1]), True)
        q_out[at, :], v_out[at, :] = queries, values
        keys = k_in[at, :]
        q_pair, k_pair = split(queries), split(keys)
        p_out[at, :] = ratio * nt(q_pair, k_pair)
        pt = ratio_t * nt(k_pair, q_pair)
        t_value = inverse[at, :]
        u_w = nn(
            split(t_value),
            columns_of(split(beta_column * values), split(beta_column * start_column * keys)),
        )
        u_value, w_value = u_w[:, :width], u_w[:, width:]
        cotangent = raw[2, at, :]
        p_high, p_low = split(pt)
        first = jnp.dot(
            jnp.concatenate([p_high, p_low], axis=1),
            jnp.concatenate([cotangent, cotangent], axis=0),
            preferred_element_type=F32,
        )
        x_y = nn(split(t_value.T), columns_of(split(first), split(tail_column * keys)))
        x_value, y_value = x_y[:, :width], x_y[:, width:]
        keys_t, queries_t = keys.T, queries.T
        b_m = nn(split(keys_t * tail_row), columns_of(split(u_value), split(w_value)))
        whole = jnp.exp(g_last)
        bt_out[c] = b_m[:, :width]
        mt_out[c] = whole * eye - b_m[:, width:]
        ct_out[c] = nn(
            columns_of(split(queries_t * start_row), split(keys_t * (-beta_row * start_row))),
            rows_of((cotangent, jnp.zeros_like(cotangent)), split(x_value)),
        )
        u_out[at, :], w_out[at, :], x_out[at, :], y_out[at, :] = u_value, w_value, x_value, y_value

    state = bt_out[0]
    back = ct_out[chunk_count - 1]
    for c in range(1, chunk_count):
        other = chunk_count - 1 - c
        state = nn(split(mt_out[c]), split(state)) + bt_out[c]
        back = nn(split(mt_out[other].T), split(back)) + ct_out[other]
    if lax.axis_size(axis) == 2 * heads:
        state_out[...] = jnp.where(group == 0, state, back)
    else:
        state_out[...] = state
    back_out[...] = back


def local_part(heads, axis, received, tails, rate, keys, inverse, v_taps, q_taps):
    length, width = keys.shape
    chunk_count = length // CHUNK
    tall = jax.ShapeDtypeStruct((length, width), F32)
    square = jax.ShapeDtypeStruct((chunk_count, width, width), F32)
    one = jax.ShapeDtypeStruct((width, width), F32)
    out_shape = [jax.ShapeDtypeStruct((3, length, width), BF16)]
    out_shape += [tall] * 7 + [square] * 3 + [one] * 2
    return pl.pallas_call(
        functools.partial(local_kernel, heads, axis),
        out_shape=out_shape,
        in_specs=[VMEM] * (2 * heads + 5),
        out_specs=[VMEM] * len(out_shape),
        scratch_shapes=[pltpu.VMEM((2, length + 8, width), F32)],
        compiler_params=params(),
        name="local_part",
    )(*received, *tails, rate, keys, inverse, v_taps, q_taps)


def final_kernel(heads, axis, first, last, *refs):
    raw_k, raw, tails, refs = refs[0], refs[1], refs[2 : 2 + heads], refs[2 + heads :]
    (rate, q_in, k_in, v_in, p_in, u_in, w_in, x_in, y_in), refs = refs[:9], refs[9:]
    tap_refs, refs = refs[:3], refs[3:]
    me, group = place_in_group(axis, heads)
    length, width = q_in.shape
    chunk_count = length // CHUNK
    frames = length // heads
    if first == 0:
        (mt_in, bt_in, ct_in, state_in, back_in), refs = refs[:5], refs[5:]
        mixed_out, conv_out, rate_grad, tap_out, rim_out, states, backs, padded = refs
        state = jnp.where(group > 0, state_in[...], 0.0)
        back = jnp.where(group < lax.axis_size(axis) // heads - 1, back_in[...], 0.0)
        states[0] = state
        backs[chunk_count] = back
        for c in range(chunk_count):
            other = chunk_count - 1 - c
            state = nn(split(mt_in[c]), split(state)) + bt_in[c]
            back = nn(split(mt_in[other].T), split(back)) + ct_in[other]
            states[c + 1] = state
            backs[other] = back
    else:
        (states, backs, mixed_before, tap_before), refs = refs[:4], refs[4:]
        (conv_out, rate_grad, tap_out), mixed_outs, (padded, mixed_out) = refs[:3], refs[3 : 3 + heads], refs[-2:]
        mixed_out[0 : first * CHUNK, :] = mixed_before[...]
    low, high = first * CHUNK, last * CHUNK
    for place, ref in enumerate((raw_k, raw.at[0], raw.at[1])):
        if first == 0:
            padded[place, 0:8, :] = tail_of(tails, place)
            padded[place, 8 : 8 + high, :] = ref[0:high, :].astype(F32)
        else:
            padded[place, low - 8 : 8 + high, :] = ref[low - 16 : high, :].astype(F32)
    taps = [ref[:, aligned(me, width)] for ref in tap_refs]
    rows, columns = grid_ids()
    sums = [[jnp.zeros((8, width), F32) for _ in range(4)] for _ in range(3)]

    for c in range(first, last):
        at = pl.ds(c * CHUNK, CHUNK)
        decay_row, beta_row = rate[0, c : c + 1, :], rate[1, c : c + 1, :]
        g_column, g_row, g_last = decay_forms(decay_row, rows, columns)
        beta_column = as_column(beta_row, rows, columns)
        start_column = jnp.exp(g_column)
        tail_column = jnp.exp(g_last - g_column)
        ratio, ratio_t = ratio_forms(g_column, g_row, rows, columns)
        keys, queries = k_in[at, :], q_in[at, :]
        k_pair, q_pair = split(keys), split(queries)
        s_pair, d_pair = split(states[c]), split(backs[c + 1])
        u_value = u_in[at, :] - nn(split(w_in[at, :]), s_pair)
        x_value = x_in[at, :] + nn(split(y_in[at, :]), d_pair)
        u_pair, x_pair = split(u_value), split(x_value)
        mixed = start_column * nn(q_pair, s_pair) + nn(split(p_in[at, :]), u_pair)
        cotangent = raw[2, at, :]
        o_pair = (cotangent, jnp.zeros_like(cotangent))
        cotangent = cotangent.astype(F32)
        ox_pair = rows_of(o_pair, x_pair)
        ox_u = nt(ox_pair, u_pair)
        u_ox = nt(u_pair, ox_pair)
        ox_s = nt(ox_pair, s_pair)
        u_d = nt(u_pair, d_pair)
        strict = jnp.where(columns < rows, beta_column * ratio, 0.0)
        strict_t = jnp.where(columns > rows, beta_row * ratio_t, 0.0)
        e_value = ratio * ox_u[:CHUNK]
        f_value = strict * ox_u[CHUNK:] + strict_t * u_ox[:, CHUNK:]
        e_t = ratio_t * u_ox[:, :CHUNK]
        d_queries = start_column * ox_s[:CHUNK] + nn(split(e_value), k_pair)
        d_keys = (
            tail_column * u_d
            - (beta_column * start_column) * ox_s[CHUNK:]
            + nn(columns_of(split(e_t), split(-f_value)), rows_of(q_pair, k_pair))
        )
        d_values = beta_column * x_value
        mixed_out[at, :] = mixed.astype(BF16)
        d_beta = jnp.sum(x_value * u_value, axis=1, keepdims=True) / beta_column
        d_g = jnp.sum(cotangent * mixed - d_values * v_in[at, :], axis=1, keepdims=True)
        kept = jnp.sum(
            jnp.sum(states[c + 1] * backs[c + 1], axis=1, keepdims=True), axis=0, keepdims=True
        )
        rate_grad[0, c - first : c - first + 1, :] = (
            jnp.sum(jnp.where(rows >= columns, d_g, 0.0), axis=0, keepdims=True) + kept
        )
        rate_grad[1, c - first : c - first + 1, :] = as_row(d_beta, rows, columns)
        for place, (grad, unit) in enumerate(((d_keys, keys), (d_values, None), (d_queries, queries))):
            start = c * CHUNK
            shifted = [padded[place, start + 5 + i : start + 5 + i + CHUNK, :] for i in range(4)]
            c_value = taps[place][0:1] * shifted[0]
            for offset in range(1, 4):
                c_value = c_value + taps[place][offset : offset + 1] * shifted[offset]
            gate = jax.nn.sigmoid(c_value)
            if unit is not None:
                y = c_value * gate
                scale = lax.rsqrt(jnp.sum(y * y, axis=1, keepdims=True) + 1e-06)
                grad = scale * (grad - unit * jnp.sum(unit * grad, axis=1, keepdims=True))
            grad = grad * (gate * (1.0 + c_value * (1.0 - gate)))
            conv_out[place, start - low : start - low + CHUNK, :] = grad
            for offset in range(4):
                part = (grad * shifted[offset]).reshape(CHUNK // 8, 8, width)
                sums[place][offset] = sums[place][offset] + jnp.sum(part, axis=0)
            if c == 0:
                rim_out[place] = grad[0:8]
    tap_out[...] = jnp.zeros_like(tap_out) if first == 0 else tap_before[...]
    for place, row in ((0, 4), (1, 8), (2, 0)):
        for offset in range(4):
            tap_out[row + offset : row + offset + 1, :] += jnp.sum(
                sums[place][offset], axis=0, keepdims=True
            )
    if first > 0:
        for step in range(heads):
            mixed_outs[step][...] = mixed_out[aligned(peer(me, heads, step), frames), :]


def final_part(heads, axis, first, last, shared, more):
    length, width = shared[3 + heads].shape
    chunk_count = length // CHUNK
    count = last - first
    mixed = [jax.ShapeDtypeStruct((count * CHUNK, width), BF16)]
    out_shape = [
        jax.ShapeDtypeStruct((3, count * CHUNK, width), F32),
        jax.ShapeDtypeStruct((2, count, CHUNK), F32),
        jax.ShapeDtypeStruct((16, width), F32),
    ]
    scratch = [pltpu.VMEM((3, length + 8, width), F32)]
    if first == 0:
        chain = jax.ShapeDtypeStruct((chunk_count + 1, width, width), F32)
        out_shape = mixed + out_shape
        out_shape += [jax.ShapeDtypeStruct((3, 8, width), F32), chain, chain]
    else:
        out_shape += [jax.ShapeDtypeStruct((length // heads, width), BF16)] * heads
        scratch += [pltpu.VMEM((length, width), BF16)]
    args = [*shared, *more]
    return pl.pallas_call(
        functools.partial(final_kernel, heads, axis, first, last),
        out_shape=out_shape,
        in_specs=[VMEM] * len(args),
        out_specs=[VMEM] * len(out_shape),
        scratch_shapes=scratch,
        compiler_params=params(),
        name="final_part",
    )(*args)


def input_kernel(heads, axis, *refs):
    conv_first, conv_rest, rim, rate_first, rate_rest = refs[:5]
    tap_refs, blocks, refs = refs[5:8], refs[8 : 8 + heads], refs[8 + heads :]
    extended, result, rate_grad, lines = refs
    me, _ = place_in_group(axis, heads)
    length, width = result.shape[1:]
    frames = length // heads
    per = frames // CHUNK
    early = conv_first.shape[1]
    rate_grad[:, 0 : early // CHUNK, :] = rate_first[...]
    rate_grad[:, early // CHUNK :, :] = rate_rest[...]
    taps = [ref[:, aligned(me, width)] for ref in tap_refs]
    for place in range(3):
        extended[place, 0:early, :] = conv_first[place]
        extended[place, early:length, :] = conv_rest[place]
        extended[place, length:, :] = rim[place]
        for c in range(length // CHUNK):
            start = c * CHUNK
            grad = taps[place][3:4] * extended[place, start : start + CHUNK, :]
            for offset in range(3):
                at = start + 3 - offset
                grad = grad + taps[place][offset : offset + 1] * extended[place, at : at + CHUNK, :]
            result[(place + 1) % 3, start : start + CHUNK, :] = grad.astype(BF16)
    lines[...] = jnp.zeros_like(lines)
    for step in range(heads):
        target = peer(me, heads, step)
        for place in range(3):
            blocks[step][place * frames : (place + 1) * frames, :] = result[
                place, aligned(target, frames), :
            ]
        for kind in range(2):
            for c in range(per):
                line = rate_grad[kind, pl.ds(target * per + c, 1), :]
                for part, value in enumerate(three_rows(line)):
                    at = (part * 2 + kind) * per + c
                    lines[at : at + 1, :] = value
        blocks[step][3 * frames :, :] = lines[...].astype(BF16)


def input_part(heads, axis, convs, rim, rate_grads, tap_args):
    length, width = convs[0].shape[1] + convs[1].shape[1], convs[0].shape[2]
    frames = length // heads
    out_shape = [jax.ShapeDtypeStruct((3 * frames + line_rows(frames), width), BF16)] * heads
    args = [*convs, rim, *rate_grads, *tap_args]
    return pl.pallas_call(
        functools.partial(input_kernel, heads, axis),
        out_shape=out_shape,
        in_specs=[VMEM] * len(args),
        out_specs=[VMEM] * heads,
        scratch_shapes=[
            pltpu.VMEM((3, length + 8, width), F32),
            pltpu.VMEM((3, length, width), BF16),
            pltpu.VMEM((2, length // CHUNK, CHUNK), F32),
            pltpu.VMEM((line_rows(frames), CHUNK), F32),
        ],
        compiler_params=params(),
        name="input_part",
    )(*args)


def trade(values, axis, heads):
    count = lax.axis_size(axis)
    moved = [values[0]]
    for step in range(1, heads):
        pairs = [(d, d - d % heads + member(d % heads, heads, step)) for d in range(count)]
        moved.append(lax.ppermute(values[step], axis, pairs))
    return moved


def member(place, heads, step):
    return place ^ step if heads & (heads - 1) == 0 else (heads - place + step) % heads


def along(value, axis, steps):
    count = lax.axis_size(axis)
    return lax.ppermute(
        value, axis, [(d, d + steps) for d in range(count) if 0 <= d + steps < count]
    )


def total_over(value, axis, stride):
    count = lax.axis_size(axis)
    distance = stride
    while distance < count:
        value = value + lax.ppermute(value, axis, [(d, d ^ distance) for d in range(count)])
        distance *= 2
    return value


def body(q, k, v, q_taps, k_taps, v_taps, log_decay, write_strength, cotangent):
    axis = "tm"
    heads = log_decay.shape[2]
    count = lax.axis_size(axis)
    groups = count // heads
    q, k, v, o = q[0], k[0], v[0], cotangent[0]
    rate_lines = jnp.concatenate([log_decay[0].T, write_strength[0].T], axis=0)
    key_sends, rest_sends, tails = pack(heads, axis, q, k, v, o, rate_lines)
    key_blocks = trade(key_sends, axis, heads)
    tails = [
        lax.ppermute(
            tails[head], axis, [(g * heads - 1, g * heads + head) for g in range(1, groups)]
        )
        for head in range(heads)
    ]
    rest_blocks = trade(rest_sends, axis, heads)
    tap_args = (k_taps, v_taps, q_taps)
    raw_k, rate, keys, inverse = key_part(heads, axis, q.shape[0], key_blocks, tails, k_taps)
    parts = local_part(heads, axis, rest_blocks, tails, rate, keys, inverse, v_taps, q_taps)
    raw, queries, values, p, u, w, x, y, mt, bt, ct, state, back = parts
    if groups == 2:
        arriving = returning = lax.ppermute(
            state, axis, [(d, (d + heads) % count) for d in range(count)]
        )
    else:
        arriving, returning = jnp.zeros_like(state), jnp.zeros_like(back)
        exact = lax.Precision.HIGHEST
        for step in range(groups - 1):
            arriving = along(state, axis, heads)
            returning = along(back, axis, -heads)
            if step < groups - 2:
                state, back = arriving, returning
                for c in range(mt.shape[0]):
                    other = mt.shape[0] - 1 - c
                    state = jnp.dot(mt[c], state, precision=exact) + bt[c]
                    back = jnp.dot(mt[other].T, back, precision=exact) + ct[other]
    shared = (raw_k, raw, *tails, rate, queries, keys, values, p, u, w, x, y, *tap_args)
    chunk_count = mt.shape[0]
    mixed, conv, rate_grad, taps, rim, states, backs = final_part(
        heads, axis, 0, 1, shared, (mt, bt, ct, arriving, returning)
    )
    rim = along(rim, axis, -heads)
    later = final_part(heads, axis, 1, chunk_count, shared, (states, backs, mixed, taps))
    mixed = trade(later[3:], axis, heads)
    taps = total_over(total_over(later[2], "dp", 1), axis, heads)
    taps = trade([taps] * heads, axis, heads)
    blocks = input_part(heads, axis, (conv, later[0]), rim, (rate_grad, later[1]), tap_args)
    blocks = trade(blocks, axis, heads)
    outs = unpack(heads, axis, mixed, blocks, taps)
    return (
        outs[0][None],
        outs[1][None],
        outs[2][None],
        outs[3][None],
        outs[6],
        outs[7],
        outs[8],
        outs[4].T[None],
        outs[5].T[None],
    )


def solution(mesh):
    split_spec, whole_spec = P("dp", "tm", None), P()
    in_specs = (split_spec,) * 3 + (whole_spec,) * 3 + (split_spec,) * 3
    out_specs = (split_spec,) * 4 + (whole_spec,) * 3 + (split_spec,) * 2
    return jax.shard_map(body, mesh=mesh, in_specs=in_specs, out_specs=out_specs, check_vma=False)
```

time: 943 us -> 109 us (0.12); the launches traced: 931 us -> 108 us
  other arithmetic: 461 us -> 1.32 us
  matrix products: 162 us -> 0 us
  local copies, waits for them, and re-layouts: 134 us -> 3.38 us
  blocking collectives: 52.5 us -> 0 us
  Pallas kernels: 0 us -> 35.9 us
  starting transfers between devices: 65.8 us -> 38 us
  between operations: 15.7 us -> 1.15 us
  waiting for transfers between devices: 38.6 us -> 28.4 us
    another operation x98 -> x0, other arithmetic: 414 us -> none  [the longest x76 406 us: block_step(): lax.linalg.triangular_solve(system_matrix, targets, left_side=True, lower...]
    dot_general x127 -> x0, matrix products: 142 us -> none  [the longest x20 28.1 us: block_step(): jnp.einsum('hsv,hsk->hvk', updates, tail_decay[:, :, None] * keys_now, pr...]
    psum x1 -> x0, blocking collectives: 52.5 us -> none  [body(): conv_totals = lax.psum((grads[4], grads[5], grads[6]), ('dp', 'tm'))]
    pallas_call x0 -> x7, Pallas kernels: none -> 35.9 us  [the longest x2 14.4 us: final_part(): pl.pallas_call(functools.partial(final_kernel, heads, axis, first, last),...]
    ppermute x14 -> x24, starting transfers between devices: 65.6 us -> 38 us  [the longest x15 25.5 us: trade(): moved.append(lax.ppermute(values[step], axis, pairs))]
    mul x35 -> x0, local copies, waits for them, and re-layouts: 23.9 us -> none  [the longest x12 8.29 us: block_step(): lower_part = jnp.where(strictly, betas[:, :, None] * ratios * key_gram, 0.0)]
    another operation x20 -> x0, matrix products: 20.1 us -> none  [block_step(): lax.linalg.triangular_solve(system_matrix, targets, left_side=True, lower...]
    another operation x31 -> x0, local copies, waits for them, and re-layouts: 19.9 us -> none
  transfers between devices with their start and end apart: 16 -> 24, of which waited for: 8 -> 11; matrix products, arithmetic and copies ran while one was open for 47% -> 0% of each run, Pallas kernels for 0% -> 13%
where the time goes in v1:
time: 109 us; the launch traced here: 108 us
  starting transfers between devices  38 us (35%)
  Pallas kernels  35.9 us (33%)
  waiting for transfers between devices  28.4 us (26%)
  local copies, waits for them, and re-layouts  3.38 us (3%)
  other arithmetic  1.32 us (1%)
  between operations  1.15 us (1%)
    ppermute x15, starting transfers between devices, trade(): moved.append(lax.ppermute(values[step], axis, pairs))  25.5 us
    ppermute x15, waiting for transfers between devices, trade(): moved.append(lax.ppermute(values[step], axis, pairs))  21 us
    pallas_call x2, Pallas kernels, final_part(): pl.pallas_call(functools.partial(final_kernel, heads, axis, first, last),...  14.4 us
    pallas_call x1, Pallas kernels, local_part(): pl.pallas_call(functools.partial(local_kernel, heads, axis), out_shape=ou...  8.8 us
    pallas_call x1, Pallas kernels, key_part(): pl.pallas_call(functools.partial(key_kernel, heads, axis), out_shape=out_...  5.3 us
    ppermute x3, starting transfers between devices, total_over(): lax.ppermute(value, axis, [(d, d ^ distance) for d in range(count)])  5.06 us
    ppermute x3, waiting for transfers between devices, total_over(): lax.ppermute(value, axis, [(d, d ^ distance) for d in range(count)])  4.93 us
    unnamed x52, local copies, waits for them, and re-layouts  3.38 us
  transfers between devices with their start and end apart: 24, of which 11 were waited for; matrix products, arithmetic and copies ran while one was open for 0% of the time, Pallas kernels for 13%

profile of v1, /device:TPU:0, one launch (start us, length us, event | category | flops | bytes accessed | tf_op | source)
XLA Modules:
  0.0 108.2 jit_solution(4484191084590008558)
XLA Ops:
  0.6 1.3 %pad_maximum_fusion.refs_4_ = f32[8,256]{1,0:T(8,128)} fusion(f32[4,256]{1,0:T(4,128)} %bitcast.24, f32[4,256]{1,0:T(4,128)} %bitcast.25), kind=kLoop, calls=%fused_computation | loop fusion | flops 2048 | bytes 16384 | tf_op jit(solution)/shard_map/concatenate | solution.py:618
  2.0 2.2 %pack.1 = (bf16[272,128]{1,0:T(8,128)(2,1)}, bf16[272,128]{1,0:T(8,128)(2,1)}, bf16[272,128]{1,0:T(8,128)(2,1)}, bf16[272,128]{1,0:T(8,128)(2,1)}, bf16[3,256,12...) custom-call(bf16[256,512]{1,0:T(8,128)(2,1)} %bitcast.20, ...), custom_call_target="tpu_custom_call" | custom-call | tf_op jit(solution)/shard_map/pack/pallas_call | solution.py:121
  4.2 3.0 %collective-permute-start.7 = (bf16[3,256,128]{2,1,0:T(8,128)(2,1)}, bf16[3,256,128]{2,1,0:T(8,128)(2,1)S(1)}, u32[]{:S(2)}, u32[]{:S(2)}) collective-permute-start(bf16[3,256,128]{2,1,0:T(8,128)(2,1)} %get-tuple-element.74), channel_id=1, source_target_pairs={{0,1},{1,0},{2,3},{3,2},{4,5},{5,4},{6,7},{7,6},{8,9},{9,8},{10,11... | collective-permute-start | bytes 589832 | tf_op jit(solution)/shard_map/ppermute | solution.py:588
  7.2 1.6 %collective-permute-start.8 = (bf16[3,256,128]{2,1,0:T(8,128)(2,1)}, bf16[3,256,128]{2,1,0:T(8,128)(2,1)S(1)}, u32[]{:S(2)}, u32[]{:S(2)}) collective-permute-start(bf16[3,256,128]{2,1,0:T(8,128)(2,1)} %get-tuple-element.75), channel_id=1, source_target_pairs={{0,2},{1,3},{2,0},{3,1},{4,6},{5,7},{6,4},{7,5},{8,10},{9,11},{10,... | collective-permute-start | bytes 589832 | tf_op jit(solution)/shard_map/ppermute | solution.py:588
  8.8 1.9 %collective-permute-start = (bf16[272,128]{1,0:T(8,128)(2,1)}, bf16[272,128]{1,0:T(8,128)(2,1)S(1)}, u32[]{:S(2)}, u32[]{:S(2)}) collective-permute-start(bf16[272,128]{1,0:T(8,128)(2,1)} %get-tuple-element.65), channel_id=1, source_target_pairs={{0,1},{1,0},{2,3},{3,2},{4,5},{5,4},{6,7},{7,6},{8,9},{9,8},{10,11... | collective-permute-start | bytes 208904 | tf_op jit(solution)/shard_map/ppermute | solution.py:588
  13.4 1.6 %collective-permute-start.1 = (bf16[272,128]{1,0:T(8,128)(2,1)}, bf16[272,128]{1,0:T(8,128)(2,1)S(1)}, u32[]{:S(2)}, u32[]{:S(2)}) collective-permute-start(bf16[272,128]{1,0:T(8,128)(2,1)} %get-tuple-element.66), channel_id=1, source_target_pairs={{0,2},{1,3},{2,0},{3,1},{4,6},{5,7},{6,4},{7,5},{8,10},{9,11},{10,... | collective-permute-start | bytes 208904 | tf_op jit(solution)/shard_map/ppermute | solution.py:588
  15.1 2.9 %collective-permute-done.refs_1_ = bf16[272,128]{1,0:T(8,128)(2,1)S(1)} collective-permute-done((bf16[272,128]{1,0:T(8,128)(2,1)}, bf16[272,128]{1,0:T(8,128)(2,1)S(1)}, u32[]{:S(2)}, u32[]{:S(2)}) %collective-permute-start) | collective-permute-done | bytes 69664 | tf_op jit(solution)/shard_map/ppermute | solution.py:588
  18.0 8.7 %collective-permute-start.2 = (bf16[272,128]{1,0:T(8,128)(2,1)}, bf16[272,128]{1,0:T(8,128)(2,1)S(1)}, u32[]{:S(2)}, u32[]{:S(2)}) collective-permute-start(bf16[272,128]{1,0:T(8,128)(2,1)} %get-tuple-element.67), channel_id=1, source_target_pairs={{0,3},{1,2},{2,1},{3,0},{4,7},{5,6},{6,5},{7,4},{8,11},{9,10},{10,... | collective-permute-start | bytes 208904 | tf_op jit(solution)/shard_map/ppermute | solution.py:588
  26.7 3.2 %collective-permute-done.2.refs_3_ = bf16[272,128]{1,0:T(8,128)(2,1)S(1)} collective-permute-done((bf16[272,128]{1,0:T(8,128)(2,1)}, bf16[272,128]{1,0:T(8,128)(2,1)S(1)}, u32[]{:S(2)}, u32[]{:S(2)}) %collective-permute-start.2) | collective-permute-done | bytes 69664 | tf_op jit(solution)/shard_map/ppermute | solution.py:588
  30.5 5.3 %key_part.1 = (bf16[1024,128]{1,0:T(8,128)(2,1)}, f32[2,8,128]{2,1,0:T(8,128)}, f32[1024,128]{1,0:T(8,128)}, f32[1024,128]{1,0:T(8,128)}) custom-call(bf16[272,128]{1,0:T(8,128)(2,1)} %get-tuple-element.64.refs_0_, bf16[272,128]{1,0:T(8,128)(2,1)} %copy-done.11, bf16[272,128]{1,0:T(8,128)(2,1)} %copy-done.12, bf16[272,128]{1,0:T(8,128)(2,1)} %copy-done.13, ...), custom_call_target="tpu_custom_call" | custom-call | tf_op jit(solution)/shard_map/key_part/pallas_call | solution.py:273
  36.6 8.8 %local_part.1 = (bf16[3,1024,128]{2,1,0:T(8,128)(2,1)}, f32[1024,128]{1,0:T(8,128)}, f32[1024,128]{1,0:T(8,128)}, f32[1024,128]{1,0:T(8,128)}, f32[1024,128]{1,0...) custom-call(bf16[3,256,128]{2,1,0:T(8,128)(2,1)} %get-tuple-element., ...), custom_call_target="tpu_custom_call" | custom-call | tf_op jit(solution)/shard_map/local_part/pallas_call | solution.py:372
  45.4 3.3 %collective-permute-start.10 = (f32[128,128]{1,0:T(8,128)}, f32[128,128]{1,0:T(8,128)S(1)}, u32[]{:S(2)}, u32[]{:S(2)}) collective-permute-start(f32[128,128]{1,0:T(8,128)} %get-tuple-element.91), channel_id=1, source_target_pairs={{0,4},{1,5},{2,6},{3,7},{4,0},{5,1},{6,2},{7,3},{8,12},{9,13},{10,... | collective-permute-start | bytes 196616 | tf_op jit(solution)/shard_map/ppermute | solution.py:633
  48.8 2.5 %collective-permute-done.10.refs_21_.refs_22_ = f32[128,128]{1,0:T(8,128)S(1)} collective-permute-done((f32[128,128]{1,0:T(8,128)}, f32[128,128]{1,0:T(8,128)S(1)}, u32[]{:S(2)}, u32[]{:S(2)}) %collective-permute-start.10) | collective-permute-done | bytes 65568 | tf_op jit(solution)/shard_map/ppermute | solution.py:633
  51.9 5.7 %final_part.2 = (bf16[128,128]{1,0:T(8,128)(2,1)}, f32[3,128,128]{2,1,0:T(8,128)}, f32[2,1,128]{2,1,0:T(1,128)}, f32[16,128]{1,0:T(8,128)}, f32[3,8,128]{2,1,0:T...) custom-call(bf16[1024,128]{1,0:T(8,128)(2,1)} %get-tuple-element.72.refs_0_, ...), custom_call_target="tpu_custom_call" | custom-call | tf_op jit(solution)/shard_map/final_part/pallas_call | solution.py:512
  57.6 1.5 %collective-permute-start.14 = (f32[3,8,128]{2,1,0:T(8,128)}, f32[3,8,128]{2,1,0:T(8,128)S(1)}, u32[]{:S(2)}, u32[]{:S(2)}) collective-permute-start(f32[3,8,128]{2,1,0:T(8,128)} %get-tuple-element.102), channel_id=1, source_target_pairs={{4,0},{5,1},{6,2},{7,3},{12,8},{13,9},{14,10},{15,11},{20,16},{21,... | collective-permute-start | bytes 36872 | tf_op jit(solution)/shard_map/ppermute | solution.py:598
  59.1 8.7 %final_part.3 = (f32[3,896,128]{2,1,0:T(8,128)}, f32[2,7,128]{2,1,0:T(8,128)}, f32[16,128]{1,0:T(8,128)}, bf16[256,128]{1,0:T(8,128)(2,1)}, bf16[256,128]{1,0:T(...) custom-call(bf16[1024,128]{1,0:T(8,128)(2,1)} %get-tuple-element.72.refs_0_, ...), custom_call_target="tpu_custom_call" | custom-call | tf_op jit(solution)/shard_map/final_part/pallas_call | solution.py:512
  68.4 2.8 %input_part.1 = (bf16[784,128]{1,0:T(8,128)(2,1)}, bf16[784,128]{1,0:T(8,128)(2,1)}, bf16[784,128]{1,0:T(8,128)(2,1)}, bf16[784,128]{1,0:T(8,128)(2,1)}) custom-call(f32[3,128,128]{2,1,0:T(8,128)} %get-tuple-element.100.refs_0_, f32[3,896,128]{2,1,0:T(8,128)} %get-tuple-element.101.refs_1_, f32[3,8,128]{2,1,0:T(8,128)} %copy-done.18, ...), custom_call_target="tpu_custom_call" | custom-call | tf_op jit(solution)/shard_map/input_part/pallas_call | solution.py:567
  71.2 3.0 %collective-permute-start.15 = (bf16[784,128]{1,0:T(8,128)(2,1)}, bf16[784,128]{1,0:T(8,128)(2,1)S(1)}, u32[]{:S(2)}, u32[]{:S(2)}) collective-permute-start(bf16[784,128]{1,0:T(8,128)(2,1)} %get-tuple-element.106), channel_id=1, source_target_pairs={{0,1},{1,0},{2,3},{3,2},{4,5},{5,4},{6,7},{7,6},{8,9},{9,8},{10,11... | collective-permute-start | bytes 602120 | tf_op jit(solution)/shard_map/ppermute | solution.py:588
  74.2 1.5 %collective-permute-start.17 = (bf16[784,128]{1,0:T(8,128)(2,1)}, bf16[784,128]{1,0:T(8,128)(2,1)S(1)}, u32[]{:S(2)}, u32[]{:S(2)}) collective-permute-start(bf16[784,128]{1,0:T(8,128)(2,1)} %get-tuple-element.108), channel_id=1, source_target_pairs={{0,3},{1,2},{2,1},{3,0},{4,7},{5,6},{6,5},{7,4},{8,11},{9,10},{10,... | collective-permute-start | bytes 602120 | tf_op jit(solution)/shard_map/ppermute | solution.py:588
  75.7 2.0 %collective-permute-start.11 = (bf16[256,128]{1,0:T(8,128)(2,1)S(1)}, bf16[256,128]{1,0:T(8,128)(2,1)S(1)}, u32[]{:S(2)}, u32[]{:S(2)}) collective-permute-start(bf16[256,128]{1,0:T(8,128)(2,1)S(1)} %copy-done.25), channel_id=1, source_target_pairs={{0,1},{1,0},{2,3},{3,2},{4,5},{5,4},{6,7},{7,6},{8,9},{9,8},{10,11... | collective-permute-start | bytes 196616 | tf_op jit(solution)/shard_map/ppermute | solution.py:588
  77.7 1.2 %collective-permute-done.18 = f32[16,128]{1,0:T(8,128)S(1)} collective-permute-done((f32[16,128]{1,0:T(8,128)S(1)}, f32[16,128]{1,0:T(8,128)S(1)}, u32[]{:S(2)}, u32[]{:S(2)}) %collective-permute-start.18) | collective-permute-done | bytes 8224 | tf_op jit(solution)/shard_map/ppermute | solution.py:607
  78.8 1.5 %collective-permute-start.19 = (f32[16,128]{1,0:T(8,128)S(1)}, f32[16,128]{1,0:T(8,128)S(1)}, u32[]{:S(2)}, u32[]{:S(2)}) collective-permute-start(f32[16,128]{1,0:T(8,128)S(1)} %add.9), channel_id=1, source_target_pairs={{0,16},{8,24},{16,0},{24,8},{1,17},{9,25},{17,1},{25,9},{2,18},{10... | collective-permute-start | bytes 24584 | tf_op jit(solution)/shard_map/ppermute | solution.py:607
  80.3 2.1 %collective-permute-done.19 = f32[16,128]{1,0:T(8,128)S(1)} collective-permute-done((f32[16,128]{1,0:T(8,128)S(1)}, f32[16,128]{1,0:T(8,128)S(1)}, u32[]{:S(2)}, u32[]{:S(2)}) %collective-permute-start.19) | collective-permute-done | bytes 8224 | tf_op jit(solution)/shard_map/ppermute | solution.py:607
  82.5 3.5 %collective-permute-start.20 = (f32[16,128]{1,0:T(8,128)S(1)}, f32[16,128]{1,0:T(8,128)S(1)}, u32[]{:S(2)}, u32[]{:S(2)}) collective-permute-start(f32[16,128]{1,0:T(8,128)S(1)} %add.10), channel_id=1, source_target_pairs={{0,4},{1,5},{2,6},{3,7},{4,0},{5,1},{6,2},{7,3},{8,12},{9,13},{10,... | collective-permute-start | bytes 24584 | tf_op jit(solution)/shard_map/ppermute | solution.py:607
  86.0 1.6 %collective-permute-done.20 = f32[16,128]{1,0:T(8,128)S(1)} collective-permute-done((f32[16,128]{1,0:T(8,128)S(1)}, f32[16,128]{1,0:T(8,128)S(1)}, u32[]{:S(2)}, u32[]{:S(2)}) %collective-permute-start.20) | collective-permute-done | bytes 8224 | tf_op jit(solution)/shard_map/ppermute | solution.py:607
  88.2 4.0 %collective-permute-done.23.refs_11_ = f32[16,128]{1,0:T(8,128)S(1)} collective-permute-done((f32[16,128]{1,0:T(8,128)S(1)}, f32[16,128]{1,0:T(8,128)S(1)}, u32[]{:S(2)}, u32[]{:S(2)}) %collective-permute-start.23) | collective-permute-done | bytes 8224 | tf_op jit(solution)/shard_map/ppermute | solution.py:588
  92.2 3.6 %collective-permute-done.22.refs_10_ = f32[16,128]{1,0:T(8,128)S(1)} collective-permute-done((f32[16,128]{1,0:T(8,128)S(1)}, f32[16,128]{1,0:T(8,128)S(1)}, u32[]{:S(2)}, u32[]{:S(2)}) %collective-permute-start.22) | collective-permute-done | bytes 8224 | tf_op jit(solution)/shard_map/ppermute | solution.py:588
  95.9 3.6 %collective-permute-done.21.refs_9_ = f32[16,128]{1,0:T(8,128)S(1)} collective-permute-done((f32[16,128]{1,0:T(8,128)S(1)}, f32[16,128]{1,0:T(8,128)S(1)}, u32[]{:S(2)}, u32[]{:S(2)}) %collective-permute-start.21) | collective-permute-done | bytes 8224 | tf_op jit(solution)/shard_map/ppermute | solution.py:588
  99.6 1.6 %collective-permute-start.13 = (bf16[256,128]{1,0:T(8,128)(2,1)S(1)}, bf16[256,128]{1,0:T(8,128)(2,1)S(1)}, u32[]{:S(2)}, u32[]{:S(2)}) collective-permute-start(bf16[256,128]{1,0:T(8,128)(2,1)S(1)} %copy-done.23), channel_id=1, source_target_pairs={{0,3},{1,2},{2,1},{3,0},{4,7},{5,6},{6,5},{7,4},{8,11},{9,10},{10,... | collective-permute-start | bytes 196616 | tf_op jit(solution)/shard_map/ppermute | solution.py:588
  101.1 2.7 %collective-permute-done.12.refs_2_ = bf16[256,128]{1,0:T(8,128)(2,1)S(1)} collective-permute-done((bf16[256,128]{1,0:T(8,128)(2,1)S(1)}, bf16[256,128]{1,0:T(8,128)(2,1)S(1)}, u32[]{:S(2)}, u32[]{:S(2)}) %collective-permute-start.12) | collective-permute-done | bytes 65568 | tf_op jit(solution)/shard_map/ppermute | solution.py:588
  103.8 1.0 collective-permute-done.13.refs_3_
  105.6 2.4 %unpack.1 = (bf16[256,512]{1,0:T(8,128)(2,1)}, bf16[256,512]{1,0:T(8,128)(2,1)}, bf16[256,512]{1,0:T(8,128)(2,1)}, bf16[256,512]{1,0:T(8,128)(2,1)}, f32[4,256]{...) custom-call(bf16[256,128]{1,0:T(8,128)(2,1)} %get-tuple-element.96.refs_0_, ...), custom_call_target="tpu_custom_call" | custom-call | tf_op jit(solution)/shard_map/unpack/pallas_call | solution.py:164
  (79 shorter events, 6.6 us)
Async XLA Ops:
  4.2 31.6 %collective-permute-start.7 = (bf16[3,256,128]{2,1,0:T(8,128)(2,1)}, bf16[3,256,128]{2,1,0:T(8,128)(2,1)S(1)}, u32[]{:S(2)}, u32[]{:S(2)}) collective-permute-start(bf16[3,256,128]{2,1,0:T(8,128)(2,1)} %get-tuple-element.74), channel_id=1, source_target_pairs={{0,1},{1,0},{2,3},{3,2},{4,5},{5,4},{6,7},{7,6},{8,9},{9,8},{10,11... | collective-permute-start | bytes 589832 | tf_op jit(solution)/shard_map/ppermute | solution.py:588
  7.2 28.6 %collective-permute-start.8 = (bf16[3,256,128]{2,1,0:T(8,128)(2,1)}, bf16[3,256,128]{2,1,0:T(8,128)(2,1)S(1)}, u32[]{:S(2)}, u32[]{:S(2)}) collective-permute-start(bf16[3,256,128]{2,1,0:T(8,128)(2,1)} %get-tuple-element.75), channel_id=1, source_target_pairs={{0,2},{1,3},{2,0},{3,1},{4,6},{5,7},{6,4},{7,5},{8,10},{9,11},{10,... | collective-permute-start | bytes 589832 | tf_op jit(solution)/shard_map/ppermute | solution.py:588
  8.8 27.1 %collective-permute-start.9 = (bf16[3,256,128]{2,1,0:T(8,128)(2,1)}, bf16[3,256,128]{2,1,0:T(8,128)(2,1)S(1)}, u32[]{:S(2)}, u32[]{:S(2)}) collective-permute-start(bf16[3,256,128]{2,1,0:T(8,128)(2,1)} %get-tuple-element.76), channel_id=1, source_target_pairs={{0,3},{1,2},{2,1},{3,0},{4,7},{5,6},{6,5},{7,4},{8,11},{9,10},{10,... | collective-permute-start | bytes 589832 | tf_op jit(solution)/shard_map/ppermute | solution.py:588
  8.8 9.2 %collective-permute-start = (bf16[272,128]{1,0:T(8,128)(2,1)}, bf16[272,128]{1,0:T(8,128)(2,1)S(1)}, u32[]{:S(2)}, u32[]{:S(2)}) collective-permute-start(bf16[272,128]{1,0:T(8,128)(2,1)} %get-tuple-element.65), channel_id=1, source_target_pairs={{0,1},{1,0},{2,3},{3,2},{4,5},{5,4},{6,7},{7,6},{8,9},{9,8},{10,11... | collective-permute-start | bytes 208904 | tf_op jit(solution)/shard_map/ppermute | solution.py:588
  10.7 0.7 collective-permute-start.3
  11.4 18.6 %copy-start.7 = (bf16[3,8,128]{2,1,0:T(8,128)(2,1)}, bf16[3,8,128]{2,1,0:T(8,128)(2,1)S(1)}, u32[]{:S(2)}) copy-start(bf16[3,8,128]{2,1,0:T(8,128)(2,1)S(1)} %collective-permute-done.3.refs_4_.refs_2_) | copy-start | bytes 18436
  11.4 0.7 collective-permute-start.4
  12.0 17.9 %copy-start.8 = (bf16[3,8,128]{2,1,0:T(8,128)(2,1)}, bf16[3,8,128]{2,1,0:T(8,128)(2,1)S(1)}, u32[]{:S(2)}) copy-start(bf16[3,8,128]{2,1,0:T(8,128)(2,1)S(1)} %collective-permute-done.4.refs_5_.refs_3_) | copy-start | bytes 18436
  12.1 0.7 collective-permute-start.5
  12.7 17.2 %copy-start.9 = (bf16[3,8,128]{2,1,0:T(8,128)(2,1)}, bf16[3,8,128]{2,1,0:T(8,128)(2,1)S(1)}, u32[]{:S(2)}) copy-start(bf16[3,8,128]{2,1,0:T(8,128)(2,1)S(1)} %collective-permute-done.5.refs_6_.refs_4_) | copy-start | bytes 18436
  12.7 0.7 collective-permute-start.6
  13.4 16.5 %copy-start.10 = (bf16[3,8,128]{2,1,0:T(8,128)(2,1)}, bf16[3,8,128]{2,1,0:T(8,128)(2,1)S(1)}, u32[]{:S(2)}) copy-start(bf16[3,8,128]{2,1,0:T(8,128)(2,1)S(1)} %collective-permute-done.6.refs_7_.refs_5_) | copy-start | bytes 18436
  13.4 13.3 %collective-permute-start.1 = (bf16[272,128]{1,0:T(8,128)(2,1)}, bf16[272,128]{1,0:T(8,128)(2,1)S(1)}, u32[]{:S(2)}, u32[]{:S(2)}) collective-permute-start(bf16[272,128]{1,0:T(8,128)(2,1)} %get-tuple-element.66), channel_id=1, source_target_pairs={{0,2},{1,3},{2,0},{3,1},{4,6},{5,7},{6,4},{7,5},{8,10},{9,11},{10,... | collective-permute-start | bytes 208904 | tf_op jit(solution)/shard_map/ppermute | solution.py:588
  18.0 11.9 %collective-permute-start.2 = (bf16[272,128]{1,0:T(8,128)(2,1)}, bf16[272,128]{1,0:T(8,128)(2,1)S(1)}, u32[]{:S(2)}, u32[]{:S(2)}) collective-permute-start(bf16[272,128]{1,0:T(8,128)(2,1)} %get-tuple-element.67), channel_id=1, source_target_pairs={{0,3},{1,2},{2,1},{3,0},{4,7},{5,6},{6,5},{7,4},{8,11},{9,10},{10,... | collective-permute-start | bytes 208904 | tf_op jit(solution)/shard_map/ppermute | solution.py:588
  45.4 5.8 %collective-permute-start.10 = (f32[128,128]{1,0:T(8,128)}, f32[128,128]{1,0:T(8,128)S(1)}, u32[]{:S(2)}, u32[]{:S(2)}) collective-permute-start(f32[128,128]{1,0:T(8,128)} %get-tuple-element.91), channel_id=1, source_target_pairs={{0,4},{1,5},{2,6},{3,7},{4,0},{5,1},{6,2},{7,3},{8,12},{9,13},{10,... | collective-permute-start | bytes 196616 | tf_op jit(solution)/shard_map/ppermute | solution.py:633
  57.6 10.2 %collective-permute-start.14 = (f32[3,8,128]{2,1,0:T(8,128)}, f32[3,8,128]{2,1,0:T(8,128)S(1)}, u32[]{:S(2)}, u32[]{:S(2)}) collective-permute-start(f32[3,8,128]{2,1,0:T(8,128)} %get-tuple-element.102), channel_id=1, source_target_pairs={{4,0},{5,1},{6,2},{7,3},{12,8},{13,9},{14,10},{15,11},{20,16},{21,... | collective-permute-start | bytes 36872 | tf_op jit(solution)/shard_map/ppermute | solution.py:598
  67.8 31.7 %copy-start.24 = (bf16[256,128]{1,0:T(8,128)(2,1)S(1)}, bf16[256,128]{1,0:T(8,128)(2,1)}, u32[]{:S(2)}) copy-start(bf16[256,128]{1,0:T(8,128)(2,1)} %get-tuple-element.98) | copy-start | bytes 196612
  67.8 31.8 %copy-start.23 = (bf16[256,128]{1,0:T(8,128)(2,1)S(1)}, bf16[256,128]{1,0:T(8,128)(2,1)}, u32[]{:S(2)}) copy-start(bf16[256,128]{1,0:T(8,128)(2,1)} %get-tuple-element.99) | copy-start | bytes 196612
  71.2 33.6 %collective-permute-start.15 = (bf16[784,128]{1,0:T(8,128)(2,1)}, bf16[784,128]{1,0:T(8,128)(2,1)S(1)}, u32[]{:S(2)}, u32[]{:S(2)}) collective-permute-start(bf16[784,128]{1,0:T(8,128)(2,1)} %get-tuple-element.106), channel_id=1, source_target_pairs={{0,1},{1,0},{2,3},{3,2},{4,5},{5,4},{6,7},{7,6},{8,9},{9,8},{10,11... | collective-permute-start | bytes 602120 | tf_op jit(solution)/shard_map/ppermute | solution.py:588
  74.2 30.6 %collective-permute-start.16 = (bf16[784,128]{1,0:T(8,128)(2,1)}, bf16[784,128]{1,0:T(8,128)(2,1)S(1)}, u32[]{:S(2)}, u32[]{:S(2)}) collective-permute-start(bf16[784,128]{1,0:T(8,128)(2,1)} %get-tuple-element.107), channel_id=1, source_target_pairs={{0,2},{1,3},{2,0},{3,1},{4,6},{5,7},{6,4},{7,5},{8,10},{9,11},{10,... | collective-permute-start | bytes 602120 | tf_op jit(solution)/shard_map/ppermute | solution.py:588
  74.2 30.7 %collective-permute-start.17 = (bf16[784,128]{1,0:T(8,128)(2,1)}, bf16[784,128]{1,0:T(8,128)(2,1)S(1)}, u32[]{:S(2)}, u32[]{:S(2)}) collective-permute-start(bf16[784,128]{1,0:T(8,128)(2,1)} %get-tuple-element.108), channel_id=1, source_target_pairs={{0,3},{1,2},{2,1},{3,0},{4,7},{5,6},{6,5},{7,4},{8,11},{9,10},{10,... | collective-permute-start | bytes 602120 | tf_op jit(solution)/shard_map/ppermute | solution.py:588
  75.7 23.9 %collective-permute-start.11 = (bf16[256,128]{1,0:T(8,128)(2,1)S(1)}, bf16[256,128]{1,0:T(8,128)(2,1)S(1)}, u32[]{:S(2)}, u32[]{:S(2)}) collective-permute-start(bf16[256,128]{1,0:T(8,128)(2,1)S(1)} %copy-done.25), channel_id=1, source_target_pairs={{0,1},{1,0},{2,3},{3,2},{4,5},{5,4},{6,7},{7,6},{8,9},{9,8},{10,11... | collective-permute-start | bytes 196616 | tf_op jit(solution)/shard_map/ppermute | solution.py:588
  77.7 1.2 %collective-permute-start.18 = (f32[16,128]{1,0:T(8,128)S(1)}, f32[16,128]{1,0:T(8,128)S(1)}, u32[]{:S(2)}, u32[]{:S(2)}) collective-permute-start(f32[16,128]{1,0:T(8,128)S(1)} %copy-done.22), channel_id=1, source_target_pairs={{0,8},{8,0},{16,24},{24,16},{1,9},{9,1},{17,25},{25,17},{2,10},{10... | collective-permute-start | bytes 24584 | tf_op jit(solution)/shard_map/ppermute | solution.py:607
  78.8 3.7 %collective-permute-start.19 = (f32[16,128]{1,0:T(8,128)S(1)}, f32[16,128]{1,0:T(8,128)S(1)}, u32[]{:S(2)}, u32[]{:S(2)}) collective-permute-start(f32[16,128]{1,0:T(8,128)S(1)} %add.9), channel_id=1, source_target_pairs={{0,16},{8,24},{16,0},{24,8},{1,17},{9,25},{17,1},{25,9},{2,18},{10... | collective-permute-start | bytes 24584 | tf_op jit(solution)/shard_map/ppermute | solution.py:607
  82.5 5.2 %collective-permute-start.20 = (f32[16,128]{1,0:T(8,128)S(1)}, f32[16,128]{1,0:T(8,128)S(1)}, u32[]{:S(2)}, u32[]{:S(2)}) collective-permute-start(f32[16,128]{1,0:T(8,128)S(1)} %add.10), channel_id=1, source_target_pairs={{0,4},{1,5},{2,6},{3,7},{4,0},{5,1},{6,2},{7,3},{8,12},{9,13},{10,... | collective-permute-start | bytes 24584 | tf_op jit(solution)/shard_map/ppermute | solution.py:607
  87.7 17.2 %copy-start.17 = (f32[16,128]{1,0:T(8,128)}, f32[16,128]{1,0:T(8,128)S(1)}, u32[]{:S(2)}) copy-start(f32[16,128]{1,0:T(8,128)S(1)} %add.11.refs_8_) | copy-start | bytes 24580
  87.7 4.5 %collective-permute-start.23 = (f32[16,128]{1,0:T(8,128)S(1)}, f32[16,128]{1,0:T(8,128)S(1)}, u32[]{:S(2)}, u32[]{:S(2)}) collective-permute-start(f32[16,128]{1,0:T(8,128)S(1)} %add.11.refs_8_), channel_id=1, source_target_pairs={{0,3},{1,2},{2,1},{3,0},{4,7},{5,6},{6,5},{7,4},{8,11},{9,10},{10,... | collective-permute-start | bytes 24584 | tf_op jit(solution)/shard_map/ppermute | solution.py:588
  92.2 12.6 %copy-start.19 = (f32[16,128]{1,0:T(8,128)}, f32[16,128]{1,0:T(8,128)S(1)}, u32[]{:S(2)}) copy-start(f32[16,128]{1,0:T(8,128)S(1)} %collective-permute-done.23.refs_11_) | copy-start | bytes 24580
  92.2 3.7 %collective-permute-start.22 = (f32[16,128]{1,0:T(8,128)S(1)}, f32[16,128]{1,0:T(8,128)S(1)}, u32[]{:S(2)}, u32[]{:S(2)}) collective-permute-start(f32[16,128]{1,0:T(8,128)S(1)} %add.11.refs_8_), channel_id=1, source_target_pairs={{0,2},{1,3},{2,0},{3,1},{4,6},{5,7},{6,4},{7,5},{8,10},{9,11},{10,... | collective-permute-start | bytes 24584 | tf_op jit(solution)/shard_map/ppermute | solution.py:588
  95.9 3.7 %collective-permute-start.21 = (f32[16,128]{1,0:T(8,128)S(1)}, f32[16,128]{1,0:T(8,128)S(1)}, u32[]{:S(2)}, u32[]{:S(2)}) collective-permute-start(f32[16,128]{1,0:T(8,128)S(1)} %add.11.refs_8_), channel_id=1, source_target_pairs={{0,1},{1,0},{2,3},{3,2},{4,5},{5,4},{6,7},{7,6},{8,9},{9,8},{10,11... | collective-permute-start | bytes 24584 | tf_op jit(solution)/shard_map/ppermute | solution.py:588
  99.5 4.3 %collective-permute-start.12 = (bf16[256,128]{1,0:T(8,128)(2,1)S(1)}, bf16[256,128]{1,0:T(8,128)(2,1)S(1)}, u32[]{:S(2)}, u32[]{:S(2)}) collective-permute-start(bf16[256,128]{1,0:T(8,128)(2,1)S(1)} %copy-done.24), channel_id=1, source_target_pairs={{0,2},{1,3},{2,0},{3,1},{4,6},{5,7},{6,4},{7,5},{8,10},{9,11},{10,... | collective-permute-start | bytes 196616 | tf_op jit(solution)/shard_map/ppermute | solution.py:588
  99.6 5.2 %collective-permute-start.13 = (bf16[256,128]{1,0:T(8,128)(2,1)S(1)}, bf16[256,128]{1,0:T(8,128)(2,1)S(1)}, u32[]{:S(2)}, u32[]{:S(2)}) collective-permute-start(bf16[256,128]{1,0:T(8,128)(2,1)S(1)} %copy-done.23), channel_id=1, source_target_pairs={{0,3},{1,2},{2,1},{3,0},{4,7},{5,6},{6,5},{7,4},{8,11},{9,10},{10,... | collective-permute-start | bytes 196616 | tf_op jit(solution)/shard_map/ppermute | solution.py:588
  (18 other events, 60.6 us)

commit v2 on v1

v2 whole, which is shorter than its diff:
```python
import functools

import jax
import jax.numpy as jnp
from jax import lax
from jax.experimental import pallas as pl
from jax.experimental.pallas import tpu as pltpu
from jax.sharding import PartitionSpec as P

F32 = jnp.float32
BF16 = jnp.bfloat16
CHUNK = 128
VMEM = pl.BlockSpec(memory_space=pltpu.VMEM)


def params(**more):
    return pltpu.CompilerParams(vmem_limit_bytes=40 * 1024 * 1024, **more)


def cost(microseconds):
    return pl.CostEstimate(
        flops=int(microseconds * 1.0e9), bytes_accessed=int(microseconds * 3.0e6), transcendentals=0
    )


def split(x):
    high = x.astype(BF16)
    return high, (x - high.astype(F32)).astype(BF16)


def nn(a, b):
    left = jnp.concatenate([a[0], a[0], a[1]], axis=1)
    right = jnp.concatenate([b[0], b[1], b[0]], axis=0)
    return jnp.dot(left, right, preferred_element_type=F32)


def nt(a, b):
    left = jnp.concatenate([a[0], a[0], a[1]], axis=1)
    right = jnp.concatenate([b[0], b[1], b[0]], axis=1)
    return lax.dot_general(left, right, (((1,), (1,)), ((), ())), preferred_element_type=F32)


def rows_of(*pairs):
    return tuple(jnp.concatenate(parts, axis=0) for parts in zip(*pairs))


def columns_of(*pairs):
    return tuple(jnp.concatenate(parts, axis=1) for parts in zip(*pairs))


def grid_ids():
    rows = lax.broadcasted_iota(jnp.int32, (CHUNK, CHUNK), 0)
    columns = lax.broadcasted_iota(jnp.int32, (CHUNK, CHUNK), 1)
    return rows, columns


def as_column(row, rows, columns):
    return jnp.sum(jnp.where(rows == columns, row, 0.0), axis=1, keepdims=True)


def as_row(column, rows, columns):
    return jnp.sum(jnp.where(rows == columns, column, 0.0), axis=0, keepdims=True)


def decay_forms(decay_row, rows, columns):
    g_column = jnp.sum(jnp.where(columns <= rows, decay_row, 0.0), axis=1, keepdims=True)
    g_row = as_row(g_column, rows, columns)
    g_last = jnp.sum(decay_row, axis=1, keepdims=True)
    return g_column, g_row, g_last


def place_in_group(axis, heads):
    index = lax.axis_index(axis)
    return lax.rem(index, heads), lax.div(index, heads)


def peer(me, heads, step):
    return me ^ step if heads & (heads - 1) == 0 else lax.rem(heads - me + step, heads)


def aligned(index, size):
    return pl.ds(pl.multiple_of(index * size, size), size)


def three_rows(values):
    high = values.astype(BF16).astype(F32)
    middle = (values - high).astype(BF16).astype(F32)
    return high, middle, values - high - middle


def pack_kernel(heads, axis, *refs):
    (q_ref, k_ref, v_ref, o_ref), rates, refs = refs[:4], refs[4:6], refs[6:]
    blocks, tails, lines = refs[:heads], refs[heads : 2 * heads], refs[-1]
    me, _ = place_in_group(axis, heads)
    frames, width = q_ref.shape[0], q_ref.shape[1] // heads
    per = frames // CHUNK
    lines[...] = jnp.zeros_like(lines)
    line_ids = lax.broadcasted_iota(jnp.int32, (heads, frames), 0)
    for step in range(heads):
        target = peer(me, heads, step)
        lanes = aligned(target, width)
        for place, ref in enumerate((k_ref, v_ref, q_ref, o_ref)):
            blocks[step][place * frames : (place + 1) * frames, :] = ref[:, lanes]
        for kind in range(2):
            line = jnp.where(line_ids == target, rates[kind][...], 0.0)
            line = jnp.sum(line, axis=0, keepdims=True)
            for part, line in enumerate(three_rows(line)):
                for c in range(per):
                    at = (part * 2 + kind) * per + c
                    lines[at : at + 1, :] = line[:, c * CHUNK : (c + 1) * CHUNK]
        blocks[step][4 * frames :, :] = lines[...].astype(BF16)
    for head in range(heads):
        for place, ref in enumerate((k_ref, v_ref, q_ref)):
            tails[head][place] = ref[frames - 8 : frames, head * width : (head + 1) * width]


def line_rows(frames):
    return -(-6 * (frames // CHUNK) // 16) * 16


def pack(heads, axis, q, k, v, o, decays, betas):
    frames, features = q.shape
    width = features // heads
    out_shape = [jax.ShapeDtypeStruct((4 * frames + line_rows(frames), width), BF16)] * heads
    out_shape += [jax.ShapeDtypeStruct((3, 8, width), BF16)] * heads
    outs = pl.pallas_call(
        functools.partial(pack_kernel, heads, axis),
        out_shape=out_shape,
        in_specs=[VMEM] * 6,
        out_specs=[VMEM] * len(out_shape),
        scratch_shapes=[pltpu.VMEM((line_rows(frames), CHUNK), F32)],
        compiler_params=params(),
        cost_estimate=cost(2),
        name="pack",
    )(q, k, v, o, decays, betas)
    return outs[:heads], outs[heads:]


def unpack_kernel(heads, axis, *refs):
    grads, refs = refs[:heads], refs[heads:]
    outs, rate_outs = refs[:4], refs[4:]
    me, _ = place_in_group(axis, heads)
    width = grads[0].shape[1]
    frames = outs[0].shape[0]
    per = frames // CHUNK
    line_ids = lax.broadcasted_iota(jnp.int32, (heads, CHUNK), 0)
    for step in range(heads):
        source = peer(me, heads, step)
        for place in range(4):
            outs[place][:, aligned(source, width)] = grads[step][
                place * frames : (place + 1) * frames, :
            ]
        lines = grads[step][4 * frames :, :].astype(F32)
        for kind, out in enumerate(rate_outs):
            for c in range(per):
                line = sum(
                    lines[(part * 2 + kind) * per + c : (part * 2 + kind) * per + c + 1, :]
                    for part in range(3)
                )
                at = slice(c * CHUNK, (c + 1) * CHUNK)
                out[:, at] = jnp.where(line_ids == source, line, 0.0 if step == 0 else out[:, at])


def unpack(heads, axis, frames, grads):
    width = grads[0].shape[1]
    out_shape = [jax.ShapeDtypeStruct((frames, heads * width), BF16)] * 4
    out_shape += [jax.ShapeDtypeStruct((heads, frames), F32)] * 2
    return pl.pallas_call(
        functools.partial(unpack_kernel, heads, axis),
        out_shape=out_shape,
        in_specs=[VMEM] * heads,
        out_specs=[VMEM] * 6,
        compiler_params=params(),
        cost_estimate=cost(2),
        name="unpack",
    )(*grads)


def convolve(padded_ref, place, start, taps):
    total = taps[0:1] * padded_ref[place, 5 + start : 5 + start + CHUNK, :]
    for offset in range(1, 4):
        at = 5 + start + offset
        total = total + taps[offset : offset + 1] * padded_ref[place, at : at + CHUNK, :]
    return total


def tail_of(tails, place):
    tail = tails[0][place].astype(F32)
    for other in tails[1:]:
        tail = tail + other[place].astype(F32)
    return tail


def activated(c_value, unit):
    y = c_value * jax.nn.sigmoid(c_value)
    if unit:
        y = y * lax.rsqrt(jnp.sum(y * y, axis=1, keepdims=True) + 1e-06)
    return y


def ratio_forms(g_column, g_row, rows, columns):
    inclusive, above = columns <= rows, columns >= rows
    ratio = jnp.where(inclusive, jnp.exp(jnp.where(inclusive, g_column - g_row, 0.0)), 0.0)
    ratio_t = jnp.where(above, jnp.exp(jnp.where(above, g_row - g_column, 0.0)), 0.0)
    return ratio, ratio_t


def local_kernel(heads, axis, *refs):
    received, tails, tap_refs, refs = refs[:heads], refs[heads : 2 * heads], refs[2 * heads : 2 * heads + 3], refs[2 * heads + 3 :]
    (raw, rate_out, k_out, q_out, v_out, p_out, u_out, w_out, x_out, y_out) = refs[:10]
    (mt_out, bt_out, ct_out, state_out, back_out) = refs[10:15]
    inverse, padded, lower_high, lower_low = refs[15:]
    me, group = place_in_group(axis, heads)
    length, width = k_out.shape
    frames = length // heads
    per = frames // CHUNK
    chunk_count = length // CHUNK
    for place in range(3):
        padded[place, 0:8, :] = tail_of(tails, place)
    for step in range(heads):
        source = peer(me, heads, step)
        for place in range(4):
            block = received[step][place * frames : (place + 1) * frames, :]
            raw[place, aligned(source, frames), :] = block
            if place < 3:
                at = pl.ds(pl.multiple_of(source * frames + 8, 8), frames)
                padded[place, at, :] = block.astype(F32)
        lines = received[step][4 * frames :, :].astype(F32)
        for kind in range(2):
            for c in range(per):
                at = kind * per + c
                line = lines[at : at + 1] + lines[at + 2 * per : at + 2 * per + 1]
                line = line + lines[at + 4 * per : at + 4 * per + 1]
                rate_out[kind, pl.ds(source * per + c, 1), :] = line
    rows, columns = grid_ids()
    eye = jnp.where(rows == columns, 1.0, 0.0)
    masks = []
    for level in range(CHUNK.bit_length() - 1):
        masks.append(
            ((rows >> (level + 1)) == (columns >> (level + 1)))
            & ((rows >> level) != (columns >> level))
            & (rows > columns)
        )
    taps = [ref[:, aligned(me, width)] for ref in tap_refs]
    for c in range(chunk_count):
        at = pl.ds(c * CHUNK, CHUNK)
        g_column, g_row, g_last = decay_forms(rate_out[0, c : c + 1, :], rows, columns)
        beta_column = as_column(rate_out[1, c : c + 1, :], rows, columns)
        keys = activated(convolve(padded, 0, c * CHUNK, taps[0]), True)
        k_out[at, :] = keys
        k_pair = split(keys)
        below = columns < rows
        ratio = jnp.exp(jnp.where(below, g_column - g_row, 0.0))
        lower = jnp.where(below, beta_column * ratio * nt(k_pair, k_pair), 0.0)
        high, low = split(lower)
        lower_high[at, :] = high
        lower_low[at, :] = low
        inverse[at, :] = eye - jnp.where(masks[0], lower, 0.0)
    zero = jnp.zeros((CHUNK, CHUNK), BF16)
    for level in range(1, len(masks)):
        halfway = []
        for c in range(chunk_count):
            at = pl.ds(c * CHUNK, CHUNK)
            off = (
                jnp.where(masks[level], lower_high[at, :], zero),
                jnp.where(masks[level], lower_low[at, :], zero),
            )
            halfway.append(nn(off, split(inverse[at, :])))
        for c in range(chunk_count):
            at = pl.ds(c * CHUNK, CHUNK)
            t_value = inverse[at, :]
            inverse[at, :] = t_value - nn(split(t_value), split(halfway[c]))

    for c in range(chunk_count):
        at = pl.ds(c * CHUNK, CHUNK)
        g_column, g_row, g_last, beta_row, beta_column = chunk_forms(rate_out, c, rows, columns)
        ratio, ratio_t = ratio_forms(g_column, g_row, rows, columns)
        start_column, start_row = jnp.exp(g_column), jnp.exp(g_row)
        tail_column, tail_row = jnp.exp(g_last - g_column), jnp.exp(g_last - g_row)
        values = activated(convolve(padded, 1, c * CHUNK, taps[1]), False)
        queries = activated(convolve(padded, 2, c * CHUNK, taps[2]), True)
        q_out[at, :], v_out[at, :] = queries, values
        keys = k_out[at, :]
        q_pair, k_pair = split(queries), split(keys)
        p_out[at, :] = ratio * nt(q_pair, k_pair)
        pt = ratio_t * nt(k_pair, q_pair)
        t_value = inverse[at, :]
        u_w = nn(
            split(t_value),
            columns_of(split(beta_column * values), split(beta_column * start_column * keys)),
        )
        u_value, w_value = u_w[:, :width], u_w[:, width:]
        cotangent = raw[3, at, :]
        p_high, p_low = split(pt)
        first = jnp.dot(
            jnp.concatenate([p_high, p_low], axis=1),
            jnp.concatenate([cotangent, cotangent], axis=0),
            preferred_element_type=F32,
        )
        x_y = nn(split(t_value.T), columns_of(split(first), split(tail_column * keys)))
        x_value, y_value = x_y[:, :width], x_y[:, width:]
        keys_t, queries_t = keys.T, queries.T
        b_m = nn(split(keys_t * tail_row), columns_of(split(u_value), split(w_value)))
        whole = jnp.exp(g_last)
        bt_out[c] = b_m[:, :width]
        mt_out[c] = whole * eye - b_m[:, width:]
        ct_out[c] = nn(
            columns_of(split(queries_t * start_row), split(keys_t * (-beta_row * start_row))),
            rows_of((cotangent, jnp.zeros_like(cotangent)), split(x_value)),
        )
        u_out[at, :], w_out[at, :], x_out[at, :], y_out[at, :] = u_value, w_value, x_value, y_value

    state = bt_out[0]
    back = ct_out[chunk_count - 1]
    for c in range(1, chunk_count):
        other = chunk_count - 1 - c
        state = nn(split(mt_out[c]), split(state)) + bt_out[c]
        back = nn(split(mt_out[other].T), split(back)) + ct_out[other]
    if lax.axis_size(axis) == 2 * heads:
        state_out[...] = jnp.where(group == 0, state, back)
    else:
        state_out[...] = state
    back_out[...] = back


def local_part(heads, axis, frames, received, tails, tap_args):
    width = received[0].shape[1]
    length = heads * frames
    chunk_count = length // CHUNK
    tall = pltpu.VMEM((length, width), F32)
    square = pltpu.VMEM((chunk_count, width, width), F32)
    one = jax.ShapeDtypeStruct((width, width), F32)
    out_shape = [pltpu.VMEM((4, length, width), BF16), pltpu.VMEM((2, chunk_count, CHUNK), F32)]
    out_shape += [tall] * 8 + [square] * 3 + [one] * 2
    return pl.pallas_call(
        functools.partial(local_kernel, heads, axis),
        out_shape=out_shape,
        in_specs=[VMEM] * (2 * heads + 3),
        out_specs=[VMEM] * len(out_shape),
        scratch_shapes=[
            pltpu.VMEM((length, CHUNK), F32),
            pltpu.VMEM((3, length + 8, width), F32),
            pltpu.VMEM((length, CHUNK), BF16),
            pltpu.VMEM((length, CHUNK), BF16),
        ],
        compiler_params=params(),
        cost_estimate=cost(10),
        name="local_part",
    )(*received, *tails, *tap_args)


def chunk_forms(rate, c, rows, columns):
    decay_row, beta_row = rate[0, c : c + 1, :], rate[1, c : c + 1, :]
    g_column, g_row, g_last = decay_forms(decay_row, rows, columns)
    return g_column, g_row, g_last, beta_row, as_column(beta_row, rows, columns)


def chunk_back(c, forms, given, ids, padded, taps, sums):
    g_column, g_row, g_last, beta_row, beta_column = forms
    keys, queries, values, u_value, x_value, state, back, cotangent, kept_row = given
    rows, columns = ids
    width = keys.shape[1]
    start_column = jnp.exp(g_column)
    tail_column = jnp.exp(g_last - g_column)
    ratio, ratio_t = ratio_forms(g_column, g_row, rows, columns)
    k_pair, q_pair = split(keys), split(queries)
    u_pair, x_pair = split(u_value), split(x_value)
    s_pair, d_pair = split(state), split(back)
    ox_pair = rows_of((cotangent, jnp.zeros_like(cotangent)), x_pair)
    ox_u = nt(ox_pair, u_pair)
    u_ox = nt(u_pair, ox_pair)
    ox_s = nt(ox_pair, s_pair)
    u_d = nt(u_pair, d_pair)
    strict = jnp.where(columns < rows, beta_column * ratio, 0.0)
    strict_t = jnp.where(columns > rows, beta_row * ratio_t, 0.0)
    e_value = ratio * ox_u[:CHUNK]
    f_value = strict * ox_u[CHUNK:] + strict_t * u_ox[:, CHUNK:]
    e_t = ratio_t * u_ox[:, :CHUNK]
    d_queries = start_column * ox_s[:CHUNK] + nn(split(e_value), k_pair)
    d_keys = (
        tail_column * u_d
        - (beta_column * start_column) * ox_s[CHUNK:]
        + nn(columns_of(split(e_t), split(-f_value)), rows_of(q_pair, k_pair))
    )
    d_values = beta_column * x_value
    d_beta = jnp.sum(x_value * u_value, axis=1, keepdims=True) / beta_column
    d_g = jnp.sum(d_values * values, axis=1, keepdims=True)
    decay_row = kept_row - jnp.sum(jnp.where(rows >= columns, d_g, 0.0), axis=0, keepdims=True)
    made = []
    for place, (grad, unit) in enumerate(((d_keys, keys), (d_values, None), (d_queries, queries))):
        at = c * CHUNK + 5
        shifted = [padded[place, at + i : at + i + CHUNK, :] for i in range(4)]
        c_value = taps[place][0:1] * shifted[0]
        for offset in range(1, 4):
            c_value = c_value + taps[place][offset : offset + 1] * shifted[offset]
        gate = jax.nn.sigmoid(c_value)
        if unit is not None:
            y = c_value * gate
            scale = lax.rsqrt(jnp.sum(y * y, axis=1, keepdims=True) + 1e-06)
            grad = scale * (grad - unit * jnp.sum(unit * grad, axis=1, keepdims=True))
        grad = grad * (gate * (1.0 + c_value * (1.0 - gate)))
        made.append(grad)
        for offset in range(4):
            part = (grad * shifted[offset]).reshape(CHUNK // 8, 8, width)
            sums[place][offset] = sums[place][offset] + jnp.sum(part, axis=0)
    return made, decay_row, as_row(d_beta, rows, columns)


def state_kernel(heads, axis, *refs):
    raw, tails, refs = refs[0], refs[1 : 1 + heads], refs[1 + heads :]
    (rate, q_in, k_in, v_in, p_in, u_in, w_in, x_in, y_in), refs = refs[:9], refs[9:]
    tap_refs, (mt_in, bt_in, ct_in, state_in, back_in), refs = refs[:3], refs[3:8], refs[8:]
    u_out, x_out, states, backs, kept_out, conv_out, rate_grad, tap_out, rim_out = refs[:9]
    mixed_all, padded = refs[9:]
    me, group = place_in_group(axis, heads)
    length, width = q_in.shape
    chunk_count = length // CHUNK
    rows, columns = grid_ids()

    state = jnp.where(group > 0, state_in[...], 0.0)
    back = jnp.where(group < lax.axis_size(axis) // heads - 1, back_in[...], 0.0)
    states[0] = state
    backs[chunk_count] = back
    for c in range(chunk_count):
        other = chunk_count - 1 - c
        state = nn(split(mt_in[c]), split(state)) + bt_in[c]
        back = nn(split(mt_in[other].T), split(back)) + ct_in[other]
        states[c + 1] = state
        backs[other] = back

    for c in range(chunk_count):
        at = pl.ds(c * CHUNK, CHUNK)
        s_pair, d_pair = split(states[c]), split(backs[c + 1])
        g_column, g_row, g_last, beta_row, beta_column = chunk_forms(rate, c, rows, columns)
        u_value = u_in[at, :] - nn(split(w_in[at, :]), s_pair)
        x_value = x_in[at, :] + nn(split(y_in[at, :]), d_pair)
        mixed = jnp.exp(g_column) * nn(split(q_in[at, :]), s_pair)
        mixed = mixed + nn(split(p_in[at, :]), split(u_value))
        u_out[at, :], x_out[at, :] = u_value, x_value
        mixed_all[at, :] = mixed.astype(BF16)
        d_g = jnp.sum(raw[3, at, :].astype(F32) * mixed, axis=1, keepdims=True)
        kept = jnp.sum(states[c + 1] * backs[c + 1], axis=1, keepdims=True)
        kept_out[c : c + 1, :] = jnp.sum(
            jnp.where(rows >= columns, d_g, 0.0) + kept, axis=0, keepdims=True
        )

    for place in range(3):
        padded[place, 0:8, :] = tail_of(tails, place)
        padded[place, 8:, :] = raw[place, 0:CHUNK, :].astype(F32)
    taps = [ref[:, aligned(me, width)] for ref in tap_refs]
    sums = [[jnp.zeros((8, width), F32) for _ in range(4)] for _ in range(3)]
    at = pl.ds(0, CHUNK)
    given = (k_in[at, :], q_in[at, :], v_in[at, :], u_out[at, :], x_out[at, :])
    given += (states[0], backs[1], raw[3, at, :], kept_out[0:1, :])
    forms = chunk_forms(rate, 0, rows, columns)
    made, decay_row, beta_row = chunk_back(0, forms, given, (rows, columns), padded, taps, sums)
    rate_grad[0], rate_grad[1] = decay_row, beta_row
    for place in range(3):
        conv_out[place] = made[place]
        rim_out[place] = made[place][0:8]
        for offset in range(4):
            tap_out[4 * place + offset] = sums[place][offset]


def state_part(heads, axis, shared, more):
    length, width = shared[2 + heads].shape
    chunk_count = length // CHUNK
    tall = pltpu.VMEM((length, width), F32)
    chain = pltpu.VMEM((chunk_count + 1, width, width), F32)
    out_shape = [
        tall,
        tall,
        chain,
        chain,
        pltpu.VMEM((chunk_count, CHUNK), F32),
        pltpu.VMEM((3, CHUNK, width), F32),
        pltpu.VMEM((2, 1, CHUNK), F32),
        pltpu.VMEM((12, 8, width), F32),
        jax.ShapeDtypeStruct((3, 8, width), F32),
        pltpu.VMEM((length, width), BF16),
    ]
    args = [*shared, *more]
    return pl.pallas_call(
        functools.partial(state_kernel, heads, axis),
        out_shape=out_shape,
        in_specs=[VMEM] * len(args),
        out_specs=[VMEM] * len(out_shape),
        scratch_shapes=[
            pltpu.VMEM((3, CHUNK + 8, width), F32),
        ],
        compiler_params=params(),
        cost_estimate=cost(7),
        name="state_part",
    )(*args)


def final_kernel(heads, axis, *refs):
    raw, rate, q_in, k_in, v_in, u_in, x_in, states, backs, kept, tap_before = refs[:11]
    tap_refs, refs = refs[11:14], refs[14:]
    conv_out, rate_grad, tap_out, padded = refs
    me, _ = place_in_group(axis, heads)
    length, width = q_in.shape
    rows, columns = grid_ids()
    for place in range(3):
        padded[place, CHUNK - 8 :, :] = raw[place, CHUNK - 16 :, :].astype(F32)
    taps = [ref[:, aligned(me, width)] for ref in tap_refs]
    sums = [[tap_before[4 * place + offset] for offset in range(4)] for place in range(3)]
    for c in range(1, length // CHUNK):
        at = pl.ds(c * CHUNK, CHUNK)
        given = (k_in[at, :], q_in[at, :], v_in[at, :], u_in[at, :], x_in[at, :])
        given += (states[c], backs[c + 1], raw[3, at, :], kept[c : c + 1, :])
        forms = chunk_forms(rate, c, rows, columns)
        made, decay_row, beta_row = chunk_back(
            c, forms, given, (rows, columns), padded, taps, sums
        )
        rate_grad[0, c - 1 : c, :] = decay_row
        rate_grad[1, c - 1 : c, :] = beta_row
        for place in range(3):
            conv_out[place, (c - 1) * CHUNK : c * CHUNK, :] = made[place]
    tap_out[...] = jnp.zeros_like(tap_out)
    for place, row in ((0, 4), (1, 8), (2, 0)):
        for offset in range(4):
            tap_out[row + offset : row + offset + 1, aligned(me, width)] = jnp.sum(
                sums[place][offset], axis=0, keepdims=True
            )


def final_part(heads, axis, args):
    length, width = args[2].shape
    count = length // CHUNK - 1
    out_shape = [
        pltpu.VMEM((3, count * CHUNK, width), F32),
        pltpu.VMEM((2, count, CHUNK), F32),
        jax.ShapeDtypeStruct((16, heads * width), F32),
    ]
    return pl.pallas_call(
        functools.partial(final_kernel, heads, axis),
        out_shape=out_shape,
        in_specs=[VMEM] * len(args),
        out_specs=[VMEM] * 3,
        scratch_shapes=[pltpu.VMEM((3, length + 8, width), F32)],
        compiler_params=params(),
        cost_estimate=cost(8),
        name="final_part",
    )(*args)


def input_kernel(heads, axis, *refs):
    conv_first, conv_rest, rim, rate_first, rate_rest = refs[:5]
    tap_refs, mixed, refs = refs[5:8], refs[8], refs[9:]
    blocks, refs = refs[:heads], refs[heads:]
    extended, result, rate_grad, lines = refs
    me, _ = place_in_group(axis, heads)
    length, width = result.shape[1:]
    frames = length // heads
    per = frames // CHUNK
    early = conv_first.shape[1]
    rate_grad[:, 0 : early // CHUNK, :] = rate_first[...]
    rate_grad[:, early // CHUNK :, :] = rate_rest[...]
    taps = [ref[:, aligned(me, width)] for ref in tap_refs]
    for place in range(3):
        extended[place, 0:early, :] = conv_first[place]
        extended[place, early:length, :] = conv_rest[place]
        extended[place, length:, :] = rim[place]
        for c in range(length // CHUNK):
            start = c * CHUNK
            grad = taps[place][3:4] * extended[place, start : start + CHUNK, :]
            for offset in range(3):
                at = start + 3 - offset
                grad = grad + taps[place][offset : offset + 1] * extended[place, at : at + CHUNK, :]
            result[(place + 1) % 3, start : start + CHUNK, :] = grad.astype(BF16)
    lines[...] = jnp.zeros_like(lines)
    for step in range(heads):
        target = peer(me, heads, step)
        blocks[step][0:frames, :] = mixed[aligned(target, frames), :]
        for place in range(3):
            blocks[step][(1 + place) * frames : (2 + place) * frames, :] = result[
                place, aligned(target, frames), :
            ]
        for kind in range(2):
            for c in range(per):
                line = rate_grad[kind, pl.ds(target * per + c, 1), :]
                for part, value in enumerate(three_rows(line)):
                    at = (part * 2 + kind) * per + c
                    lines[at : at + 1, :] = value
        blocks[step][4 * frames :, :] = lines[...].astype(BF16)


def input_part(heads, axis, convs, rim, rate_grads, tap_args, mixed):
    length, width = convs[0].shape[1] + convs[1].shape[1], convs[0].shape[2]
    frames = length // heads
    out_shape = [jax.ShapeDtypeStruct((4 * frames + line_rows(frames), width), BF16)] * heads
    args = [*convs, rim, *rate_grads, *tap_args, mixed]
    return pl.pallas_call(
        functools.partial(input_kernel, heads, axis),
        out_shape=out_shape,
        in_specs=[VMEM] * len(args),
        out_specs=[VMEM] * heads,
        scratch_shapes=[
            pltpu.VMEM((3, length + 8, width), F32),
            pltpu.VMEM((3, length, width), BF16),
            pltpu.VMEM((2, length // CHUNK, CHUNK), F32),
            pltpu.VMEM((line_rows(frames), CHUNK), F32),
        ],
        compiler_params=params(),
        cost_estimate=cost(3),
        name="input_part",
    )(*args)


def on_chip(value):
    return pltpu.with_memory_space_constraint(value, pltpu.VMEM)


def trade_one(value, axis, heads, step):
    count = lax.axis_size(axis)
    if step == 0:
        return value
    pairs = [(d, d - d % heads + member(d % heads, heads, step)) for d in range(count)]
    return lax.ppermute(value, axis, pairs)


def trade(values, axis, heads):
    return [trade_one(value, axis, heads, step) for step, value in enumerate(values)]


def member(place, heads, step):
    return place ^ step if heads & (heads - 1) == 0 else (heads - place + step) % heads


def along(value, axis, steps):
    count = lax.axis_size(axis)
    return lax.ppermute(
        value, axis, [(d, d + steps) for d in range(count) if 0 <= d + steps < count]
    )


def sum_rounds(axes):
    outer, inner = (lax.axis_size(axis) for axis in axes)
    if outer & (outer - 1) or inner & (inner - 1):
        return None
    bits = [inner << place for place in range(outer.bit_length() - 1)]
    bits += [1 << place for place in range(inner.bit_length() - 1)]
    rounds = [bits[:1]] if len(bits) % 2 else []
    return rounds + [bits[at : at + 2] for at in range(len(bits) % 2, len(bits), 2)]


def sum_round(value, axes, masks):
    count = lax.axis_size(axes)

    def swapped(mask):
        return lax.ppermute(value, axes, [(d, d ^ mask) for d in range(count)])

    if len(masks) == 1:
        return value + swapped(masks[0])
    near, far = masks
    return (value + swapped(near)) + (swapped(far) + swapped(near | far))


def body(q, k, v, q_taps, k_taps, v_taps, log_decay, write_strength, cotangent):
    axis = "tm"
    heads = log_decay.shape[2]
    count = lax.axis_size(axis)
    groups = count // heads
    q, k, v, o = (pltpu.with_memory_space_constraint(a[0], pltpu.HBM) for a in (q, k, v, cotangent))
    decays, betas = (
        pltpu.with_memory_space_constraint(a[0].T, pltpu.HBM) for a in (log_decay, write_strength)
    )
    sends, tails = pack(heads, axis, q, k, v, o, decays, betas)
    blocks = [on_chip(b) for b in trade(sends, axis, heads)]
    tails = [
        on_chip(
            lax.ppermute(
                tails[head], axis, [(g * heads - 1, g * heads + head) for g in range(1, groups)]
            )
        )
        for head in range(heads)
    ]
    tap_args = (k_taps, v_taps, q_taps)
    parts = local_part(heads, axis, q.shape[0], blocks, tails, tap_args)
    raw, rate, keys, queries, values, p, u, w, x, y, mt, bt, ct, state, back = parts
    if groups == 2:
        arriving = returning = lax.ppermute(
            state, axis, [(d, (d + heads) % count) for d in range(count)]
        )
    else:
        arriving, returning = jnp.zeros_like(state), jnp.zeros_like(back)
        exact = lax.Precision.HIGHEST
        for step in range(groups - 1):
            arriving = along(state, axis, heads)
            returning = along(back, axis, -heads)
            if step < groups - 2:
                state, back = arriving, returning
                for c in range(mt.shape[0]):
                    other = mt.shape[0] - 1 - c
                    state = jnp.dot(mt[c], state, precision=exact) + bt[c]
                    back = jnp.dot(mt[other].T, back, precision=exact) + ct[other]
    shared = (raw, *tails, rate, queries, keys, values, p, u, w, x, y, *tap_args)
    u, x, states, backs, kept, conv, rate_grad, taps, rim, mixed = state_part(
        heads, axis, shared, (mt, bt, ct, on_chip(arriving), on_chip(returning))
    )
    rim = along(rim, axis, -heads)
    args = (raw, rate, queries, keys, values, u, x, states, backs, kept, taps, *tap_args)
    more_conv, more_rate, taps = final_part(heads, axis, args)
    blocks = input_part(
        heads,
        axis,
        (conv, more_conv),
        on_chip(rim),
        (rate_grad, more_rate),
        tap_args,
        mixed,
    )
    taps, *blocks = lax.optimization_barrier((taps, *blocks))
    axes = ("dp", axis)
    rounds = sum_rounds(axes)
    if rounds is None:
        taps = lax.psum(taps, axes)
        moved = trade(blocks, axis, heads)
    else:
        moved = [trade_one(blocks[step], axis, heads, step) for step in range(heads - 1)]
        for masks in rounds[:2]:
            taps = sum_round(taps, axes, masks)
        late, taps = lax.optimization_barrier((blocks[-1], taps))
        moved.append(trade_one(late, axis, heads, heads - 1))
        taps, *moved[1:-1] = lax.optimization_barrier((taps, *moved[1:-1]))
        for masks in rounds[2:]:
            taps = sum_round(taps, axes, masks)
    blocks = [on_chip(b) for b in moved]
    mixed, d_q, d_k, d_v, d_decay, d_beta = unpack(heads, axis, q.shape[0], blocks)
    return (
        mixed[None],
        d_q[None],
        d_k[None],
        d_v[None],
        taps[0:4],
        taps[4:8],
        taps[8:12],
        d_decay.T[None],
        d_beta.T[None],
    )


def solution(mesh):
    split_spec, whole_spec = P("dp", "tm", None), P()
    in_specs = (split_spec,) * 3 + (whole_spec,) * 3 + (split_spec,) * 3
    out_specs = (split_spec,) * 4 + (whole_spec,) * 3 + (split_spec,) * 2
    return jax.shard_map(body, mesh=mesh, in_specs=in_specs, out_specs=out_specs, check_vma=False)
```

time: 109 us -> 70.3 us (0.64)
  Pallas kernels: 35.9 us -> 20.9 us
  starting transfers between devices: 38 us -> 24.9 us
  waiting for transfers between devices: 28.4 us -> 22.8 us
  local copies, waits for them, and re-layouts: 3.38 us -> 0.62 us
  other arithmetic: 1.32 us -> 0.03 us
    ppermute x18 -> x13, starting transfers between devices: 30.5 us -> 18 us  [the longest x6 9.94 us: trade_one(): return lax.ppermute(value, axis, pairs)]
    pallas_call x3 -> x2, Pallas kernels: 19.7 us -> 7.35 us  [the longest x1 3.93 us: final_part(): pl.pallas_call(functools.partial(final_kernel, heads, axis), out_shape=ou...]
    ppermute x18 -> x13, waiting for transfers between devices: 26 us -> 19.3 us  [the longest x6 13.3 us: trade_one(): return lax.ppermute(value, axis, pairs)]
    unnamed x52 -> x6, local copies, waits for them, and re-layouts: 3.38 us -> 0.01 us
    pallas_call x1, Pallas kernels: 2.78 us -> 0.58 us  [input_part(): pl.pallas_call(functools.partial(input_kernel, heads, axis), out_shape=ou...]
    pallas_call x1, Pallas kernels: 8.8 us -> 10.5 us  [local_part(): pl.pallas_call(functools.partial(local_kernel, heads, axis), out_shape=ou...]
    pallas_call x1, Pallas kernels: 2.37 us -> 1.03 us  [unpack(): pl.pallas_call(functools.partial(unpack_kernel, heads, axis), out_shape=o...]
    concatenate x1 -> x0, other arithmetic: 1.31 us -> none  [body(): rate_lines = jnp.concatenate([log_decay[0].T, write_strength[0].T], axis=0)]
  transfers between devices with their start and end apart: 24 -> 19, of which waited for: 11 -> 8; matrix products, arithmetic and copies ran while one was open for 0% -> 1% of each run, Pallas kernels for 13% -> 6%
where the time goes in v2:
time: 70.3 us; the launch traced here: 70.1 us
  starting transfers between devices  24.9 us (35%)
  waiting for transfers between devices  22.8 us (32%)
  Pallas kernels  20.9 us (30%)
  between operations  0.81 us (1%)
    ppermute x6, waiting for transfers between devices, trade_one(): return lax.ppermute(value, axis, pairs)  13.3 us
    pallas_call x1, Pallas kernels, local_part(): pl.pallas_call(functools.partial(local_kernel, heads, axis), out_shape=ou...  10.5 us
    ppermute x6, starting transfers between devices, trade_one(): return lax.ppermute(value, axis, pairs)  9.94 us
    ppermute x7, starting transfers between devices, swapped(): return lax.ppermute(value, axes, [(d, d ^ mask) for d in range(count)])  8.08 us
    ppermute x7, waiting for transfers between devices, swapped(): return lax.ppermute(value, axes, [(d, d ^ mask) for d in range(count)])  6.09 us
    pallas_call x1, Pallas kernels, final_part(): pl.pallas_call(functools.partial(final_kernel, heads, axis), out_shape=ou...  3.93 us
    pallas_call x1, Pallas kernels, state_part(): pl.pallas_call(functools.partial(state_kernel, heads, axis), out_shape=ou...  3.42 us
    ppermute x1, starting transfers between devices, body(): lax.ppermute(state, axis, [(d, (d + heads) % count) for d in range(count)])  2.75 us
  transfers between devices with their start and end apart: 19, of which 8 were waited for; matrix products, arithmetic and copies ran while one was open for 1% of the time, Pallas kernels for 6%

profile of v2, /device:TPU:0, one launch (start us, length us, event | category | flops | bytes accessed | tf_op | source)
XLA Modules:
  0.0 70.1 jit_solution(14983386812060045005)
XLA Ops:
  0.7 1.4 %pack.1 = (bf16[1040,128]{1,0:T(8,128)(2,1)S(1)}, bf16[1040,128]{1,0:T(8,128)(2,1)S(1)}, bf16[1040,128]{1,0:T(8,128)(2,1)S(1)}, bf16[1040,128]{1,0:T(8,128)(2,1)...) custom-call(bf16[256,512]{1,0:T(8,128)(2,1)} %bitcast.20, ...), custom_call_target="tpu_custom_call" | custom-call | flops 2000000000 | bytes 6000000 | tf_op jit(solution)/shard_map/pack/pallas_call | solution.py:126
  2.1 3.0 %collective-permute-start = (bf16[1040,128]{1,0:T(8,128)(2,1)S(1)}, bf16[1040,128]{1,0:T(8,128)(2,1)S(1)}, u32[]{:S(2)}, u32[]{:S(2)}) collective-permute-start(bf16[1040,128]{1,0:T(8,128)(2,1)S(1)} %get-tuple-element.65), channel_id=1, source_target_pairs={{0,1},{1,0},{2,3},{3,2},{4,5},{5,4},{6,7},{7,6},{8,9},{9,8},{10,11... | collective-permute-start | bytes 798728 | tf_op jit(solution)/shard_map/ppermute | solution.py:620
  5.1 1.6 %collective-permute-start.1 = (bf16[1040,128]{1,0:T(8,128)(2,1)S(1)}, bf16[1040,128]{1,0:T(8,128)(2,1)S(1)}, u32[]{:S(2)}, u32[]{:S(2)}) collective-permute-start(bf16[1040,128]{1,0:T(8,128)(2,1)S(1)} %get-tuple-element.66), channel_id=1, source_target_pairs={{0,2},{1,3},{2,0},{3,1},{4,6},{5,7},{6,4},{7,5},{8,10},{9,11},{10,... | collective-permute-start | bytes 798728 | tf_op jit(solution)/shard_map/ppermute | solution.py:620
  6.7 0.7 collective-permute-start.3
  7.3 0.7 collective-permute-start.4
  8.0 0.7 collective-permute-start.5
  8.7 0.7 collective-permute-start.6
  9.4 2.1 %collective-permute-done.refs_1_ = bf16[1040,128]{1,0:T(8,128)(2,1)S(1)} collective-permute-done((bf16[1040,128]{1,0:T(8,128)(2,1)S(1)}, bf16[1040,128]{1,0:T(8,128)(2,1)S(1)}, u32[]{:S(2)}, u32[]{:S(2)}) %collective-permute-start) | collective-permute-done | bytes 266272 | tf_op jit(solution)/shard_map/ppermute | solution.py:620
  11.5 2.9 %collective-permute-done.1.refs_2_ = bf16[1040,128]{1,0:T(8,128)(2,1)S(1)} collective-permute-done((bf16[1040,128]{1,0:T(8,128)(2,1)S(1)}, bf16[1040,128]{1,0:T(8,128)(2,1)S(1)}, u32[]{:S(2)}, u32[]{:S(2)}) %collective-permute-start.1) | collective-permute-done | bytes 266272 | tf_op jit(solution)/shard_map/ppermute | solution.py:620
  14.4 4.0 %collective-permute-done.2.refs_3_ = bf16[1040,128]{1,0:T(8,128)(2,1)S(1)} collective-permute-done((bf16[1040,128]{1,0:T(8,128)(2,1)S(1)}, bf16[1040,128]{1,0:T(8,128)(2,1)S(1)}, u32[]{:S(2)}, u32[]{:S(2)}) %collective-permute-start.2) | collective-permute-done | bytes 266272 | tf_op jit(solution)/shard_map/ppermute | solution.py:620
  18.5 10.5 %local_part.1 = (bf16[4,1024,128]{2,1,0:T(8,128)(2,1)S(1)}, f32[2,8,128]{2,1,0:T(8,128)S(1)}, f32[1024,128]{1,0:T(8,128)S(1)}, f32[1024,128]{1,0:T(8,128)S(1)}, ...) custom-call(bf16[1040,128]{1,0:T(8,128)(2,1)S(1)} %get-tuple-element, ...), custom_call_target="tpu_custom_call" | custom-call | flops 10000000000 | bytes 30000000 | tf_op jit(solution)/shard_map/local_part/pallas_call | solution.py:335
  29.0 2.8 %collective-permute-start.7 = (f32[128,128]{1,0:T(8,128)S(1)}, f32[128,128]{1,0:T(8,128)S(1)}, u32[]{:S(2)}, u32[]{:S(2)}) collective-permute-start(f32[128,128]{1,0:T(8,128)S(1)} %get-tuple-element.85), channel_id=1, source_target_pairs={{0,4},{1,5},{2,6},{3,7},{4,0},{5,1},{6,2},{7,3},{8,12},{9,13},{10,... | collective-permute-start | bytes 196616 | tf_op jit(solution)/shard_map/ppermute | solution.py:683
  31.7 2.4 %collective-permute-done.7.refs_20_.refs_21_ = f32[128,128]{1,0:T(8,128)S(1)} collective-permute-done((f32[128,128]{1,0:T(8,128)S(1)}, f32[128,128]{1,0:T(8,128)S(1)}, u32[]{:S(2)}, u32[]{:S(2)}) %collective-permute-start.7) | collective-permute-done | bytes 65568 | tf_op jit(solution)/shard_map/ppermute | solution.py:683
  34.1 3.4 %state_part.1 = (f32[1024,128]{1,0:T(8,128)S(1)}, f32[1024,128]{1,0:T(8,128)S(1)}, f32[9,128,128]{2,1,0:T(8,128)S(1)}, f32[9,128,128]{2,1,0:T(8,128)S(1)}, f32[8...) custom-call(bf16[4,1024,128]{2,1,0:T(8,128)(2,1)S(1)} %get-tuple-ele, ...), custom_call_target="tpu_custom_call" | custom-call | flops 7000000000 | bytes 21000000 | tf_op jit(solution)/shard_map/state_part/pallas_call | solution.py:483
  37.6 1.5 %collective-permute-start.8 = (f32[3,8,128]{2,1,0:T(8,128)S(1)}, f32[3,8,128]{2,1,0:T(8,128)S(1)}, u32[]{:S(2)}, u32[]{:S(2)}) collective-permute-start(f32[3,8,128]{2,1,0:T(8,128)S(1)} %get-tuple-element.95), channel_id=1, source_target_pairs={{4,0},{5,1},{6,2},{7,3},{12,8},{13,9},{14,10},{15,11},{20,16},{21,... | collective-permute-start | bytes 36872 | tf_op jit(solution)/shard_map/ppermute | solution.py:633
  39.1 3.9 %final_part.1 = (f32[3,896,128]{2,1,0:T(8,128)S(1)}, f32[2,7,128]{2,1,0:T(8,128)S(1)}, f32[16,512]{1,0:T(8,128)S(1)}) custom-call(bf16[4,1024,128]{2,1,0:T(8,128)(2,1)S(1)} %get-tuple-element.72.refs_0_, f32[2,8,128]{2,1,0:T(8,128)S(1)} %get-tuple-element.73.refs_5_.refs_1_, f32[1024,128]{1,0:T(8,128)S(1)} %get-tuple-element.74.refs_6_.refs_2_, ...), custom_call_target="tpu_custom_call" | custom-call | flops 8000000000 | bytes 24000000 | tf_op jit(solution)/shard_map/final_part/pallas_call | solution.py:536
  43.0 1.1 %collective-permute-done.8.refs_2_ = f32[3,8,128]{2,1,0:T(8,128)S(1)} collective-permute-done((f32[3,8,128]{2,1,0:T(8,128)S(1)}, f32[3,8,128]{2,1,0:T(8,128)S(1)}, u32[]{:S(2)}, u32[]{:S(2)}) %collective-permute-start.8) | collective-permute-done | bytes 12320 | tf_op jit(solution)/shard_map/ppermute | solution.py:633
  44.1 0.6 input_part.1
  44.7 0.1 collective-permute-start.9
  44.7 1.7 %collective-permute-start.13 = (bf16[1040,128]{1,0:T(8,128)(2,1)S(1)}, bf16[1040,128]{1,0:T(8,128)(2,1)S(1)}, u32[]{:S(2)}, u32[]{:S(2)}) collective-permute-start(bf16[1040,128]{1,0:T(8,128)(2,1)S(1)} %get-tuple-element.107), channel_id=1, source_target_pairs={{0,1},{1,0},{2,3},{3,2},{4,5},{5,4},{6,7},{7,6},{8,9},{9,8},{10,11... | collective-permute-start | bytes 798728 | tf_op jit(solution)/shard_map/ppermute | solution.py:620
  46.5 1.6 %collective-permute-start.14 = (bf16[1040,128]{1,0:T(8,128)(2,1)S(1)}, bf16[1040,128]{1,0:T(8,128)(2,1)S(1)}, u32[]{:S(2)}, u32[]{:S(2)}) collective-permute-start(bf16[1040,128]{1,0:T(8,128)(2,1)S(1)} %get-tuple-element.108), channel_id=1, source_target_pairs={{0,2},{1,3},{2,0},{3,1},{4,6},{5,7},{6,4},{7,5},{8,10},{9,11},{10,... | collective-permute-start | bytes 798728 | tf_op jit(solution)/shard_map/ppermute | solution.py:620
  48.0 1.6 %collective-permute-start.12 = (f32[16,512]{1,0:T(8,128)S(1)}, f32[16,512]{1,0:T(8,128)S(1)}, u32[]{:S(2)}, u32[]{:S(2)}) collective-permute-start(f32[16,512]{1,0:T(8,128)S(1)} %add.21), channel_id=1, source_target_pairs={{0,17},{1,16},{2,19},{3,18},{4,21},{5,20},{6,23},{7,22},{8,25},{9,... | collective-permute-start | bytes 98312 | tf_op jit(solution)/shard_map/ppermute | solution.py:652
  49.6 1.5 %collective-permute-start.11 = (f32[16,512]{1,0:T(8,128)S(1)}, f32[16,512]{1,0:T(8,128)S(1)}, u32[]{:S(2)}, u32[]{:S(2)}) collective-permute-start(f32[16,512]{1,0:T(8,128)S(1)} %add.21), channel_id=1, source_target_pairs={{0,1},{1,0},{2,3},{3,2},{4,5},{5,4},{6,7},{7,6},{8,9},{9,8},{10,11... | collective-permute-start | bytes 98312 | tf_op jit(solution)/shard_map/ppermute | solution.py:652
  51.1 0.5 collective-permute-start.10
  51.6 4.1 %collective-permute-done.12 = f32[16,512]{1,0:T(8,128)S(1)} collective-permute-done((f32[16,512]{1,0:T(8,128)S(1)}, f32[16,512]{1,0:T(8,128)S(1)}, u32[]{:S(2)}, u32[]{:S(2)}) %collective-permute-start.12) | collective-permute-done | bytes 32800 | tf_op jit(solution)/shard_map/ppermute | solution.py:652
  55.8 3.6 %collective-permute-start.18 = (f32[16,512]{1,0:T(8,128)S(1)}, f32[16,512]{1,0:T(8,128)S(1)}, u32[]{:S(2)}, u32[]{:S(2)}) collective-permute-start(f32[16,512]{1,0:T(8,128)S(1)} %add_add_fusion.1), channel_id=1, source_target_pairs={{0,6},{1,7},{2,4},{3,5},{4,2},{5,3},{6,0},{7,1},{8,14},{9,15},{10,... | collective-permute-start | bytes 98312 | tf_op jit(solution)/shard_map/ppermute | solution.py:652
  59.3 0.9 %collective-permute-start.16 = (f32[16,512]{1,0:T(8,128)S(1)}, f32[16,512]{1,0:T(8,128)S(1)}, u32[]{:S(2)}, u32[]{:S(2)}) collective-permute-start(f32[16,512]{1,0:T(8,128)S(1)} %add_add_fusion.1), channel_id=1, source_target_pairs={{0,2},{1,3},{2,0},{3,1},{4,6},{5,7},{6,4},{7,5},{8,10},{9,11},{10,... | collective-permute-start | bytes 98312 | tf_op jit(solution)/shard_map/ppermute | solution.py:652
  60.2 2.1 %collective-permute-start.15 = (bf16[1040,128]{1,0:T(8,128)(2,1)S(1)}, bf16[1040,128]{1,0:T(8,128)(2,1)S(1)}, u32[]{:S(2)}, u32[]{:S(2)}) collective-permute-start(bf16[1040,128]{1,0:T(8,128)(2,1)S(1)} %get-tuple-element.111), channel_id=1, source_target_pairs={{0,3},{1,2},{2,1},{3,0},{4,7},{5,6},{6,5},{7,4},{8,11},{9,10},{10,... | collective-permute-start | bytes 798728 | tf_op jit(solution)/shard_map/ppermute | solution.py:620
  62.3 2.0 %collective-permute-done.17 = f32[16,512]{1,0:T(8,128)S(1)} collective-permute-done((f32[16,512]{1,0:T(8,128)S(1)}, f32[16,512]{1,0:T(8,128)S(1)}, u32[]{:S(2)}, u32[]{:S(2)}) %collective-permute-start.17) | collective-permute-done | bytes 32800 | tf_op jit(solution)/shard_map/ppermute | solution.py:652
  64.3 0.6 fusion
  64.9 4.2 %collective-permute-done.15.refs_3_ = bf16[1040,128]{1,0:T(8,128)(2,1)S(1)} collective-permute-done((bf16[1040,128]{1,0:T(8,128)(2,1)S(1)}, bf16[1040,128]{1,0:T(8,128)(2,1)S(1)}, u32[]{:S(2)}, u32[]{:S(2)}) %collective-permute-start.15) | collective-permute-done | bytes 266272 | tf_op jit(solution)/shard_map/ppermute | solution.py:620
  69.0 1.0 %unpack.1 = (bf16[256,512]{1,0:T(8,128)(2,1)}, bf16[256,512]{1,0:T(8,128)(2,1)}, bf16[256,512]{1,0:T(8,128)(2,1)}, bf16[256,512]{1,0:T(8,128)(2,1)}, f32[4,256]{1,0:T(4,128)}, /*index=5*/f32[4,256]{1,0:T(4,128)}) custom-call(bf16[1040,128]{1,0:T(8,128)(2,1)S(1)} %get-tuple-element.103.refs_0_, bf16[1040,128]{1,0:T(8,128)(2,1)S(1)} %collective-permute-done.13.refs_1_, ...), custom_call_target="tpu_custom_call" | custom-call | flops 2000000000 | bytes 6000000 | tf_op jit(solution)/shard_map/unpack/pallas_call | solution.py:168
  (22 shorter events, 0.1 us)
Async XLA Ops:
  0.6 17.8 %copy-start = (f32[4,512]{1,0:T(4,128)S(1)}, f32[4,512]{1,0:T(4,128)}, u32[]{:S(2)}) copy-start(f32[4,512]{1,0:T(4,128)} %refs_5_.1) | copy-start | bytes 24580
  0.7 17.8 %copy-start.1 = (f32[4,512]{1,0:T(4,128)S(1)}, f32[4,512]{1,0:T(4,128)}, u32[]{:S(2)}) copy-start(f32[4,512]{1,0:T(4,128)} %refs_6_.1) | copy-start | bytes 24580
  0.7 17.8 %copy-start.2 = (f32[4,512]{1,0:T(4,128)S(1)}, f32[4,512]{1,0:T(4,128)}, u32[]{:S(2)}) copy-start(f32[4,512]{1,0:T(4,128)} %refs_7_.1) | copy-start | bytes 24580
  2.1 9.4 %collective-permute-start = (bf16[1040,128]{1,0:T(8,128)(2,1)S(1)}, bf16[1040,128]{1,0:T(8,128)(2,1)S(1)}, u32[]{:S(2)}, u32[]{:S(2)}) collective-permute-start(bf16[1040,128]{1,0:T(8,128)(2,1)S(1)} %get-tuple-element.65), channel_id=1, source_target_pairs={{0,1},{1,0},{2,3},{3,2},{4,5},{5,4},{6,7},{7,6},{8,9},{9,8},{10,11... | collective-permute-start | bytes 798728 | tf_op jit(solution)/shard_map/ppermute | solution.py:620
  5.1 9.3 %collective-permute-start.1 = (bf16[1040,128]{1,0:T(8,128)(2,1)S(1)}, bf16[1040,128]{1,0:T(8,128)(2,1)S(1)}, u32[]{:S(2)}, u32[]{:S(2)}) collective-permute-start(bf16[1040,128]{1,0:T(8,128)(2,1)S(1)} %get-tuple-element.66), channel_id=1, source_target_pairs={{0,2},{1,3},{2,0},{3,1},{4,6},{5,7},{6,4},{7,5},{8,10},{9,11},{10,... | collective-permute-start | bytes 798728 | tf_op jit(solution)/shard_map/ppermute | solution.py:620
  6.7 11.8 %collective-permute-start.2 = (bf16[1040,128]{1,0:T(8,128)(2,1)S(1)}, bf16[1040,128]{1,0:T(8,128)(2,1)S(1)}, u32[]{:S(2)}, u32[]{:S(2)}) collective-permute-start(bf16[1040,128]{1,0:T(8,128)(2,1)S(1)} %get-tuple-element.67), channel_id=1, source_target_pairs={{0,3},{1,2},{2,1},{3,0},{4,7},{5,6},{6,5},{7,4},{8,11},{9,10},{10,... | collective-permute-start | bytes 798728 | tf_op jit(solution)/shard_map/ppermute | solution.py:620
  6.7 1.3 %collective-permute-start.3 = (bf16[3,8,128]{2,1,0:T(8,128)(2,1)S(1)}, bf16[3,8,128]{2,1,0:T(8,128)(2,1)S(1)}, u32[]{:S(2)}, u32[]{:S(2)}) collective-permute-start(bf16[3,8,128]{2,1,0:T(8,128)(2,1)S(1)} %get-tuple-element.68), channel_id=1, source_target_pairs={{3,4},{11,12},{19,20},{27,28}} | collective-permute-start | bytes 18440 | tf_op jit(solution)/shard_map/ppermute | solution.py:673
  7.3 1.4 %collective-permute-start.4 = (bf16[3,8,128]{2,1,0:T(8,128)(2,1)S(1)}, bf16[3,8,128]{2,1,0:T(8,128)(2,1)S(1)}, u32[]{:S(2)}, u32[]{:S(2)}) collective-permute-start(bf16[3,8,128]{2,1,0:T(8,128)(2,1)S(1)} %get-tuple-element.69), channel_id=1, source_target_pairs={{3,5},{11,13},{19,21},{27,29}} | collective-permute-start | bytes 18440 | tf_op jit(solution)/shard_map/ppermute | solution.py:673
  8.0 1.4 %collective-permute-start.5 = (bf16[3,8,128]{2,1,0:T(8,128)(2,1)S(1)}, bf16[3,8,128]{2,1,0:T(8,128)(2,1)S(1)}, u32[]{:S(2)}, u32[]{:S(2)}) collective-permute-start(bf16[3,8,128]{2,1,0:T(8,128)(2,1)S(1)} %get-tuple-element.70), channel_id=1, source_target_pairs={{3,6},{11,14},{19,22},{27,30}} | collective-permute-start | bytes 18440 | tf_op jit(solution)/shard_map/ppermute | solution.py:673
  8.7 0.7 collective-permute-start.6
  29.0 5.2 %collective-permute-start.7 = (f32[128,128]{1,0:T(8,128)S(1)}, f32[128,128]{1,0:T(8,128)S(1)}, u32[]{:S(2)}, u32[]{:S(2)}) collective-permute-start(f32[128,128]{1,0:T(8,128)S(1)} %get-tuple-element.85), channel_id=1, source_target_pairs={{0,4},{1,5},{2,6},{3,7},{4,0},{5,1},{6,2},{7,3},{8,12},{9,13},{10,... | collective-permute-start | bytes 196616 | tf_op jit(solution)/shard_map/ppermute | solution.py:683
  37.6 6.5 %collective-permute-start.8 = (f32[3,8,128]{2,1,0:T(8,128)S(1)}, f32[3,8,128]{2,1,0:T(8,128)S(1)}, u32[]{:S(2)}, u32[]{:S(2)}) collective-permute-start(f32[3,8,128]{2,1,0:T(8,128)S(1)} %get-tuple-element.95), channel_id=1, source_target_pairs={{4,0},{5,1},{6,2},{7,3},{12,8},{13,9},{14,10},{15,11},{20,16},{21,... | collective-permute-start | bytes 36872 | tf_op jit(solution)/shard_map/ppermute | solution.py:633
  44.7 3.4 %collective-permute-start.9 = (f32[16,512]{1,0:T(8,128)S(1)}, f32[16,512]{1,0:T(8,128)S(1)}, u32[]{:S(2)}, u32[]{:S(2)}) collective-permute-start(f32[16,512]{1,0:T(8,128)S(1)} %get-tuple-element.105), channel_id=1, source_target_pairs={{0,8},{1,9},{2,10},{3,11},{4,12},{5,13},{6,14},{7,15},{8,0},{9,1},... | collective-permute-start | bytes 98312 | tf_op jit(solution)/shard_map/ppermute | solution.py:652
  44.7 11.0 %collective-permute-start.13 = (bf16[1040,128]{1,0:T(8,128)(2,1)S(1)}, bf16[1040,128]{1,0:T(8,128)(2,1)S(1)}, u32[]{:S(2)}, u32[]{:S(2)}) collective-permute-start(bf16[1040,128]{1,0:T(8,128)(2,1)S(1)} %get-tuple-element.107), channel_id=1, source_target_pairs={{0,1},{1,0},{2,3},{3,2},{4,5},{5,4},{6,7},{7,6},{8,9},{9,8},{10,11... | collective-permute-start | bytes 798728 | tf_op jit(solution)/shard_map/ppermute | solution.py:620
  46.5 9.3 %collective-permute-start.14 = (bf16[1040,128]{1,0:T(8,128)(2,1)S(1)}, bf16[1040,128]{1,0:T(8,128)(2,1)S(1)}, u32[]{:S(2)}, u32[]{:S(2)}) collective-permute-start(bf16[1040,128]{1,0:T(8,128)(2,1)S(1)} %get-tuple-element.108), channel_id=1, source_target_pairs={{0,2},{1,3},{2,0},{3,1},{4,6},{5,7},{6,4},{7,5},{8,10},{9,11},{10,... | collective-permute-start | bytes 798728 | tf_op jit(solution)/shard_map/ppermute | solution.py:620
  48.0 7.7 %collective-permute-start.12 = (f32[16,512]{1,0:T(8,128)S(1)}, f32[16,512]{1,0:T(8,128)S(1)}, u32[]{:S(2)}, u32[]{:S(2)}) collective-permute-start(f32[16,512]{1,0:T(8,128)S(1)} %add.21), channel_id=1, source_target_pairs={{0,17},{1,16},{2,19},{3,18},{4,21},{5,20},{6,23},{7,22},{8,25},{9,... | collective-permute-start | bytes 98312 | tf_op jit(solution)/shard_map/ppermute | solution.py:652
  49.6 6.1 %collective-permute-start.11 = (f32[16,512]{1,0:T(8,128)S(1)}, f32[16,512]{1,0:T(8,128)S(1)}, u32[]{:S(2)}, u32[]{:S(2)}) collective-permute-start(f32[16,512]{1,0:T(8,128)S(1)} %add.21), channel_id=1, source_target_pairs={{0,1},{1,0},{2,3},{3,2},{4,5},{5,4},{6,7},{7,6},{8,9},{9,8},{10,11... | collective-permute-start | bytes 98312 | tf_op jit(solution)/shard_map/ppermute | solution.py:652
  51.1 4.6 %collective-permute-start.10 = (f32[16,512]{1,0:T(8,128)S(1)}, f32[16,512]{1,0:T(8,128)S(1)}, u32[]{:S(2)}, u32[]{:S(2)}) collective-permute-start(f32[16,512]{1,0:T(8,128)S(1)} %add.21), channel_id=1, source_target_pairs={{0,16},{1,17},{2,18},{3,19},{4,20},{5,21},{6,22},{7,23},{8,24},{9,... | collective-permute-start | bytes 98312 | tf_op jit(solution)/shard_map/ppermute | solution.py:652
  55.8 6.5 %collective-permute-start.18 = (f32[16,512]{1,0:T(8,128)S(1)}, f32[16,512]{1,0:T(8,128)S(1)}, u32[]{:S(2)}, u32[]{:S(2)}) collective-permute-start(f32[16,512]{1,0:T(8,128)S(1)} %add_add_fusion.1), channel_id=1, source_target_pairs={{0,6},{1,7},{2,4},{3,5},{4,2},{5,3},{6,0},{7,1},{8,14},{9,15},{10,... | collective-permute-start | bytes 98312 | tf_op jit(solution)/shard_map/ppermute | solution.py:652
  59.3 4.9 %collective-permute-start.17 = (f32[16,512]{1,0:T(8,128)S(1)}, f32[16,512]{1,0:T(8,128)S(1)}, u32[]{:S(2)}, u32[]{:S(2)}) collective-permute-start(f32[16,512]{1,0:T(8,128)S(1)} %add_add_fusion.1), channel_id=1, source_target_pairs={{0,4},{1,5},{2,6},{3,7},{4,0},{5,1},{6,2},{7,3},{8,12},{9,13},{10,... | collective-permute-start | bytes 98312 | tf_op jit(solution)/shard_map/ppermute | solution.py:652
  59.3 4.9 %collective-permute-start.16 = (f32[16,512]{1,0:T(8,128)S(1)}, f32[16,512]{1,0:T(8,128)S(1)}, u32[]{:S(2)}, u32[]{:S(2)}) collective-permute-start(f32[16,512]{1,0:T(8,128)S(1)} %add_add_fusion.1), channel_id=1, source_target_pairs={{0,2},{1,3},{2,0},{3,1},{4,6},{5,7},{6,4},{7,5},{8,10},{9,11},{10,... | collective-permute-start | bytes 98312 | tf_op jit(solution)/shard_map/ppermute | solution.py:652
  60.2 8.8 %collective-permute-start.15 = (bf16[1040,128]{1,0:T(8,128)(2,1)S(1)}, bf16[1040,128]{1,0:T(8,128)(2,1)S(1)}, u32[]{:S(2)}, u32[]{:S(2)}) collective-permute-start(bf16[1040,128]{1,0:T(8,128)(2,1)S(1)} %get-tuple-element.111), channel_id=1, source_target_pairs={{0,3},{1,2},{2,1},{3,0},{4,7},{5,6},{6,5},{7,4},{8,11},{9,10},{10,... | collective-permute-start | bytes 798728 | tf_op jit(solution)/shard_map/ppermute | solution.py:620

commit v3 on v2

--- a/solution.py
+++ b/solution.py
@@ -406,12 +406,25 @@
     return made, decay_row, as_row(d_beta, rows, columns)
 
 
+def chunk_mixed(c, forms, given, before, state, back, later, ids):
+    g_column, beta_column = forms[0], forms[4]
+    queries, cotangent, p_value, w_value, y_value = given
+    rows, columns = ids
+    s_pair, d_pair = split(state), split(back)
+    u_value = before[0] - nn(split(w_value), s_pair)
+    x_value = before[1] + nn(split(y_value), d_pair)
+    mixed = jnp.exp(g_column) * nn(split(queries), s_pair) + nn(split(p_value), split(u_value))
+    d_g = jnp.sum(cotangent.astype(F32) * mixed, axis=1, keepdims=True)
+    kept = jnp.sum(later * back, axis=1, keepdims=True)
+    kept_row = jnp.sum(jnp.where(rows >= columns, d_g, 0.0) + kept, axis=0, keepdims=True)
+    return u_value, x_value, mixed.astype(BF16), kept_row
+
+
 def state_kernel(heads, axis, *refs):
     raw, tails, refs = refs[0], refs[1 : 1 + heads], refs[1 + heads :]
     (rate, q_in, k_in, v_in, p_in, u_in, w_in, x_in, y_in), refs = refs[:9], refs[9:]
     tap_refs, (mt_in, bt_in, ct_in, state_in, back_in), refs = refs[:3], refs[3:8], refs[8:]
-    u_out, x_out, states, backs, kept_out, conv_out, rate_grad, tap_out, rim_out = refs[:9]
-    mixed_all, padded = refs[9:]
+    states, backs, conv_out, rate_grad, tap_out, rim_out, mixed_out, padded = refs
     me, group = place_in_group(axis, heads)
     length, width = q_in.shape
     chunk_count = length // CHUNK
@@ -428,31 +441,19 @@
         states[c + 1] = state
         backs[other] = back
 
-    for c in range(chunk_count):
-        at = pl.ds(c * CHUNK, CHUNK)
-        s_pair, d_pair = split(states[c]), split(backs[c + 1])
-        g_column, g_row, g_last, beta_row, beta_column = chunk_forms(rate, c, rows, columns)
-        u_value = u_in[at, :] - nn(split(w_in[at, :]), s_pair)
-        x_value = x_in[at, :] + nn(split(y_in[at, :]), d_pair)
-        mixed = jnp.exp(g_column) * nn(split(q_in[at, :]), s_pair)
-        mixed = mixed + nn(split(p_in[at, :]), split(u_value))
-        u_out[at, :], x_out[at, :] = u_value, x_value
-        mixed_all[at, :] = mixed.astype(BF16)
-        d_g = jnp.sum(raw[3, at, :].astype(F32) * mixed, axis=1, keepdims=True)
-        kept = jnp.sum(states[c + 1] * backs[c + 1], axis=1, keepdims=True)
-        kept_out[c : c + 1, :] = jnp.sum(
-            jnp.where(rows >= columns, d_g, 0.0) + kept, axis=0, keepdims=True
-        )
-
     for place in range(3):
         padded[place, 0:8, :] = tail_of(tails, place)
         padded[place, 8:, :] = raw[place, 0:CHUNK, :].astype(F32)
     taps = [ref[:, aligned(me, width)] for ref in tap_refs]
     sums = [[jnp.zeros((8, width), F32) for _ in range(4)] for _ in range(3)]
     at = pl.ds(0, CHUNK)
-    given = (k_in[at, :], q_in[at, :], v_in[at, :], u_out[at, :], x_out[at, :])
-    given += (states[0], backs[1], raw[3, at, :], kept_out[0:1, :])
     forms = chunk_forms(rate, 0, rows, columns)
+    given = (q_in[at, :], raw[3, at, :], p_in[at, :], w_in[at, :], y_in[at, :])
+    u_value, x_value, mixed_out[...], kept_row = chunk_mixed(
+        0, forms, given, (u_in[at, :], x_in[at, :]), states[0], backs[1], states[1], (rows, columns)
+    )
+    given = (k_in[at, :], q_in[at, :], v_in[at, :], u_value, x_value)
+    given += (states[0], backs[1], raw[3, at, :], kept_row)
     made, decay_row, beta_row = chunk_back(0, forms, given, (rows, columns), padded, taps, sums)
     rate_grad[0], rate_grad[1] = decay_row, beta_row
     for place in range(3):
@@ -465,19 +466,15 @@
 def state_part(heads, axis, shared, more):
     length, width = shared[2 + heads].shape
     chunk_count = length // CHUNK
-    tall = pltpu.VMEM((length, width), F32)
     chain = pltpu.VMEM((chunk_count + 1, width, width), F32)
     out_shape = [
-        tall,
-        tall,
         chain,
         chain,
-        pltpu.VMEM((chunk_count, CHUNK), F32),
         pltpu.VMEM((3, CHUNK, width), F32),
         pltpu.VMEM((2, 1, CHUNK), F32),
         pltpu.VMEM((12, 8, width), F32),
         jax.ShapeDtypeStruct((3, 8, width), F32),
-        pltpu.VMEM((length, width), BF16),
+        pltpu.VMEM((CHUNK, width), BF16),
     ]
     args = [*shared, *more]
     return pl.pallas_call(
@@ -495,9 +492,8 @@
 
 
 def final_kernel(heads, axis, *refs):
-    raw, rate, q_in, k_in, v_in, u_in, x_in, states, backs, kept, tap_before = refs[:11]
-    tap_refs, refs = refs[11:14], refs[14:]
-    conv_out, rate_grad, tap_out, padded = refs
+    raw, rate, q_in, k_in, v_in, p_in, u_in, w_in, x_in, y_in, states, backs, tap_before = refs[:13]
+    tap_refs, (conv_out, rate_grad, tap_out, mixed_out, padded) = refs[13:16], refs[16:]
     me, _ = place_in_group(axis, heads)
     length, width = q_in.shape
     rows, columns = grid_ids()
@@ -507,9 +503,16 @@
     sums = [[tap_before[4 * place + offset] for offset in range(4)] for place in range(3)]
     for c in range(1, length // CHUNK):
         at = pl.ds(c * CHUNK, CHUNK)
-        given = (k_in[at, :], q_in[at, :], v_in[at, :], u_in[at, :], x_in[at, :])
-        given += (states[c], backs[c + 1], raw[3, at, :], kept[c : c + 1, :])
         forms = chunk_forms(rate, c, rows, columns)
+        around = states[c], backs[c + 1]
+        given = (q_in[at, :], raw[3, at, :], p_in[at, :], w_in[at, :], y_in[at, :])
+        before = u_in[at, :], x_in[at, :]
+        u_value, x_value, mixed, kept_row = chunk_mixed(
+            c, forms, given, before, *around, states[c + 1], (rows, columns)
+        )
+        mixed_out[(c - 1) * CHUNK : c * CHUNK, :] = mixed
+        given = (k_in[at, :], q_in[at, :], v_in[at, :], u_value, x_value, *around)
+        given += (raw[3, at, :], kept_row)
         made, decay_row, beta_row = chunk_back(
             c, forms, given, (rows, columns), padded, taps, sums
         )
@@ -532,12 +535,13 @@
         pltpu.VMEM((3, count * CHUNK, width), F32),
         pltpu.VMEM((2, count, CHUNK), F32),
         jax.ShapeDtypeStruct((16, heads * width), F32),
+        pltpu.VMEM((count * CHUNK, width), BF16),
     ]
     return pl.pallas_call(
         functools.partial(final_kernel, heads, axis),
         out_shape=out_shape,
         in_specs=[VMEM] * len(args),
-        out_specs=[VMEM] * 3,
+        out_specs=[VMEM] * 4,
         scratch_shapes=[pltpu.VMEM((3, length + 8, width), F32)],
         compiler_params=params(),
         cost_estimate=cost(8),
@@ -547,7 +551,7 @@
 
 def input_kernel(heads, axis, *refs):
     conv_first, conv_rest, rim, rate_first, rate_rest = refs[:5]
-    tap_refs, mixed, refs = refs[5:8], refs[8], refs[9:]
+    tap_refs, mixed_first, mixed_rest, refs = refs[5:8], refs[8], refs[9], refs[10:]
     blocks, refs = refs[:heads], refs[heads:]
     extended, result, rate_grad, lines = refs
     me, _ = place_in_group(axis, heads)
@@ -558,6 +562,8 @@
     rate_grad[:, 0 : early // CHUNK, :] = rate_first[...]
     rate_grad[:, early // CHUNK :, :] = rate_rest[...]
     taps = [ref[:, aligned(me, width)] for ref in tap_refs]
+    result[3, 0:early, :] = mixed_first[...]
+    result[3, early:, :] = mixed_rest[...]
     for place in range(3):
         extended[place, 0:early, :] = conv_first[place]
         extended[place, early:length, :] = conv_rest[place]
@@ -572,11 +578,9 @@
     lines[...] = jnp.zeros_like(lines)
     for step in range(heads):
         target = peer(me, heads, step)
-        blocks[step][0:frames, :] = mixed[aligned(target, frames), :]
-        for place in range(3):
-            blocks[step][(1 + place) * frames : (2 + place) * frames, :] = result[
-                place, aligned(target, frames), :
-            ]
+        for place in range(4):
+            at = (place + 1) % 4 * frames
+            blocks[step][at : at + frames, :] = result[place, aligned(target, frames), :]
         for kind in range(2):
             for c in range(per):
                 line = rate_grad[kind, pl.ds(target * per + c, 1), :]
@@ -590,7 +594,7 @@
     length, width = convs[0].shape[1] + convs[1].shape[1], convs[0].shape[2]
     frames = length // heads
     out_shape = [jax.ShapeDtypeStruct((4 * frames + line_rows(frames), width), BF16)] * heads
-    args = [*convs, rim, *rate_grads, *tap_args, mixed]
+    args = [*convs, rim, *rate_grads, *tap_args, *mixed]
     return pl.pallas_call(
         functools.partial(input_kernel, heads, axis),
         out_shape=out_shape,
@@ -598,7 +602,7 @@
         out_specs=[VMEM] * heads,
         scratch_shapes=[
             pltpu.VMEM((3, length + 8, width), F32),
-            pltpu.VMEM((3, length, width), BF16),
+            pltpu.VMEM((4, length, width), BF16),
             pltpu.VMEM((2, length // CHUNK, CHUNK), F32),
             pltpu.VMEM((line_rows(frames), CHUNK), F32),
         ],
@@ -639,14 +643,14 @@
     outer, inner = (lax.axis_size(axis) for axis in axes)
     if outer & (outer - 1) or inner & (inner - 1):
         return None
-    bits = [inner << place for place in range(outer.bit_length() - 1)]
-    bits += [1 << place for place in range(inner.bit_length() - 1)]
-    rounds = [bits[:1]] if len(bits) % 2 else []
-    return rounds + [bits[at : at + 2] for at in range(len(bits) % 2, len(bits), 2)]
+    high = [inner << place for place in range(outer.bit_length() - 1)]
+    low = [1 << place for place in range(inner.bit_length() - 1)]
+    bits = high[:1] + low[:1] + high[1:] + low[1:]
+    return [[bit] for bit in bits[:-2]] + [bits[-2:]]
 
 
 def sum_round(value, axes, masks):
-    count = lax.axis_size(axes)
+    count = lax.axis_size(axes[0]) * lax.axis_size(axes[1])
 
     def swapped(mask):
         return lax.ppermute(value, axes, [(d, d ^ mask) for d in range(count)])
@@ -696,12 +700,16 @@
                     state = jnp.dot(mt[c], state, precision=exact) + bt[c]
                     back = jnp.dot(mt[other].T, back, precision=exact) + ct[other]
     shared = (raw, *tails, rate, queries, keys, values, p, u, w, x, y, *tap_args)
-    u, x, states, backs, kept, conv, rate_grad, taps, rim, mixed = state_part(
+    states, backs, conv, rate_grad, taps, rim, mixed = state_part(
         heads, axis, shared, (mt, bt, ct, on_chip(arriving), on_chip(returning))
     )
     rim = along(rim, axis, -heads)
-    args = (raw, rate, queries, keys, values, u, x, states, backs, kept, taps, *tap_args)
-    more_conv, more_rate, taps = final_part(heads, axis, args)
+    args = (raw, rate, queries, keys, values, p, u, w, x, y, states, backs, taps, *tap_args)
+    more_conv, more_rate, taps, more_mixed = final_part(heads, axis, args)
+    axes = ("dp", axis)
+    rounds = sum_rounds(axes)
+    if rounds:
+        taps = sum_round(taps, axes, rounds[0])
     blocks = input_part(
         heads,
         axis,
@@ -709,23 +717,19 @@
         on_chip(rim),
         (rate_grad, more_rate),
         tap_args,
-        mixed,
+        (mixed, more_mixed),
     )
     taps, *blocks = lax.optimization_barrier((taps, *blocks))
-    axes = ("dp", axis)
-    rounds = sum_rounds(axes)
-    if rounds is None:
+    if rounds:
+        taps = sum_round(taps, axes, rounds[1])
+    moved = trade(blocks, axis, heads)
+    if rounds:
+        for masks in rounds[2:-1]:
+            taps = sum_round(taps, axes, masks)
+        taps, *moved[1:-1] = lax.optimization_barrier((taps, *moved[1:-1]))
+        taps = sum_round(taps, axes, rounds[-1])
+    else:
         taps = lax.psum(taps, axes)
-        moved = trade(blocks, axis, heads)
-    else:
-        moved = [trade_one(blocks[step], axis, heads, step) for step in range(heads - 1)]
-        for masks in rounds[:2]:
-            taps = sum_round(taps, axes, masks)
-        late, taps = lax.optimization_barrier((blocks[-1], taps))
-        moved.append(trade_one(late, axis, heads, heads - 1))
-        taps, *moved[1:-1] = lax.optimization_barrier((taps, *moved[1:-1]))
-        for masks in rounds[2:]:
-            taps = sum_round(taps, axes, masks)
     blocks = [on_chip(b) for b in moved]
     mixed, d_q, d_k, d_v, d_decay, d_beta = unpack(heads, axis, q.shape[0], blocks)
     return (

time: 70.3 us -> 68 us (0.967)
  starting transfers between devices: 24.9 us -> 23.9 us
  waiting for transfers between devices: 22.8 us -> 22 us
    ppermute x7 -> x6, waiting for transfers between devices: 6.09 us -> 10.4 us  [swapped(): return lax.ppermute(value, axes, [(d, d ^ mask) for d in range(count)])]
    ppermute x6, waiting for transfers between devices: 13.3 us -> 9.08 us  [trade_one(): return lax.ppermute(value, axis, pairs)]
    ppermute x6, starting transfers between devices: 9.94 us -> 8.06 us  [trade_one(): return lax.ppermute(value, axis, pairs)]
    pallas_call x1, Pallas kernels: 3.42 us -> 2.04 us  [state_part(): pl.pallas_call(functools.partial(state_kernel, heads, axis), out_shape=ou...]
    ppermute x1, waiting for transfers between devices: 1.07 us -> 0.08 us  [along(): lax.ppermute(value, axis, [(d, d + steps) for d in range(count) if 0 <= d...]
    pallas_call x1, Pallas kernels: 3.93 us -> 4.84 us  [final_part(): pl.pallas_call(functools.partial(final_kernel, heads, axis), out_shape=ou...]
    ppermute x7 -> x6, starting transfers between devices: 8.08 us -> 8.96 us  [swapped(): return lax.ppermute(value, axes, [(d, d ^ mask) for d in range(count)])]
  transfers between devices with their start and end apart: 19 -> 18, of which waited for: 8 -> 10; matrix products, arithmetic and copies ran while one was open for 1% -> 0% of each run, Pallas kernels for 6% -> 10%
where the time goes in v3:
time: 68 us; the launch traced here: 67.8 us
  starting transfers between devices  23.9 us (35%)
  waiting for transfers between devices  22 us (32%)
  Pallas kernels  20.4 us (30%)
  between operations  0.8 us (1%)
    pallas_call x1, Pallas kernels, local_part(): pl.pallas_call(functools.partial(local_kernel, heads, axis), out_shape=ou...  10.5 us
    ppermute x6, waiting for transfers between devices, swapped(): return lax.ppermute(value, axes, [(d, d ^ mask) for d in range(count)])  10.4 us
    ppermute x6, waiting for transfers between devices, trade_one(): return lax.ppermute(value, axis, pairs)  9.08 us
    ppermute x6, starting transfers between devices, swapped(): return lax.ppermute(value, axes, [(d, d ^ mask) for d in range(count)])  8.96 us
    ppermute x6, starting transfers between devices, trade_one(): return lax.ppermute(value, axis, pairs)  8.06 us
    pallas_call x1, Pallas kernels, final_part(): pl.pallas_call(functools.partial(final_kernel, heads, axis), out_shape=ou...  4.84 us
    ppermute x1, starting transfers between devices, body(): lax.ppermute(state, axis, [(d, (d + heads) % count) for d in range(count)])  2.75 us
    ppermute x4, starting transfers between devices, body(): lax.ppermute(tails[head], axis, [(g * heads - 1, g * heads + head) for g...  2.63 us
  transfers between devices with their start and end apart: 18, of which 10 were waited for; matrix products, arithmetic and copies ran while one was open for 0% of the time, Pallas kernels for 10%

profile of v3, /device:TPU:0, one launch (start us, length us, event | category | flops | bytes accessed | tf_op | source)
XLA Modules:
  0.0 67.8 jit_solution(1667935861781971841)
XLA Ops:
  0.7 1.4 %pack.1 = (bf16[1040,128]{1,0:T(8,128)(2,1)S(1)}, bf16[1040,128]{1,0:T(8,128)(2,1)S(1)}, bf16[1040,128]{1,0:T(8,128)(2,1)S(1)}, bf16[1040,128]{1,0:T(8,128)(2,1)...) custom-call(bf16[256,512]{1,0:T(8,128)(2,1)} %bitcast.20, ...), custom_call_target="tpu_custom_call" | custom-call | flops 2000000000 | bytes 6000000 | tf_op jit(solution)/shard_map/pack/pallas_call | solution.py:126
  2.1 3.0 %collective-permute-start = (bf16[1040,128]{1,0:T(8,128)(2,1)S(1)}, bf16[1040,128]{1,0:T(8,128)(2,1)S(1)}, u32[]{:S(2)}, u32[]{:S(2)}) collective-permute-start(bf16[1040,128]{1,0:T(8,128)(2,1)S(1)} %get-tuple-element.61), channel_id=1, source_target_pairs={{0,1},{1,0},{2,3},{3,2},{4,5},{5,4},{6,7},{7,6},{8,9},{9,8},{10,11... | collective-permute-start | bytes 798728 | tf_op jit(solution)/shard_map/ppermute | solution.py:624
  5.1 1.6 %collective-permute-start.1 = (bf16[1040,128]{1,0:T(8,128)(2,1)S(1)}, bf16[1040,128]{1,0:T(8,128)(2,1)S(1)}, u32[]{:S(2)}, u32[]{:S(2)}) collective-permute-start(bf16[1040,128]{1,0:T(8,128)(2,1)S(1)} %get-tuple-element.62), channel_id=1, source_target_pairs={{0,2},{1,3},{2,0},{3,1},{4,6},{5,7},{6,4},{7,5},{8,10},{9,11},{10,... | collective-permute-start | bytes 798728 | tf_op jit(solution)/shard_map/ppermute | solution.py:624
  6.7 0.7 collective-permute-start.3
  7.3 0.7 collective-permute-start.4
  8.0 0.7 collective-permute-start.5
  8.7 0.7 collective-permute-start.6
  9.4 2.1 %collective-permute-done.refs_1_ = bf16[1040,128]{1,0:T(8,128)(2,1)S(1)} collective-permute-done((bf16[1040,128]{1,0:T(8,128)(2,1)S(1)}, bf16[1040,128]{1,0:T(8,128)(2,1)S(1)}, u32[]{:S(2)}, u32[]{:S(2)}) %collective-permute-start) | collective-permute-done | bytes 266272 | tf_op jit(solution)/shard_map/ppermute | solution.py:624
  11.5 2.9 %collective-permute-done.1.refs_2_ = bf16[1040,128]{1,0:T(8,128)(2,1)S(1)} collective-permute-done((bf16[1040,128]{1,0:T(8,128)(2,1)S(1)}, bf16[1040,128]{1,0:T(8,128)(2,1)S(1)}, u32[]{:S(2)}, u32[]{:S(2)}) %collective-permute-start.1) | collective-permute-done | bytes 266272 | tf_op jit(solution)/shard_map/ppermute | solution.py:624
  14.4 4.0 %collective-permute-done.2.refs_3_ = bf16[1040,128]{1,0:T(8,128)(2,1)S(1)} collective-permute-done((bf16[1040,128]{1,0:T(8,128)(2,1)S(1)}, bf16[1040,128]{1,0:T(8,128)(2,1)S(1)}, u32[]{:S(2)}, u32[]{:S(2)}) %collective-permute-start.2) | collective-permute-done | bytes 266272 | tf_op jit(solution)/shard_map/ppermute | solution.py:624
  18.5 10.5 %local_part.1 = (bf16[4,1024,128]{2,1,0:T(8,128)(2,1)S(1)}, f32[2,8,128]{2,1,0:T(8,128)S(1)}, f32[1024,128]{1,0:T(8,128)S(1)}, f32[1024,128]{1,0:T(8,128)S(1)}, ...) custom-call(bf16[1040,128]{1,0:T(8,128)(2,1)S(1)} %get-tuple-element, ...), custom_call_target="tpu_custom_call" | custom-call | flops 10000000000 | bytes 30000000 | tf_op jit(solution)/shard_map/local_part/pallas_call | solution.py:335
  29.0 2.8 %collective-permute-start.7 = (f32[128,128]{1,0:T(8,128)S(1)}, f32[128,128]{1,0:T(8,128)S(1)}, u32[]{:S(2)}, u32[]{:S(2)}) collective-permute-start(f32[128,128]{1,0:T(8,128)S(1)} %get-tuple-element.81), channel_id=1, source_target_pairs={{0,4},{1,5},{2,6},{3,7},{4,0},{5,1},{6,2},{7,3},{8,12},{9,13},{10,... | collective-permute-start | bytes 196616 | tf_op jit(solution)/shard_map/ppermute | solution.py:687
  31.7 2.4 %collective-permute-done.7.refs_20_.refs_21_ = f32[128,128]{1,0:T(8,128)S(1)} collective-permute-done((f32[128,128]{1,0:T(8,128)S(1)}, f32[128,128]{1,0:T(8,128)S(1)}, u32[]{:S(2)}, u32[]{:S(2)}) %collective-permute-start.7) | collective-permute-done | bytes 65568 | tf_op jit(solution)/shard_map/ppermute | solution.py:687
  34.1 2.0 %state_part.1 = (f32[9,128,128]{2,1,0:T(8,128)S(1)}, f32[9,128,128]{2,1,0:T(8,128)S(1)}, f32[3,128,128]{2,1,0:T(8,128)S(1)}, f32[2,1,128]{2,1,0:T(1,128)S(1)}, f...) custom-call(bf16[4,1024,128]{2,1,0:T(8,128)(2,1)S(1)} %get-tuple-element.68.refs_0_, ...), custom_call_target="tpu_custom_call" | custom-call | flops 7000000000 | bytes 21000000 | tf_op jit(solution)/shard_map/state_part/pallas_call | solution.py:480
  36.2 1.5 %collective-permute-start.9 = (f32[3,8,128]{2,1,0:T(8,128)S(1)}, f32[3,8,128]{2,1,0:T(8,128)S(1)}, u32[]{:S(2)}, u32[]{:S(2)}) collective-permute-start(f32[3,8,128]{2,1,0:T(8,128)S(1)} %get-tuple-element.88), channel_id=1, source_target_pairs={{4,0},{5,1},{6,2},{7,3},{12,8},{13,9},{14,10},{15,11},{20,16},{21,... | collective-permute-start | bytes 36872 | tf_op jit(solution)/shard_map/ppermute | solution.py:637
  37.7 4.8 %final_part.1 = (f32[3,896,128]{2,1,0:T(8,128)S(1)}, f32[2,7,128]{2,1,0:T(8,128)S(1)}, f32[16,512]{1,0:T(8,128)S(1)}, bf16[896,128]{1,0:T(8,128)(2,1)S(1)}) custom-call(bf16[4,1024,128]{2,1,0:T(8,128)(2,1)S(1)} %get-tuple-element.68.refs_0_, f32[2,8,128]{2,1,0:T(8,128)S(1)} %get-tuple-element.69.refs_5_.refs_1_, ...), custom_call_target="tpu_custom_call" | custom-call | flops 8000000000 | bytes 24000000 | tf_op jit(solution)/shard_map/final_part/pallas_call | solution.py:540
  42.6 0.1 collective-permute-done.9.refs_2_
  42.7 0.6 input_part.1
  43.2 0.5 collective-permute-done.8
  43.8 1.7 %collective-permute-start.12 = (bf16[1040,128]{1,0:T(8,128)(2,1)S(1)}, bf16[1040,128]{1,0:T(8,128)(2,1)S(1)}, u32[]{:S(2)}, u32[]{:S(2)}) collective-permute-start(bf16[1040,128]{1,0:T(8,128)(2,1)S(1)} %get-tuple-element.99), channel_id=1, source_target_pairs={{0,1},{1,0},{2,3},{3,2},{4,5},{5,4},{6,7},{7,6},{8,9},{9,8},{10,11... | collective-permute-start | bytes 798728 | tf_op jit(solution)/shard_map/ppermute | solution.py:624
  45.5 1.6 %collective-permute-start.13 = (bf16[1040,128]{1,0:T(8,128)(2,1)S(1)}, bf16[1040,128]{1,0:T(8,128)(2,1)S(1)}, u32[]{:S(2)}, u32[]{:S(2)}) collective-permute-start(bf16[1040,128]{1,0:T(8,128)(2,1)S(1)} %get-tuple-element.100), channel_id=1, source_target_pairs={{0,2},{1,3},{2,0},{3,1},{4,6},{5,7},{6,4},{7,5},{8,10},{9,11},{10,... | collective-permute-start | bytes 798728 | tf_op jit(solution)/shard_map/ppermute | solution.py:624
  47.0 0.2 collective-permute-start.14
  47.3 1.7 %collective-permute-start.10 = (f32[16,512]{1,0:T(8,128)S(1)}, f32[16,512]{1,0:T(8,128)S(1)}, u32[]{:S(2)}, u32[]{:S(2)}) collective-permute-start(f32[16,512]{1,0:T(8,128)S(1)} %add.18), channel_id=1, source_target_pairs={{0,1},{1,0},{2,3},{3,2},{4,5},{5,4},{6,7},{7,6},{8,9},{9,8},{10,11... | collective-permute-start | bytes 98312 | tf_op jit(solution)/shard_map/ppermute | solution.py:656
  49.0 4.6 %collective-permute-done.10 = f32[16,512]{1,0:T(8,128)S(1)} collective-permute-done((f32[16,512]{1,0:T(8,128)S(1)}, f32[16,512]{1,0:T(8,128)S(1)}, u32[]{:S(2)}, u32[]{:S(2)}) %collective-permute-start.10) | collective-permute-done | bytes 32800 | tf_op jit(solution)/shard_map/ppermute | solution.py:656
  53.5 1.7 %collective-permute-start.11 = (f32[16,512]{1,0:T(8,128)S(1)}, f32[16,512]{1,0:T(8,128)S(1)}, u32[]{:S(2)}, u32[]{:S(2)}) collective-permute-start(f32[16,512]{1,0:T(8,128)S(1)} %add.19), channel_id=1, source_target_pairs={{0,16},{1,17},{2,18},{3,19},{4,20},{5,21},{6,22},{7,23},{8,24},{9,... | collective-permute-start | bytes 98312 | tf_op jit(solution)/shard_map/ppermute | solution.py:656
  55.3 2.2 %collective-permute-done.11 = f32[16,512]{1,0:T(8,128)S(1)} collective-permute-done((f32[16,512]{1,0:T(8,128)S(1)}, f32[16,512]{1,0:T(8,128)S(1)}, u32[]{:S(2)}, u32[]{:S(2)}) %collective-permute-start.11) | collective-permute-done | bytes 32800 | tf_op jit(solution)/shard_map/ppermute | solution.py:656
  57.5 4.8 %collective-permute-start.17 = (f32[16,512]{1,0:T(8,128)S(1)}, f32[16,512]{1,0:T(8,128)S(1)}, u32[]{:S(2)}, u32[]{:S(2)}) collective-permute-start(f32[16,512]{1,0:T(8,128)S(1)} %add.20), channel_id=1, source_target_pairs={{0,6},{1,7},{2,4},{3,5},{4,2},{5,3},{6,0},{7,1},{8,14},{9,15},{10,... | collective-permute-start | bytes 98312 | tf_op jit(solution)/shard_map/ppermute | solution.py:656
  62.3 0.6 collective-permute-start.15
  63.0 1.0 %unpack.1 = (bf16[256,512]{1,0:T(8,128)(2,1)}, bf16[256,512]{1,0:T(8,128)(2,1)}, bf16[256,512]{1,0:T(8,128)(2,1)}, bf16[256,512]{1,0:T(8,128)(2,1)}, f32[4,256]{1,0:T(4,128)}, /*index=5*/f32[4,256]{1,0:T(4,128)}) custom-call(bf16[1040,128]{1,0:T(8,128)(2,1)S(1)} %get-tuple-element.97.refs_0_, bf16[1040,128]{1,0:T(8,128)(2,1)S(1)} %collective-permute-done.12.refs_1_, ...), custom_call_target="tpu_custom_call" | custom-call | flops 2000000000 | bytes 6000000 | tf_op jit(solution)/shard_map/unpack/pallas_call | solution.py:168
  64.0 0.2 collective-permute-done.17
  64.2 2.9 %collective-permute-done.16 = f32[16,512]{1,0:T(8,128)S(1)} collective-permute-done((f32[16,512]{1,0:T(8,128)S(1)}, f32[16,512]{1,0:T(8,128)S(1)}, u32[]{:S(2)}, u32[]{:S(2)}) %collective-permute-start.16) | collective-permute-done | bytes 32800 | tf_op jit(solution)/shard_map/ppermute | solution.py:656
  67.1 0.6 fusion
  (21 shorter events, 0.1 us)
Async XLA Ops:
  0.6 17.8 %copy-start = (f32[4,512]{1,0:T(4,128)S(1)}, f32[4,512]{1,0:T(4,128)}, u32[]{:S(2)}) copy-start(f32[4,512]{1,0:T(4,128)} %refs_5_.1) | copy-start | bytes 24580
  0.7 17.8 %copy-start.1 = (f32[4,512]{1,0:T(4,128)S(1)}, f32[4,512]{1,0:T(4,128)}, u32[]{:S(2)}) copy-start(f32[4,512]{1,0:T(4,128)} %refs_6_.1) | copy-start | bytes 24580
  0.7 17.8 %copy-start.2 = (f32[4,512]{1,0:T(4,128)S(1)}, f32[4,512]{1,0:T(4,128)}, u32[]{:S(2)}) copy-start(f32[4,512]{1,0:T(4,128)} %refs_7_.1) | copy-start | bytes 24580
  2.1 9.4 %collective-permute-start = (bf16[1040,128]{1,0:T(8,128)(2,1)S(1)}, bf16[1040,128]{1,0:T(8,128)(2,1)S(1)}, u32[]{:S(2)}, u32[]{:S(2)}) collective-permute-start(bf16[1040,128]{1,0:T(8,128)(2,1)S(1)} %get-tuple-element.61), channel_id=1, source_target_pairs={{0,1},{1,0},{2,3},{3,2},{4,5},{5,4},{6,7},{7,6},{8,9},{9,8},{10,11... | collective-permute-start | bytes 798728 | tf_op jit(solution)/shard_map/ppermute | solution.py:624
  5.1 9.3 %collective-permute-start.1 = (bf16[1040,128]{1,0:T(8,128)(2,1)S(1)}, bf16[1040,128]{1,0:T(8,128)(2,1)S(1)}, u32[]{:S(2)}, u32[]{:S(2)}) collective-permute-start(bf16[1040,128]{1,0:T(8,128)(2,1)S(1)} %get-tuple-element.62), channel_id=1, source_target_pairs={{0,2},{1,3},{2,0},{3,1},{4,6},{5,7},{6,4},{7,5},{8,10},{9,11},{10,... | collective-permute-start | bytes 798728 | tf_op jit(solution)/shard_map/ppermute | solution.py:624
  6.7 11.8 %collective-permute-start.2 = (bf16[1040,128]{1,0:T(8,128)(2,1)S(1)}, bf16[1040,128]{1,0:T(8,128)(2,1)S(1)}, u32[]{:S(2)}, u32[]{:S(2)}) collective-permute-start(bf16[1040,128]{1,0:T(8,128)(2,1)S(1)} %get-tuple-element.63), channel_id=1, source_target_pairs={{0,3},{1,2},{2,1},{3,0},{4,7},{5,6},{6,5},{7,4},{8,11},{9,10},{10,... | collective-permute-start | bytes 798728 | tf_op jit(solution)/shard_map/ppermute | solution.py:624
  6.7 1.3 %collective-permute-start.3 = (bf16[3,8,128]{2,1,0:T(8,128)(2,1)S(1)}, bf16[3,8,128]{2,1,0:T(8,128)(2,1)S(1)}, u32[]{:S(2)}, u32[]{:S(2)}) collective-permute-start(bf16[3,8,128]{2,1,0:T(8,128)(2,1)S(1)} %get-tuple-element.64), channel_id=1, source_target_pairs={{3,4},{11,12},{19,20},{27,28}} | collective-permute-start | bytes 18440 | tf_op jit(solution)/shard_map/ppermute | solution.py:677
  7.3 1.4 %collective-permute-start.4 = (bf16[3,8,128]{2,1,0:T(8,128)(2,1)S(1)}, bf16[3,8,128]{2,1,0:T(8,128)(2,1)S(1)}, u32[]{:S(2)}, u32[]{:S(2)}) collective-permute-start(bf16[3,8,128]{2,1,0:T(8,128)(2,1)S(1)} %get-tuple-element.65), channel_id=1, source_target_pairs={{3,5},{11,13},{19,21},{27,29}} | collective-permute-start | bytes 18440 | tf_op jit(solution)/shard_map/ppermute | solution.py:677
  8.0 1.4 %collective-permute-start.5 = (bf16[3,8,128]{2,1,0:T(8,128)(2,1)S(1)}, bf16[3,8,128]{2,1,0:T(8,128)(2,1)S(1)}, u32[]{:S(2)}, u32[]{:S(2)}) collective-permute-start(bf16[3,8,128]{2,1,0:T(8,128)(2,1)S(1)} %get-tuple-element.66), channel_id=1, source_target_pairs={{3,6},{11,14},{19,22},{27,30}} | collective-permute-start | bytes 18440 | tf_op jit(solution)/shard_map/ppermute | solution.py:677
  8.7 0.7 %collective-permute-start.6 = (bf16[3,8,128]{2,1,0:T(8,128)(2,1)S(1)}, bf16[3,8,128]{2,1,0:T(8,128)(2,1)S(1)}, u32[]{:S(2)}, u32[]{:S(2)}) collective-permute-start(bf16[3,8,128]{2,1,0:T(8,128)(2,1)S(1)} %get-tuple-element.67), channel_id=1, source_target_pairs={{3,7},{11,15},{19,23},{27,31}} | collective-permute-start | bytes 18440 | tf_op jit(solution)/shard_map/ppermute | solution.py:677
  29.0 5.2 %collective-permute-start.7 = (f32[128,128]{1,0:T(8,128)S(1)}, f32[128,128]{1,0:T(8,128)S(1)}, u32[]{:S(2)}, u32[]{:S(2)}) collective-permute-start(f32[128,128]{1,0:T(8,128)S(1)} %get-tuple-element.81), channel_id=1, source_target_pairs={{0,4},{1,5},{2,6},{3,7},{4,0},{5,1},{6,2},{7,3},{8,12},{9,13},{10,... | collective-permute-start | bytes 196616 | tf_op jit(solution)/shard_map/ppermute | solution.py:687
  36.2 6.5 %collective-permute-start.9 = (f32[3,8,128]{2,1,0:T(8,128)S(1)}, f32[3,8,128]{2,1,0:T(8,128)S(1)}, u32[]{:S(2)}, u32[]{:S(2)}) collective-permute-start(f32[3,8,128]{2,1,0:T(8,128)S(1)} %get-tuple-element.88), channel_id=1, source_target_pairs={{4,0},{5,1},{6,2},{7,3},{12,8},{13,9},{14,10},{15,11},{20,16},{21,... | collective-permute-start | bytes 36872 | tf_op jit(solution)/shard_map/ppermute | solution.py:637
  42.5 1.3 %collective-permute-start.8 = (f32[16,512]{1,0:T(8,128)S(1)}, f32[16,512]{1,0:T(8,128)S(1)}, u32[]{:S(2)}, u32[]{:S(2)}) collective-permute-start(f32[16,512]{1,0:T(8,128)S(1)} %get-tuple-element.85), channel_id=1, source_target_pairs={{0,8},{1,9},{2,10},{3,11},{4,12},{5,13},{6,14},{7,15},{8,0},{9,1},... | collective-permute-start | bytes 98312 | tf_op jit(solution)/shard_map/ppermute | solution.py:656
  43.8 13.7 %collective-permute-start.12 = (bf16[1040,128]{1,0:T(8,128)(2,1)S(1)}, bf16[1040,128]{1,0:T(8,128)(2,1)S(1)}, u32[]{:S(2)}, u32[]{:S(2)}) collective-permute-start(bf16[1040,128]{1,0:T(8,128)(2,1)S(1)} %get-tuple-element.99), channel_id=1, source_target_pairs={{0,1},{1,0},{2,3},{3,2},{4,5},{5,4},{6,7},{7,6},{8,9},{9,8},{10,11... | collective-permute-start | bytes 798728 | tf_op jit(solution)/shard_map/ppermute | solution.py:624
  45.5 12.0 %collective-permute-start.13 = (bf16[1040,128]{1,0:T(8,128)(2,1)S(1)}, bf16[1040,128]{1,0:T(8,128)(2,1)S(1)}, u32[]{:S(2)}, u32[]{:S(2)}) collective-permute-start(bf16[1040,128]{1,0:T(8,128)(2,1)S(1)} %get-tuple-element.100), channel_id=1, source_target_pairs={{0,2},{1,3},{2,0},{3,1},{4,6},{5,7},{6,4},{7,5},{8,10},{9,11},{10,... | collective-permute-start | bytes 798728 | tf_op jit(solution)/shard_map/ppermute | solution.py:624
  47.0 15.9 %collective-permute-start.14 = (bf16[1040,128]{1,0:T(8,128)(2,1)S(1)}, bf16[1040,128]{1,0:T(8,128)(2,1)S(1)}, u32[]{:S(2)}, u32[]{:S(2)}) collective-permute-start(bf16[1040,128]{1,0:T(8,128)(2,1)S(1)} %get-tuple-element.103), channel_id=1, source_target_pairs={{0,3},{1,2},{2,1},{3,0},{4,7},{5,6},{6,5},{7,4},{8,11},{9,10},{10,... | collective-permute-start | bytes 798728 | tf_op jit(solution)/shard_map/ppermute | solution.py:624
  47.3 6.2 %collective-permute-start.10 = (f32[16,512]{1,0:T(8,128)S(1)}, f32[16,512]{1,0:T(8,128)S(1)}, u32[]{:S(2)}, u32[]{:S(2)}) collective-permute-start(f32[16,512]{1,0:T(8,128)S(1)} %add.18), channel_id=1, source_target_pairs={{0,1},{1,0},{2,3},{3,2},{4,5},{5,4},{6,7},{7,6},{8,9},{9,8},{10,11... | collective-permute-start | bytes 98312 | tf_op jit(solution)/shard_map/ppermute | solution.py:656
  53.5 3.9 %collective-permute-start.11 = (f32[16,512]{1,0:T(8,128)S(1)}, f32[16,512]{1,0:T(8,128)S(1)}, u32[]{:S(2)}, u32[]{:S(2)}) collective-permute-start(f32[16,512]{1,0:T(8,128)S(1)} %add.19), channel_id=1, source_target_pairs={{0,16},{1,17},{2,18},{3,19},{4,20},{5,21},{6,22},{7,23},{8,24},{9,... | collective-permute-start | bytes 98312 | tf_op jit(solution)/shard_map/ppermute | solution.py:656
  57.5 6.7 %collective-permute-start.17 = (f32[16,512]{1,0:T(8,128)S(1)}, f32[16,512]{1,0:T(8,128)S(1)}, u32[]{:S(2)}, u32[]{:S(2)}) collective-permute-start(f32[16,512]{1,0:T(8,128)S(1)} %add.20), channel_id=1, source_target_pairs={{0,6},{1,7},{2,4},{3,5},{4,2},{5,3},{6,0},{7,1},{8,14},{9,15},{10,... | collective-permute-start | bytes 98312 | tf_op jit(solution)/shard_map/ppermute | solution.py:656
  62.3 4.8 %collective-permute-start.16 = (f32[16,512]{1,0:T(8,128)S(1)}, f32[16,512]{1,0:T(8,128)S(1)}, u32[]{:S(2)}, u32[]{:S(2)}) collective-permute-start(f32[16,512]{1,0:T(8,128)S(1)} %add.20), channel_id=1, source_target_pairs={{0,4},{1,5},{2,6},{3,7},{4,0},{5,1},{6,2},{7,3},{8,12},{9,13},{10,... | collective-permute-start | bytes 98312 | tf_op jit(solution)/shard_map/ppermute | solution.py:656
  62.3 4.8 %collective-permute-start.15 = (f32[16,512]{1,0:T(8,128)S(1)}, f32[16,512]{1,0:T(8,128)S(1)}, u32[]{:S(2)}, u32[]{:S(2)}) collective-permute-start(f32[16,512]{1,0:T(8,128)S(1)} %add.20), channel_id=1, source_target_pairs={{0,2},{1,3},{2,0},{3,1},{4,6},{5,7},{6,4},{7,5},{8,10},{9,11},{10,... | collective-permute-start | bytes 98312 | tf_op jit(solution)/shard_map/ppermute | solution.py:656

commit v4 on v3

--- a/solution.py
+++ b/solution.py
@@ -46,6 +46,22 @@
 
 def columns_of(*pairs):
     return tuple(jnp.concatenate(parts, axis=1) for parts in zip(*pairs))
+
+
+def side_by_side(chunk, indices, count):
+    indices = list(indices)
+    for at in range(0, len(indices), count):
+        running = [chunk(c) for c in indices[at : at + count]]
+        while running:
+            running = [one for one in running if next(one, None) is not None]
+
+
+def whole(steps):
+    while True:
+        try:
+            next(steps)
+        except StopIteration as ended:
+            return ended.value
 
 
 def grid_ids():
@@ -271,7 +287,7 @@
             t_value = inverse[at, :]
             inverse[at, :] = t_value - nn(split(t_value), split(halfway[c]))
 
-    for c in range(chunk_count):
+    def chunk(c):
         at = pl.ds(c * CHUNK, CHUNK)
         g_column, g_row, g_last, beta_row, beta_column = chunk_forms(rate_out, c, rows, columns)
         ratio, ratio_t = ratio_forms(g_column, g_row, rows, columns)
@@ -280,16 +296,19 @@
         values = activated(convolve(padded, 1, c * CHUNK, taps[1]), False)
         queries = activated(convolve(padded, 2, c * CHUNK, taps[2]), True)
         q_out[at, :], v_out[at, :] = queries, values
+        yield True
         keys = k_out[at, :]
         q_pair, k_pair = split(queries), split(keys)
         p_out[at, :] = ratio * nt(q_pair, k_pair)
         pt = ratio_t * nt(k_pair, q_pair)
+        yield True
         t_value = inverse[at, :]
         u_w = nn(
             split(t_value),
             columns_of(split(beta_column * values), split(beta_column * start_column * keys)),
         )
         u_value, w_value = u_w[:, :width], u_w[:, width:]
+        yield True
         cotangent = raw[3, at, :]
         p_high, p_low = split(pt)
         first = jnp.dot(
@@ -297,25 +316,32 @@
             jnp.concatenate([cotangent, cotangent], axis=0),
             preferred_element_type=F32,
         )
+        yield True
         x_y = nn(split(t_value.T), columns_of(split(first), split(tail_column * keys)))
         x_value, y_value = x_y[:, :width], x_y[:, width:]
+        yield True
         keys_t, queries_t = keys.T, queries.T
         b_m = nn(split(keys_t * tail_row), columns_of(split(u_value), split(w_value)))
         whole = jnp.exp(g_last)
         bt_out[c] = b_m[:, :width]
         mt_out[c] = whole * eye - b_m[:, width:]
+        yield True
         ct_out[c] = nn(
             columns_of(split(queries_t * start_row), split(keys_t * (-beta_row * start_row))),
             rows_of((cotangent, jnp.zeros_like(cotangent)), split(x_value)),
         )
         u_out[at, :], w_out[at, :], x_out[at, :], y_out[at, :] = u_value, w_value, x_value, y_value
 
-    state = bt_out[0]
-    back = ct_out[chunk_count - 1]
-    for c in range(1, chunk_count):
-        other = chunk_count - 1 - c
-        state = nn(split(mt_out[c]), split(state)) + bt_out[c]
-        back = nn(split(mt_out[other].T), split(back)) + ct_out[other]
+    side_by_side(chunk, range(chunk_count), 4)
+    spans = [(mt_out[c], bt_out[c], ct_out[c]) for c in range(chunk_count)]
+    while len(spans) > 1:
+        joined = []
+        for early, late in zip(spans[0::2], spans[1::2]):
+            ahead = nn(split(late[0]), columns_of(split(early[0]), split(early[1])))
+            behind = nn(split(early[0].T), split(late[2]))
+            joined.append((ahead[:, :width], ahead[:, width:] + late[1], behind + early[2]))
+        spans = joined + spans[len(spans) - len(spans) % 2 :]
+    _, state, back = spans[0]
     if lax.axis_size(axis) == 2 * heads:
         state_out[...] = jnp.where(group == 0, state, back)
     else:
@@ -371,17 +397,20 @@
     u_ox = nt(u_pair, ox_pair)
     ox_s = nt(ox_pair, s_pair)
     u_d = nt(u_pair, d_pair)
+    yield True
     strict = jnp.where(columns < rows, beta_column * ratio, 0.0)
     strict_t = jnp.where(columns > rows, beta_row * ratio_t, 0.0)
     e_value = ratio * ox_u[:CHUNK]
     f_value = strict * ox_u[CHUNK:] + strict_t * u_ox[:, CHUNK:]
     e_t = ratio_t * u_ox[:, :CHUNK]
+    yield True
     d_queries = start_column * ox_s[:CHUNK] + nn(split(e_value), k_pair)
     d_keys = (
         tail_column * u_d
         - (beta_column * start_column) * ox_s[CHUNK:]
         + nn(columns_of(split(e_t), split(-f_value)), rows_of(q_pair, k_pair))
     )
+    yield True
     d_values = beta_column * x_value
     d_beta = jnp.sum(x_value * u_value, axis=1, keepdims=True) / beta_column
     d_g = jnp.sum(d_values * values, axis=1, keepdims=True)
@@ -400,6 +429,7 @@
             grad = scale * (grad - unit * jnp.sum(unit * grad, axis=1, keepdims=True))
         grad = grad * (gate * (1.0 + c_value * (1.0 - gate)))
         made.append(grad)
+        yield True
         for offset in range(4):
             part = (grad * shifted[offset]).reshape(CHUNK // 8, 8, width)
             sums[place][offset] = sums[place][offset] + jnp.sum(part, axis=0)
@@ -413,6 +443,7 @@
     s_pair, d_pair = split(state), split(back)
     u_value = before[0] - nn(split(w_value), s_pair)
     x_value = before[1] + nn(split(y_value), d_pair)
+    yield True
     mixed = jnp.exp(g_column) * nn(split(queries), s_pair) + nn(split(p_value), split(u_value))
     d_g = jnp.sum(cotangent.astype(F32) * mixed, axis=1, keepdims=True)
     kept = jnp.sum(later * back, axis=1, keepdims=True)
@@ -449,12 +480,16 @@
     at = pl.ds(0, CHUNK)
     forms = chunk_forms(rate, 0, rows, columns)
     given = (q_in[at, :], raw[3, at, :], p_in[at, :], w_in[at, :], y_in[at, :])
-    u_value, x_value, mixed_out[...], kept_row = chunk_mixed(
-        0, forms, given, (u_in[at, :], x_in[at, :]), states[0], backs[1], states[1], (rows, columns)
+    u_value, x_value, mixed_out[...], kept_row = whole(
+        chunk_mixed(
+            0, forms, given, (u_in[at, :], x_in[at, :]), states[0], backs[1], states[1], (rows, columns)
+        )
     )
     given = (k_in[at, :], q_in[at, :], v_in[at, :], u_value, x_value)
     given += (states[0], backs[1], raw[3, at, :], kept_row)
-    made, decay_row, beta_row = chunk_back(0, forms, given, (rows, columns), padded, taps, sums)
+    made, decay_row, beta_row = whole(
+        chunk_back(0, forms, given, (rows, columns), padded, taps, sums)
+    )
     rate_grad[0], rate_grad[1] = decay_row, beta_row
     for place in range(3):
         conv_out[place] = made[place]
@@ -501,25 +536,27 @@
         padded[place, CHUNK - 8 :, :] = raw[place, CHUNK - 16 :, :].astype(F32)
     taps = [ref[:, aligned(me, width)] for ref in tap_refs]
     sums = [[tap_before[4 * place + offset] for offset in range(4)] for place in range(3)]
-    for c in range(1, length // CHUNK):
+    def chunk(c):
         at = pl.ds(c * CHUNK, CHUNK)
         forms = chunk_forms(rate, c, rows, columns)
         around = states[c], backs[c + 1]
         given = (q_in[at, :], raw[3, at, :], p_in[at, :], w_in[at, :], y_in[at, :])
         before = u_in[at, :], x_in[at, :]
-        u_value, x_value, mixed, kept_row = chunk_mixed(
+        u_value, x_value, mixed, kept_row = yield from chunk_mixed(
             c, forms, given, before, *around, states[c + 1], (rows, columns)
         )
         mixed_out[(c - 1) * CHUNK : c * CHUNK, :] = mixed
         given = (k_in[at, :], q_in[at, :], v_in[at, :], u_value, x_value, *around)
         given += (raw[3, at, :], kept_row)
-        made, decay_row, beta_row = chunk_back(
+        made, decay_row, beta_row = yield from chunk_back(
             c, forms, given, (rows, columns), padded, taps, sums
         )
         rate_grad[0, c - 1 : c, :] = decay_row
         rate_grad[1, c - 1 : c, :] = beta_row
         for place in range(3):
             conv_out[place, (c - 1) * CHUNK : c * CHUNK, :] = made[place]
+
+    side_by_side(chunk, range(1, length // CHUNK), 2)
     tap_out[...] = jnp.zeros_like(tap_out)
     for place, row in ((0, 4), (1, 8), (2, 0)):
         for offset in range(4):

time: 68 us -> 65.1 us (0.957)
  Pallas kernels: 20.4 us -> 17.5 us
    pallas_call x1, Pallas kernels: 10.5 us -> 7.8 us  [local_part(): pl.pallas_call(functools.partial(local_kernel, heads, axis), out_shape=ou...]
where the time goes in v4:
time: 65.1 us; the launch traced here: 64.9 us
  starting transfers between devices  23.9 us (37%)
  waiting for transfers between devices  22 us (34%)
  Pallas kernels  17.5 us (27%)
  between operations  0.8 us (1%)
    ppermute x6, waiting for transfers between devices, swapped(): return lax.ppermute(value, axes, [(d, d ^ mask) for d in range(count)])  10.2 us
    ppermute x6, waiting for transfers between devices, trade_one(): return lax.ppermute(value, axis, pairs)  9.08 us
    ppermute x6, starting transfers between devices, swapped(): return lax.ppermute(value, axes, [(d, d ^ mask) for d in range(count)])  8.94 us
    ppermute x6, starting transfers between devices, trade_one(): return lax.ppermute(value, axis, pairs)  8.06 us
    pallas_call x1, Pallas kernels, local_part(): pl.pallas_call(functools.partial(local_kernel, heads, axis), out_shape=ou...  7.8 us
    pallas_call x1, Pallas kernels, final_part(): pl.pallas_call(functools.partial(final_kernel, heads, axis), out_shape=ou...  4.63 us
    ppermute x1, starting transfers between devices, body(): lax.ppermute(state, axis, [(d, (d + heads) % count) for d in range(count)])  2.76 us
    ppermute x4, starting transfers between devices, body(): lax.ppermute(tails[head], axis, [(g * heads - 1, g * heads + head) for g...  2.63 us
  transfers between devices with their start and end apart: 18, of which 10 were waited for; matrix products, arithmetic and copies ran while one was open for 0% of the time, Pallas kernels for 10%

profile of v4, /device:TPU:0, one launch (start us, length us, event | category | flops | bytes accessed | tf_op | source)
XLA Modules:
  0.0 64.9 jit_solution(10182680496411404244)
XLA Ops:
  0.7 1.4 %pack.1 = (bf16[1040,128]{1,0:T(8,128)(2,1)S(1)}, bf16[1040,128]{1,0:T(8,128)(2,1)S(1)}, bf16[1040,128]{1,0:T(8,128)(2,1)S(1)}, bf16[1040,128]{1,0:T(8,128)(2,1)...) custom-call(bf16[256,512]{1,0:T(8,128)(2,1)} %bitcast.20, ...), custom_call_target="tpu_custom_call" | custom-call | flops 2000000000 | bytes 6000000 | tf_op jit(solution)/shard_map/pack/pallas_call | solution.py:142
  2.1 3.0 %collective-permute-start = (bf16[1040,128]{1,0:T(8,128)(2,1)S(1)}, bf16[1040,128]{1,0:T(8,128)(2,1)S(1)}, u32[]{:S(2)}, u32[]{:S(2)}) collective-permute-start(bf16[1040,128]{1,0:T(8,128)(2,1)S(1)} %get-tuple-element.61), channel_id=1, source_target_pairs={{0,1},{1,0},{2,3},{3,2},{4,5},{5,4},{6,7},{7,6},{8,9},{9,8},{10,11... | collective-permute-start | bytes 798728 | tf_op jit(solution)/shard_map/ppermute | solution.py:661
  5.1 1.6 %collective-permute-start.1 = (bf16[1040,128]{1,0:T(8,128)(2,1)S(1)}, bf16[1040,128]{1,0:T(8,128)(2,1)S(1)}, u32[]{:S(2)}, u32[]{:S(2)}) collective-permute-start(bf16[1040,128]{1,0:T(8,128)(2,1)S(1)} %get-tuple-element.62), channel_id=1, source_target_pairs={{0,2},{1,3},{2,0},{3,1},{4,6},{5,7},{6,4},{7,5},{8,10},{9,11},{10,... | collective-permute-start | bytes 798728 | tf_op jit(solution)/shard_map/ppermute | solution.py:661
  6.7 0.7 %collective-permute-start.3 = (bf16[3,8,128]{2,1,0:T(8,128)(2,1)S(1)}, bf16[3,8,128]{2,1,0:T(8,128)(2,1)S(1)}, u32[]{:S(2)}, u32[]{:S(2)}) collective-permute-start(bf16[3,8,128]{2,1,0:T(8,128)(2,1)S(1)} %get-tuple-element.64), channel_id=1, source_target_pairs={{3,4},{11,12},{19,20},{27,28}} | collective-permute-start | bytes 18440 | tf_op jit(solution)/shard_map/ppermute | solution.py:714
  7.3 0.7 %collective-permute-start.4 = (bf16[3,8,128]{2,1,0:T(8,128)(2,1)S(1)}, bf16[3,8,128]{2,1,0:T(8,128)(2,1)S(1)}, u32[]{:S(2)}, u32[]{:S(2)}) collective-permute-start(bf16[3,8,128]{2,1,0:T(8,128)(2,1)S(1)} %get-tuple-element.65), channel_id=1, source_target_pairs={{3,5},{11,13},{19,21},{27,29}} | collective-permute-start | bytes 18440 | tf_op jit(solution)/shard_map/ppermute | solution.py:714
  8.0 0.7 %collective-permute-start.5 = (bf16[3,8,128]{2,1,0:T(8,128)(2,1)S(1)}, bf16[3,8,128]{2,1,0:T(8,128)(2,1)S(1)}, u32[]{:S(2)}, u32[]{:S(2)}) collective-permute-start(bf16[3,8,128]{2,1,0:T(8,128)(2,1)S(1)} %get-tuple-element.66), channel_id=1, source_target_pairs={{3,6},{11,14},{19,22},{27,30}} | collective-permute-start | bytes 18440 | tf_op jit(solution)/shard_map/ppermute | solution.py:714
  8.7 0.7 %collective-permute-start.6 = (bf16[3,8,128]{2,1,0:T(8,128)(2,1)S(1)}, bf16[3,8,128]{2,1,0:T(8,128)(2,1)S(1)}, u32[]{:S(2)}, u32[]{:S(2)}) collective-permute-start(bf16[3,8,128]{2,1,0:T(8,128)(2,1)S(1)} %get-tuple-element.67), channel_id=1, source_target_pairs={{3,7},{11,15},{19,23},{27,31}} | collective-permute-start | bytes 18440 | tf_op jit(solution)/shard_map/ppermute | solution.py:714
  9.4 2.1 %collective-permute-done.refs_1_ = bf16[1040,128]{1,0:T(8,128)(2,1)S(1)} collective-permute-done((bf16[1040,128]{1,0:T(8,128)(2,1)S(1)}, bf16[1040,128]{1,0:T(8,128)(2,1)S(1)}, u32[]{:S(2)}, u32[]{:S(2)}) %collective-permute-start) | collective-permute-done | bytes 266272 | tf_op jit(solution)/shard_map/ppermute | solution.py:661
  11.5 2.9 %collective-permute-done.1.refs_2_ = bf16[1040,128]{1,0:T(8,128)(2,1)S(1)} collective-permute-done((bf16[1040,128]{1,0:T(8,128)(2,1)S(1)}, bf16[1040,128]{1,0:T(8,128)(2,1)S(1)}, u32[]{:S(2)}, u32[]{:S(2)}) %collective-permute-start.1) | collective-permute-done | bytes 266272 | tf_op jit(solution)/shard_map/ppermute | solution.py:661
  14.4 4.0 %collective-permute-done.2.refs_3_ = bf16[1040,128]{1,0:T(8,128)(2,1)S(1)} collective-permute-done((bf16[1040,128]{1,0:T(8,128)(2,1)S(1)}, bf16[1040,128]{1,0:T(8,128)(2,1)S(1)}, u32[]{:S(2)}, u32[]{:S(2)}) %collective-permute-start.2) | collective-permute-done | bytes 266272 | tf_op jit(solution)/shard_map/ppermute | solution.py:661
  18.5 7.8 %local_part.1 = (bf16[4,1024,128]{2,1,0:T(8,128)(2,1)S(1)}, f32[2,8,128]{2,1,0:T(8,128)S(1)}, f32[1024,128]{1,0:T(8,128)S(1)}, f32[1024,128]{1,0:T(8,128)S(1)}, ...) custom-call(bf16[1040,128]{1,0:T(8,128)(2,1)S(1)} %get-tuple-element, ...), custom_call_target="tpu_custom_call" | custom-call | flops 10000000000 | bytes 30000000 | tf_op jit(solution)/shard_map/local_part/pallas_call | solution.py:361
  26.3 2.8 %collective-permute-start.7 = (f32[128,128]{1,0:T(8,128)S(1)}, f32[128,128]{1,0:T(8,128)S(1)}, u32[]{:S(2)}, u32[]{:S(2)}) collective-permute-start(f32[128,128]{1,0:T(8,128)S(1)} %get-tuple-element.81), channel_id=1, source_target_pairs={{0,4},{1,5},{2,6},{3,7},{4,0},{5,1},{6,2},{7,3},{8,12},{9,13},{10,... | collective-permute-start | bytes 196616 | tf_op jit(solution)/shard_map/ppermute | solution.py:724
  29.0 2.4 %collective-permute-done.7.refs_20_.refs_21_ = f32[128,128]{1,0:T(8,128)S(1)} collective-permute-done((f32[128,128]{1,0:T(8,128)S(1)}, f32[128,128]{1,0:T(8,128)S(1)}, u32[]{:S(2)}, u32[]{:S(2)}) %collective-permute-start.7) | collective-permute-done | bytes 65568 | tf_op jit(solution)/shard_map/ppermute | solution.py:724
  31.4 2.0 %state_part.1 = (f32[9,128,128]{2,1,0:T(8,128)S(1)}, f32[9,128,128]{2,1,0:T(8,128)S(1)}, f32[3,128,128]{2,1,0:T(8,128)S(1)}, f32[2,1,128]{2,1,0:T(1,128)S(1)}, f...) custom-call(bf16[4,1024,128]{2,1,0:T(8,128)(2,1)S(1)} %get-tuple-element.68.refs_0_, ...), custom_call_target="tpu_custom_call" | custom-call | flops 7000000000 | bytes 21000000 | tf_op jit(solution)/shard_map/state_part/pallas_call | solution.py:515
  33.5 1.5 %collective-permute-start.9 = (f32[3,8,128]{2,1,0:T(8,128)S(1)}, f32[3,8,128]{2,1,0:T(8,128)S(1)}, u32[]{:S(2)}, u32[]{:S(2)}) collective-permute-start(f32[3,8,128]{2,1,0:T(8,128)S(1)} %get-tuple-element.88), channel_id=1, source_target_pairs={{4,0},{5,1},{6,2},{7,3},{12,8},{13,9},{14,10},{15,11},{20,16},{21,... | collective-permute-start | bytes 36872 | tf_op jit(solution)/shard_map/ppermute | solution.py:674
  35.0 4.6 %final_part.1 = (f32[3,896,128]{2,1,0:T(8,128)S(1)}, f32[2,7,128]{2,1,0:T(8,128)S(1)}, f32[16,512]{1,0:T(8,128)S(1)}, bf16[896,128]{1,0:T(8,128)(2,1)S(1)}) custom-call(bf16[4,1024,128]{2,1,0:T(8,128)(2,1)S(1)} %get-tuple-element.68.refs_0_, f32[2,8,128]{2,1,0:T(8,128)S(1)} %get-tuple-element.69.refs_5_.refs_1_, ...), custom_call_target="tpu_custom_call" | custom-call | flops 8000000000 | bytes 24000000 | tf_op jit(solution)/shard_map/final_part/pallas_call | solution.py:577
  39.7 0.3 collective-permute-done.9.refs_2_
  40.0 0.6 input_part.1
  40.6 0.3 collective-permute-done.8
  40.9 1.7 %collective-permute-start.12 = (bf16[1040,128]{1,0:T(8,128)(2,1)S(1)}, bf16[1040,128]{1,0:T(8,128)(2,1)S(1)}, u32[]{:S(2)}, u32[]{:S(2)}) collective-permute-start(bf16[1040,128]{1,0:T(8,128)(2,1)S(1)} %get-tuple-element.99), channel_id=1, source_target_pairs={{0,1},{1,0},{2,3},{3,2},{4,5},{5,4},{6,7},{7,6},{8,9},{9,8},{10,11... | collective-permute-start | bytes 798728 | tf_op jit(solution)/shard_map/ppermute | solution.py:661
  42.5 1.6 %collective-permute-start.13 = (bf16[1040,128]{1,0:T(8,128)(2,1)S(1)}, bf16[1040,128]{1,0:T(8,128)(2,1)S(1)}, u32[]{:S(2)}, u32[]{:S(2)}) collective-permute-start(bf16[1040,128]{1,0:T(8,128)(2,1)S(1)} %get-tuple-element.100), channel_id=1, source_target_pairs={{0,2},{1,3},{2,0},{3,1},{4,6},{5,7},{6,4},{7,5},{8,10},{9,11},{10,... | collective-permute-start | bytes 798728 | tf_op jit(solution)/shard_map/ppermute | solution.py:661
  44.1 0.2 collective-permute-start.14
  44.4 1.7 %collective-permute-start.10 = (f32[16,512]{1,0:T(8,128)S(1)}, f32[16,512]{1,0:T(8,128)S(1)}, u32[]{:S(2)}, u32[]{:S(2)}) collective-permute-start(f32[16,512]{1,0:T(8,128)S(1)} %add.18), channel_id=1, source_target_pairs={{0,1},{1,0},{2,3},{3,2},{4,5},{5,4},{6,7},{7,6},{8,9},{9,8},{10,11... | collective-permute-start | bytes 98312 | tf_op jit(solution)/shard_map/ppermute | solution.py:693
  46.0 4.6 %collective-permute-done.10 = f32[16,512]{1,0:T(8,128)S(1)} collective-permute-done((f32[16,512]{1,0:T(8,128)S(1)}, f32[16,512]{1,0:T(8,128)S(1)}, u32[]{:S(2)}, u32[]{:S(2)}) %collective-permute-start.10) | collective-permute-done | bytes 32800 | tf_op jit(solution)/shard_map/ppermute | solution.py:693
  50.6 1.7 %collective-permute-start.11 = (f32[16,512]{1,0:T(8,128)S(1)}, f32[16,512]{1,0:T(8,128)S(1)}, u32[]{:S(2)}, u32[]{:S(2)}) collective-permute-start(f32[16,512]{1,0:T(8,128)S(1)} %add.19), channel_id=1, source_target_pairs={{0,16},{1,17},{2,18},{3,19},{4,20},{5,21},{6,22},{7,23},{8,24},{9,... | collective-permute-start | bytes 98312 | tf_op jit(solution)/shard_map/ppermute | solution.py:693
  52.4 2.2 %collective-permute-done.11 = f32[16,512]{1,0:T(8,128)S(1)} collective-permute-done((f32[16,512]{1,0:T(8,128)S(1)}, f32[16,512]{1,0:T(8,128)S(1)}, u32[]{:S(2)}, u32[]{:S(2)}) %collective-permute-start.11) | collective-permute-done | bytes 32800 | tf_op jit(solution)/shard_map/ppermute | solution.py:693
  54.6 4.8 %collective-permute-start.17 = (f32[16,512]{1,0:T(8,128)S(1)}, f32[16,512]{1,0:T(8,128)S(1)}, u32[]{:S(2)}, u32[]{:S(2)}) collective-permute-start(f32[16,512]{1,0:T(8,128)S(1)} %add.20), channel_id=1, source_target_pairs={{0,6},{1,7},{2,4},{3,5},{4,2},{5,3},{6,0},{7,1},{8,14},{9,15},{10,... | collective-permute-start | bytes 98312 | tf_op jit(solution)/shard_map/ppermute | solution.py:693
  59.4 0.6 collective-permute-start.15
  60.1 1.0 %unpack.1 = (bf16[256,512]{1,0:T(8,128)(2,1)}, bf16[256,512]{1,0:T(8,128)(2,1)}, bf16[256,512]{1,0:T(8,128)(2,1)}, bf16[256,512]{1,0:T(8,128)(2,1)}, f32[4,256]{1,0:T(4,128)}, /*index=5*/f32[4,256]{1,0:T(4,128)}) custom-call(bf16[1040,128]{1,0:T(8,128)(2,1)S(1)} %get-tuple-element.97.refs_0_, bf16[1040,128]{1,0:T(8,128)(2,1)S(1)} %collective-permute-done.12.refs_1_, ...), custom_call_target="tpu_custom_call" | custom-call | flops 2000000000 | bytes 6000000 | tf_op jit(solution)/shard_map/unpack/pallas_call | solution.py:184
  61.1 0.2 collective-permute-done.17
  61.3 2.9 %collective-permute-done.16 = f32[16,512]{1,0:T(8,128)S(1)} collective-permute-done((f32[16,512]{1,0:T(8,128)S(1)}, f32[16,512]{1,0:T(8,128)S(1)}, u32[]{:S(2)}, u32[]{:S(2)}) %collective-permute-start.16) | collective-permute-done | bytes 32800 | tf_op jit(solution)/shard_map/ppermute | solution.py:693
  64.2 0.6 fusion
  (21 shorter events, 0.1 us)
Async XLA Ops:
  0.6 17.8 %copy-start = (f32[4,512]{1,0:T(4,128)S(1)}, f32[4,512]{1,0:T(4,128)}, u32[]{:S(2)}) copy-start(f32[4,512]{1,0:T(4,128)} %refs_5_.1) | copy-start | bytes 24580
  0.7 17.8 %copy-start.1 = (f32[4,512]{1,0:T(4,128)S(1)}, f32[4,512]{1,0:T(4,128)}, u32[]{:S(2)}) copy-start(f32[4,512]{1,0:T(4,128)} %refs_6_.1) | copy-start | bytes 24580
  0.7 17.8 %copy-start.2 = (f32[4,512]{1,0:T(4,128)S(1)}, f32[4,512]{1,0:T(4,128)}, u32[]{:S(2)}) copy-start(f32[4,512]{1,0:T(4,128)} %refs_7_.1) | copy-start | bytes 24580
  2.1 9.4 %collective-permute-start = (bf16[1040,128]{1,0:T(8,128)(2,1)S(1)}, bf16[1040,128]{1,0:T(8,128)(2,1)S(1)}, u32[]{:S(2)}, u32[]{:S(2)}) collective-permute-start(bf16[1040,128]{1,0:T(8,128)(2,1)S(1)} %get-tuple-element.61), channel_id=1, source_target_pairs={{0,1},{1,0},{2,3},{3,2},{4,5},{5,4},{6,7},{7,6},{8,9},{9,8},{10,11... | collective-permute-start | bytes 798728 | tf_op jit(solution)/shard_map/ppermute | solution.py:661
  5.1 9.3 %collective-permute-start.1 = (bf16[1040,128]{1,0:T(8,128)(2,1)S(1)}, bf16[1040,128]{1,0:T(8,128)(2,1)S(1)}, u32[]{:S(2)}, u32[]{:S(2)}) collective-permute-start(bf16[1040,128]{1,0:T(8,128)(2,1)S(1)} %get-tuple-element.62), channel_id=1, source_target_pairs={{0,2},{1,3},{2,0},{3,1},{4,6},{5,7},{6,4},{7,5},{8,10},{9,11},{10,... | collective-permute-start | bytes 798728 | tf_op jit(solution)/shard_map/ppermute | solution.py:661
  6.7 11.8 %collective-permute-start.2 = (bf16[1040,128]{1,0:T(8,128)(2,1)S(1)}, bf16[1040,128]{1,0:T(8,128)(2,1)S(1)}, u32[]{:S(2)}, u32[]{:S(2)}) collective-permute-start(bf16[1040,128]{1,0:T(8,128)(2,1)S(1)} %get-tuple-element.63), channel_id=1, source_target_pairs={{0,3},{1,2},{2,1},{3,0},{4,7},{5,6},{6,5},{7,4},{8,11},{9,10},{10,... | collective-permute-start | bytes 798728 | tf_op jit(solution)/shard_map/ppermute | solution.py:661
  6.7 1.3 %collective-permute-start.3 = (bf16[3,8,128]{2,1,0:T(8,128)(2,1)S(1)}, bf16[3,8,128]{2,1,0:T(8,128)(2,1)S(1)}, u32[]{:S(2)}, u32[]{:S(2)}) collective-permute-start(bf16[3,8,128]{2,1,0:T(8,128)(2,1)S(1)} %get-tuple-element.64), channel_id=1, source_target_pairs={{3,4},{11,12},{19,20},{27,28}} | collective-permute-start | bytes 18440 | tf_op jit(solution)/shard_map/ppermute | solution.py:714
  7.3 1.4 %collective-permute-start.4 = (bf16[3,8,128]{2,1,0:T(8,128)(2,1)S(1)}, bf16[3,8,128]{2,1,0:T(8,128)(2,1)S(1)}, u32[]{:S(2)}, u32[]{:S(2)}) collective-permute-start(bf16[3,8,128]{2,1,0:T(8,128)(2,1)S(1)} %get-tuple-element.65), channel_id=1, source_target_pairs={{3,5},{11,13},{19,21},{27,29}} | collective-permute-start | bytes 18440 | tf_op jit(solution)/shard_map/ppermute | solution.py:714
  8.0 1.4 %collective-permute-start.5 = (bf16[3,8,128]{2,1,0:T(8,128)(2,1)S(1)}, bf16[3,8,128]{2,1,0:T(8,128)(2,1)S(1)}, u32[]{:S(2)}, u32[]{:S(2)}) collective-permute-start(bf16[3,8,128]{2,1,0:T(8,128)(2,1)S(1)} %get-tuple-element.66), channel_id=1, source_target_pairs={{3,6},{11,14},{19,22},{27,30}} | collective-permute-start | bytes 18440 | tf_op jit(solution)/shard_map/ppermute | solution.py:714
  8.7 0.7 %collective-permute-start.6 = (bf16[3,8,128]{2,1,0:T(8,128)(2,1)S(1)}, bf16[3,8,128]{2,1,0:T(8,128)(2,1)S(1)}, u32[]{:S(2)}, u32[]{:S(2)}) collective-permute-start(bf16[3,8,128]{2,1,0:T(8,128)(2,1)S(1)} %get-tuple-element.67), channel_id=1, source_target_pairs={{3,7},{11,15},{19,23},{27,31}} | collective-permute-start | bytes 18440 | tf_op jit(solution)/shard_map/ppermute | solution.py:714
  26.3 5.2 %collective-permute-start.7 = (f32[128,128]{1,0:T(8,128)S(1)}, f32[128,128]{1,0:T(8,128)S(1)}, u32[]{:S(2)}, u32[]{:S(2)}) collective-permute-start(f32[128,128]{1,0:T(8,128)S(1)} %get-tuple-element.81), channel_id=1, source_target_pairs={{0,4},{1,5},{2,6},{3,7},{4,0},{5,1},{6,2},{7,3},{8,12},{9,13},{10,... | collective-permute-start | bytes 196616 | tf_op jit(solution)/shard_map/ppermute | solution.py:724
  33.5 6.5 %collective-permute-start.9 = (f32[3,8,128]{2,1,0:T(8,128)S(1)}, f32[3,8,128]{2,1,0:T(8,128)S(1)}, u32[]{:S(2)}, u32[]{:S(2)}) collective-permute-start(f32[3,8,128]{2,1,0:T(8,128)S(1)} %get-tuple-element.88), channel_id=1, source_target_pairs={{4,0},{5,1},{6,2},{7,3},{12,8},{13,9},{14,10},{15,11},{20,16},{21,... | collective-permute-start | bytes 36872 | tf_op jit(solution)/shard_map/ppermute | solution.py:674
  39.6 1.3 %collective-permute-start.8 = (f32[16,512]{1,0:T(8,128)S(1)}, f32[16,512]{1,0:T(8,128)S(1)}, u32[]{:S(2)}, u32[]{:S(2)}) collective-permute-start(f32[16,512]{1,0:T(8,128)S(1)} %get-tuple-element.85), channel_id=1, source_target_pairs={{0,8},{1,9},{2,10},{3,11},{4,12},{5,13},{6,14},{7,15},{8,0},{9,1},... | collective-permute-start | bytes 98312 | tf_op jit(solution)/shard_map/ppermute | solution.py:693
  40.9 13.7 %collective-permute-start.12 = (bf16[1040,128]{1,0:T(8,128)(2,1)S(1)}, bf16[1040,128]{1,0:T(8,128)(2,1)S(1)}, u32[]{:S(2)}, u32[]{:S(2)}) collective-permute-start(bf16[1040,128]{1,0:T(8,128)(2,1)S(1)} %get-tuple-element.99), channel_id=1, source_target_pairs={{0,1},{1,0},{2,3},{3,2},{4,5},{5,4},{6,7},{7,6},{8,9},{9,8},{10,11... | collective-permute-start | bytes 798728 | tf_op jit(solution)/shard_map/ppermute | solution.py:661
  42.5 12.0 %collective-permute-start.13 = (bf16[1040,128]{1,0:T(8,128)(2,1)S(1)}, bf16[1040,128]{1,0:T(8,128)(2,1)S(1)}, u32[]{:S(2)}, u32[]{:S(2)}) collective-permute-start(bf16[1040,128]{1,0:T(8,128)(2,1)S(1)} %get-tuple-element.100), channel_id=1, source_target_pairs={{0,2},{1,3},{2,0},{3,1},{4,6},{5,7},{6,4},{7,5},{8,10},{9,11},{10,... | collective-permute-start | bytes 798728 | tf_op jit(solution)/shard_map/ppermute | solution.py:661
  44.1 15.9 %collective-permute-start.14 = (bf16[1040,128]{1,0:T(8,128)(2,1)S(1)}, bf16[1040,128]{1,0:T(8,128)(2,1)S(1)}, u32[]{:S(2)}, u32[]{:S(2)}) collective-permute-start(bf16[1040,128]{1,0:T(8,128)(2,1)S(1)} %get-tuple-element.103), channel_id=1, source_target_pairs={{0,3},{1,2},{2,1},{3,0},{4,7},{5,6},{6,5},{7,4},{8,11},{9,10},{10,... | collective-permute-start | bytes 798728 | tf_op jit(solution)/shard_map/ppermute | solution.py:661
  44.4 6.3 %collective-permute-start.10 = (f32[16,512]{1,0:T(8,128)S(1)}, f32[16,512]{1,0:T(8,128)S(1)}, u32[]{:S(2)}, u32[]{:S(2)}) collective-permute-start(f32[16,512]{1,0:T(8,128)S(1)} %add.18), channel_id=1, source_target_pairs={{0,1},{1,0},{2,3},{3,2},{4,5},{5,4},{6,7},{7,6},{8,9},{9,8},{10,11... | collective-permute-start | bytes 98312 | tf_op jit(solution)/shard_map/ppermute | solution.py:693
  50.6 3.9 %collective-permute-start.11 = (f32[16,512]{1,0:T(8,128)S(1)}, f32[16,512]{1,0:T(8,128)S(1)}, u32[]{:S(2)}, u32[]{:S(2)}) collective-permute-start(f32[16,512]{1,0:T(8,128)S(1)} %add.19), channel_id=1, source_target_pairs={{0,16},{1,17},{2,18},{3,19},{4,20},{5,21},{6,22},{7,23},{8,24},{9,... | collective-permute-start | bytes 98312 | tf_op jit(solution)/shard_map/ppermute | solution.py:693
  54.6 6.7 %collective-permute-start.17 = (f32[16,512]{1,0:T(8,128)S(1)}, f32[16,512]{1,0:T(8,128)S(1)}, u32[]{:S(2)}, u32[]{:S(2)}) collective-permute-start(f32[16,512]{1,0:T(8,128)S(1)} %add.20), channel_id=1, source_target_pairs={{0,6},{1,7},{2,4},{3,5},{4,2},{5,3},{6,0},{7,1},{8,14},{9,15},{10,... | collective-permute-start | bytes 98312 | tf_op jit(solution)/shard_map/ppermute | solution.py:693
  59.4 4.8 %collective-permute-start.16 = (f32[16,512]{1,0:T(8,128)S(1)}, f32[16,512]{1,0:T(8,128)S(1)}, u32[]{:S(2)}, u32[]{:S(2)}) collective-permute-start(f32[16,512]{1,0:T(8,128)S(1)} %add.20), channel_id=1, source_target_pairs={{0,4},{1,5},{2,6},{3,7},{4,0},{5,1},{6,2},{7,3},{8,12},{9,13},{10,... | collective-permute-start | bytes 98312 | tf_op jit(solution)/shard_map/ppermute | solution.py:693
  59.4 4.8 %collective-permute-start.15 = (f32[16,512]{1,0:T(8,128)S(1)}, f32[16,512]{1,0:T(8,128)S(1)}, u32[]{:S(2)}, u32[]{:S(2)}) collective-permute-start(f32[16,512]{1,0:T(8,128)S(1)} %add.20), channel_id=1, source_target_pairs={{0,2},{1,3},{2,0},{3,1},{4,6},{5,7},{6,4},{7,5},{8,10},{9,11},{10,... | collective-permute-start | bytes 98312 | tf_op jit(solution)/shard_map/ppermute | solution.py:693

commit v5 on v4

--- a/solution.py
+++ b/solution.py
@@ -682,7 +682,7 @@
         return None
     high = [inner << place for place in range(outer.bit_length() - 1)]
     low = [1 << place for place in range(inner.bit_length() - 1)]
-    bits = high[:1] + low[:1] + high[1:] + low[1:]
+    bits = low[:1] + high + low[1:]
     return [[bit] for bit in bits[:-2]] + [bits[-2:]]
 
 

time: 65.1 us -> 63 us (0.968)
  waiting for transfers between devices: 22 us -> 20.1 us
    ppermute x6, waiting for transfers between devices: 10.2 us -> 8.49 us  [swapped(): return lax.ppermute(value, axes, [(d, d ^ mask) for d in range(count)])]
where the time goes in v5:
time: 63 us; the launch traced here: 62.8 us
  starting transfers between devices  23.7 us (38%)
  waiting for transfers between devices  20.1 us (32%)
  Pallas kernels  17.5 us (28%)
  between operations  0.78 us (1%)
    ppermute x6, waiting for transfers between devices, trade_one(): return lax.ppermute(value, axis, pairs)  9.24 us
    ppermute x6, starting transfers between devices, swapped(): return lax.ppermute(value, axes, [(d, d ^ mask) for d in range(count)])  8.78 us
    ppermute x6, waiting for transfers between devices, swapped(): return lax.ppermute(value, axes, [(d, d ^ mask) for d in range(count)])  8.49 us
    ppermute x6, starting transfers between devices, trade_one(): return lax.ppermute(value, axis, pairs)  8.06 us
    pallas_call x1, Pallas kernels, local_part(): pl.pallas_call(functools.partial(local_kernel, heads, axis), out_shape=ou...  7.8 us
    pallas_call x1, Pallas kernels, final_part(): pl.pallas_call(functools.partial(final_kernel, heads, axis), out_shape=ou...  4.63 us
    ppermute x1, starting transfers between devices, body(): lax.ppermute(state, axis, [(d, (d + heads) % count) for d in range(count)])  2.76 us
    ppermute x4, starting transfers between devices, body(): lax.ppermute(tails[head], axis, [(g * heads - 1, g * heads + head) for g...  2.63 us
  transfers between devices with their start and end apart: 18, of which 10 were waited for; matrix products, arithmetic and copies ran while one was open for 0% of the time, Pallas kernels for 10%

profile of v5, /device:TPU:0, one launch (start us, length us, event | category | flops | bytes accessed | tf_op | source)
XLA Modules:
  0.0 62.8 jit_solution(3371685369609336859)
XLA Ops:
  0.7 1.4 %pack.1 = (bf16[1040,128]{1,0:T(8,128)(2,1)S(1)}, bf16[1040,128]{1,0:T(8,128)(2,1)S(1)}, bf16[1040,128]{1,0:T(8,128)(2,1)S(1)}, bf16[1040,128]{1,0:T(8,128)(2,1)...) custom-call(bf16[256,512]{1,0:T(8,128)(2,1)} %bitcast.20, ...), custom_call_target="tpu_custom_call" | custom-call | flops 2000000000 | bytes 6000000 | tf_op jit(solution)/shard_map/pack/pallas_call | solution.py:142
  2.1 3.0 %collective-permute-start = (bf16[1040,128]{1,0:T(8,128)(2,1)S(1)}, bf16[1040,128]{1,0:T(8,128)(2,1)S(1)}, u32[]{:S(2)}, u32[]{:S(2)}) collective-permute-start(bf16[1040,128]{1,0:T(8,128)(2,1)S(1)} %get-tuple-element.61), channel_id=1, source_target_pairs={{0,1},{1,0},{2,3},{3,2},{4,5},{5,4},{6,7},{7,6},{8,9},{9,8},{10,11... | collective-permute-start | bytes 798728 | tf_op jit(solution)/shard_map/ppermute | solution.py:661
  5.1 1.6 %collective-permute-start.1 = (bf16[1040,128]{1,0:T(8,128)(2,1)S(1)}, bf16[1040,128]{1,0:T(8,128)(2,1)S(1)}, u32[]{:S(2)}, u32[]{:S(2)}) collective-permute-start(bf16[1040,128]{1,0:T(8,128)(2,1)S(1)} %get-tuple-element.62), channel_id=1, source_target_pairs={{0,2},{1,3},{2,0},{3,1},{4,6},{5,7},{6,4},{7,5},{8,10},{9,11},{10,... | collective-permute-start | bytes 798728 | tf_op jit(solution)/shard_map/ppermute | solution.py:661
  6.7 0.7 %collective-permute-start.3 = (bf16[3,8,128]{2,1,0:T(8,128)(2,1)S(1)}, bf16[3,8,128]{2,1,0:T(8,128)(2,1)S(1)}, u32[]{:S(2)}, u32[]{:S(2)}) collective-permute-start(bf16[3,8,128]{2,1,0:T(8,128)(2,1)S(1)} %get-tuple-element.64), channel_id=1, source_target_pairs={{3,4},{11,12},{19,20},{27,28}} | collective-permute-start | bytes 18440 | tf_op jit(solution)/shard_map/ppermute | solution.py:714
  7.3 0.7 %collective-permute-start.4 = (bf16[3,8,128]{2,1,0:T(8,128)(2,1)S(1)}, bf16[3,8,128]{2,1,0:T(8,128)(2,1)S(1)}, u32[]{:S(2)}, u32[]{:S(2)}) collective-permute-start(bf16[3,8,128]{2,1,0:T(8,128)(2,1)S(1)} %get-tuple-element.65), channel_id=1, source_target_pairs={{3,5},{11,13},{19,21},{27,29}} | collective-permute-start | bytes 18440 | tf_op jit(solution)/shard_map/ppermute | solution.py:714
  8.0 0.7 %collective-permute-start.5 = (bf16[3,8,128]{2,1,0:T(8,128)(2,1)S(1)}, bf16[3,8,128]{2,1,0:T(8,128)(2,1)S(1)}, u32[]{:S(2)}, u32[]{:S(2)}) collective-permute-start(bf16[3,8,128]{2,1,0:T(8,128)(2,1)S(1)} %get-tuple-element.66), channel_id=1, source_target_pairs={{3,6},{11,14},{19,22},{27,30}} | collective-permute-start | bytes 18440 | tf_op jit(solution)/shard_map/ppermute | solution.py:714
  8.7 0.7 %collective-permute-start.6 = (bf16[3,8,128]{2,1,0:T(8,128)(2,1)S(1)}, bf16[3,8,128]{2,1,0:T(8,128)(2,1)S(1)}, u32[]{:S(2)}, u32[]{:S(2)}) collective-permute-start(bf16[3,8,128]{2,1,0:T(8,128)(2,1)S(1)} %get-tuple-element.67), channel_id=1, source_target_pairs={{3,7},{11,15},{19,23},{27,31}} | collective-permute-start | bytes 18440 | tf_op jit(solution)/shard_map/ppermute | solution.py:714
  9.4 2.1 %collective-permute-done.refs_1_ = bf16[1040,128]{1,0:T(8,128)(2,1)S(1)} collective-permute-done((bf16[1040,128]{1,0:T(8,128)(2,1)S(1)}, bf16[1040,128]{1,0:T(8,128)(2,1)S(1)}, u32[]{:S(2)}, u32[]{:S(2)}) %collective-permute-start) | collective-permute-done | bytes 266272 | tf_op jit(solution)/shard_map/ppermute | solution.py:661
  11.5 2.9 %collective-permute-done.1.refs_2_ = bf16[1040,128]{1,0:T(8,128)(2,1)S(1)} collective-permute-done((bf16[1040,128]{1,0:T(8,128)(2,1)S(1)}, bf16[1040,128]{1,0:T(8,128)(2,1)S(1)}, u32[]{:S(2)}, u32[]{:S(2)}) %collective-permute-start.1) | collective-permute-done | bytes 266272 | tf_op jit(solution)/shard_map/ppermute | solution.py:661
  14.4 4.0 %collective-permute-done.2.refs_3_ = bf16[1040,128]{1,0:T(8,128)(2,1)S(1)} collective-permute-done((bf16[1040,128]{1,0:T(8,128)(2,1)S(1)}, bf16[1040,128]{1,0:T(8,128)(2,1)S(1)}, u32[]{:S(2)}, u32[]{:S(2)}) %collective-permute-start.2) | collective-permute-done | bytes 266272 | tf_op jit(solution)/shard_map/ppermute | solution.py:661
  18.5 7.8 %local_part.1 = (bf16[4,1024,128]{2,1,0:T(8,128)(2,1)S(1)}, f32[2,8,128]{2,1,0:T(8,128)S(1)}, f32[1024,128]{1,0:T(8,128)S(1)}, f32[1024,128]{1,0:T(8,128)S(1)}, ...) custom-call(bf16[1040,128]{1,0:T(8,128)(2,1)S(1)} %get-tuple-element, ...), custom_call_target="tpu_custom_call" | custom-call | flops 10000000000 | bytes 30000000 | tf_op jit(solution)/shard_map/local_part/pallas_call | solution.py:361
  26.3 2.8 %collective-permute-start.7 = (f32[128,128]{1,0:T(8,128)S(1)}, f32[128,128]{1,0:T(8,128)S(1)}, u32[]{:S(2)}, u32[]{:S(2)}) collective-permute-start(f32[128,128]{1,0:T(8,128)S(1)} %get-tuple-element.81), channel_id=1, source_target_pairs={{0,4},{1,5},{2,6},{3,7},{4,0},{5,1},{6,2},{7,3},{8,12},{9,13},{10,... | collective-permute-start | bytes 196616 | tf_op jit(solution)/shard_map/ppermute | solution.py:724
  29.0 2.4 %collective-permute-done.7.refs_20_.refs_21_ = f32[128,128]{1,0:T(8,128)S(1)} collective-permute-done((f32[128,128]{1,0:T(8,128)S(1)}, f32[128,128]{1,0:T(8,128)S(1)}, u32[]{:S(2)}, u32[]{:S(2)}) %collective-permute-start.7) | collective-permute-done | bytes 65568 | tf_op jit(solution)/shard_map/ppermute | solution.py:724
  31.4 2.0 %state_part.1 = (f32[9,128,128]{2,1,0:T(8,128)S(1)}, f32[9,128,128]{2,1,0:T(8,128)S(1)}, f32[3,128,128]{2,1,0:T(8,128)S(1)}, f32[2,1,128]{2,1,0:T(1,128)S(1)}, f...) custom-call(bf16[4,1024,128]{2,1,0:T(8,128)(2,1)S(1)} %get-tuple-element.68.refs_0_, ...), custom_call_target="tpu_custom_call" | custom-call | flops 7000000000 | bytes 21000000 | tf_op jit(solution)/shard_map/state_part/pallas_call | solution.py:515
  33.5 1.5 %collective-permute-start.9 = (f32[3,8,128]{2,1,0:T(8,128)S(1)}, f32[3,8,128]{2,1,0:T(8,128)S(1)}, u32[]{:S(2)}, u32[]{:S(2)}) collective-permute-start(f32[3,8,128]{2,1,0:T(8,128)S(1)} %get-tuple-element.88), channel_id=1, source_target_pairs={{4,0},{5,1},{6,2},{7,3},{12,8},{13,9},{14,10},{15,11},{20,16},{21,... | collective-permute-start | bytes 36872 | tf_op jit(solution)/shard_map/ppermute | solution.py:674
  35.0 4.6 %final_part.1 = (f32[3,896,128]{2,1,0:T(8,128)S(1)}, f32[2,7,128]{2,1,0:T(8,128)S(1)}, f32[16,512]{1,0:T(8,128)S(1)}, bf16[896,128]{1,0:T(8,128)(2,1)S(1)}) custom-call(bf16[4,1024,128]{2,1,0:T(8,128)(2,1)S(1)} %get-tuple-element.68.refs_0_, f32[2,8,128]{2,1,0:T(8,128)S(1)} %get-tuple-element.69.refs_5_.refs_1_, ...), custom_call_target="tpu_custom_call" | custom-call | flops 8000000000 | bytes 24000000 | tf_op jit(solution)/shard_map/final_part/pallas_call | solution.py:577
  39.6 1.7 %collective-permute-start.8 = (f32[16,512]{1,0:T(8,128)S(1)}, f32[16,512]{1,0:T(8,128)S(1)}, u32[]{:S(2)}, u32[]{:S(2)}) collective-permute-start(f32[16,512]{1,0:T(8,128)S(1)} %get-tuple-element.85), channel_id=1, source_target_pairs={{0,1},{1,0},{2,3},{3,2},{4,5},{5,4},{6,7},{7,6},{8,9},{9,8},{10,11... | collective-permute-start | bytes 98312 | tf_op jit(solution)/shard_map/ppermute | solution.py:693
  41.3 0.6 input_part.1
  41.9 1.9 %collective-permute-done.8 = f32[16,512]{1,0:T(8,128)S(1)} collective-permute-done((f32[16,512]{1,0:T(8,128)S(1)}, f32[16,512]{1,0:T(8,128)S(1)}, u32[]{:S(2)}, u32[]{:S(2)}) %collective-permute-start.8) | collective-permute-done | bytes 32800 | tf_op jit(solution)/shard_map/ppermute | solution.py:693
  43.9 1.7 %collective-permute-start.12 = (bf16[1040,128]{1,0:T(8,128)(2,1)S(1)}, bf16[1040,128]{1,0:T(8,128)(2,1)S(1)}, u32[]{:S(2)}, u32[]{:S(2)}) collective-permute-start(bf16[1040,128]{1,0:T(8,128)(2,1)S(1)} %get-tuple-element.99), channel_id=1, source_target_pairs={{0,1},{1,0},{2,3},{3,2},{4,5},{5,4},{6,7},{7,6},{8,9},{9,8},{10,11... | collective-permute-start | bytes 798728 | tf_op jit(solution)/shard_map/ppermute | solution.py:661
  45.5 1.6 %collective-permute-start.13 = (bf16[1040,128]{1,0:T(8,128)(2,1)S(1)}, bf16[1040,128]{1,0:T(8,128)(2,1)S(1)}, u32[]{:S(2)}, u32[]{:S(2)}) collective-permute-start(bf16[1040,128]{1,0:T(8,128)(2,1)S(1)} %get-tuple-element.100), channel_id=1, source_target_pairs={{0,2},{1,3},{2,0},{3,1},{4,6},{5,7},{6,4},{7,5},{8,10},{9,11},{10,... | collective-permute-start | bytes 798728 | tf_op jit(solution)/shard_map/ppermute | solution.py:661
  47.1 0.2 collective-permute-start.14
  47.3 1.2 %collective-permute-done.10 = f32[16,512]{1,0:T(8,128)S(1)} collective-permute-done((f32[16,512]{1,0:T(8,128)S(1)}, f32[16,512]{1,0:T(8,128)S(1)}, u32[]{:S(2)}, u32[]{:S(2)}) %collective-permute-start.10) | collective-permute-done | bytes 32800 | tf_op jit(solution)/shard_map/ppermute | solution.py:693
  48.6 1.7 %collective-permute-start.11 = (f32[16,512]{1,0:T(8,128)S(1)}, f32[16,512]{1,0:T(8,128)S(1)}, u32[]{:S(2)}, u32[]{:S(2)}) collective-permute-start(f32[16,512]{1,0:T(8,128)S(1)} %add.19), channel_id=1, source_target_pairs={{0,16},{1,17},{2,18},{3,19},{4,20},{5,21},{6,22},{7,23},{8,24},{9,... | collective-permute-start | bytes 98312 | tf_op jit(solution)/shard_map/ppermute | solution.py:693
  50.3 2.2 %collective-permute-done.11 = f32[16,512]{1,0:T(8,128)S(1)} collective-permute-done((f32[16,512]{1,0:T(8,128)S(1)}, f32[16,512]{1,0:T(8,128)S(1)}, u32[]{:S(2)}, u32[]{:S(2)}) %collective-permute-start.11) | collective-permute-done | bytes 32800 | tf_op jit(solution)/shard_map/ppermute | solution.py:693
  52.5 0.1 collective-permute-done.12.refs_1_
  52.6 4.7 %collective-permute-start.17 = (f32[16,512]{1,0:T(8,128)S(1)}, f32[16,512]{1,0:T(8,128)S(1)}, u32[]{:S(2)}, u32[]{:S(2)}) collective-permute-start(f32[16,512]{1,0:T(8,128)S(1)} %add.20), channel_id=1, source_target_pairs={{0,6},{1,7},{2,4},{3,5},{4,2},{5,3},{6,0},{7,1},{8,14},{9,15},{10,... | collective-permute-start | bytes 98312 | tf_op jit(solution)/shard_map/ppermute | solution.py:693
  57.4 0.6 %collective-permute-start.15 = (f32[16,512]{1,0:T(8,128)S(1)}, f32[16,512]{1,0:T(8,128)S(1)}, u32[]{:S(2)}, u32[]{:S(2)}) collective-permute-start(f32[16,512]{1,0:T(8,128)S(1)} %add.20), channel_id=1, source_target_pairs={{0,2},{1,3},{2,0},{3,1},{4,6},{5,7},{6,4},{7,5},{8,10},{9,11},{10,... | collective-permute-start | bytes 98312 | tf_op jit(solution)/shard_map/ppermute | solution.py:693
  58.0 1.0 %unpack.1 = (bf16[256,512]{1,0:T(8,128)(2,1)}, bf16[256,512]{1,0:T(8,128)(2,1)}, bf16[256,512]{1,0:T(8,128)(2,1)}, bf16[256,512]{1,0:T(8,128)(2,1)}, f32[4,256]{1,0:T(4,128)}, /*index=5*/f32[4,256]{1,0:T(4,128)}) custom-call(bf16[1040,128]{1,0:T(8,128)(2,1)S(1)} %get-tuple-element.97.refs_0_, bf16[1040,128]{1,0:T(8,128)(2,1)S(1)} %collective-permute-done.12.refs_1_, ...), custom_call_target="tpu_custom_call" | custom-call | flops 2000000000 | bytes 6000000 | tf_op jit(solution)/shard_map/unpack/pallas_call | solution.py:184
  59.0 0.4 collective-permute-done.17
  59.5 2.7 %collective-permute-done.16 = f32[16,512]{1,0:T(8,128)S(1)} collective-permute-done((f32[16,512]{1,0:T(8,128)S(1)}, f32[16,512]{1,0:T(8,128)S(1)}, u32[]{:S(2)}, u32[]{:S(2)}) %collective-permute-start.16) | collective-permute-done | bytes 32800 | tf_op jit(solution)/shard_map/ppermute | solution.py:693
  62.2 0.6 fusion
  (21 shorter events, 0.1 us)
Async XLA Ops:
  0.6 17.8 %copy-start = (f32[4,512]{1,0:T(4,128)S(1)}, f32[4,512]{1,0:T(4,128)}, u32[]{:S(2)}) copy-start(f32[4,512]{1,0:T(4,128)} %refs_5_.1) | copy-start | bytes 24580
  0.7 17.8 %copy-start.1 = (f32[4,512]{1,0:T(4,128)S(1)}, f32[4,512]{1,0:T(4,128)}, u32[]{:S(2)}) copy-start(f32[4,512]{1,0:T(4,128)} %refs_6_.1) | copy-start | bytes 24580
  0.7 17.8 %copy-start.2 = (f32[4,512]{1,0:T(4,128)S(1)}, f32[4,512]{1,0:T(4,128)}, u32[]{:S(2)}) copy-start(f32[4,512]{1,0:T(4,128)} %refs_7_.1) | copy-start | bytes 24580
  2.1 9.4 %collective-permute-start = (bf16[1040,128]{1,0:T(8,128)(2,1)S(1)}, bf16[1040,128]{1,0:T(8,128)(2,1)S(1)}, u32[]{:S(2)}, u32[]{:S(2)}) collective-permute-start(bf16[1040,128]{1,0:T(8,128)(2,1)S(1)} %get-tuple-element.61), channel_id=1, source_target_pairs={{0,1},{1,0},{2,3},{3,2},{4,5},{5,4},{6,7},{7,6},{8,9},{9,8},{10,11... | collective-permute-start | bytes 798728 | tf_op jit(solution)/shard_map/ppermute | solution.py:661
  5.1 9.3 %collective-permute-start.1 = (bf16[1040,128]{1,0:T(8,128)(2,1)S(1)}, bf16[1040,128]{1,0:T(8,128)(2,1)S(1)}, u32[]{:S(2)}, u32[]{:S(2)}) collective-permute-start(bf16[1040,128]{1,0:T(8,128)(2,1)S(1)} %get-tuple-element.62), channel_id=1, source_target_pairs={{0,2},{1,3},{2,0},{3,1},{4,6},{5,7},{6,4},{7,5},{8,10},{9,11},{10,... | collective-permute-start | bytes 798728 | tf_op jit(solution)/shard_map/ppermute | solution.py:661
  6.7 11.8 %collective-permute-start.2 = (bf16[1040,128]{1,0:T(8,128)(2,1)S(1)}, bf16[1040,128]{1,0:T(8,128)(2,1)S(1)}, u32[]{:S(2)}, u32[]{:S(2)}) collective-permute-start(bf16[1040,128]{1,0:T(8,128)(2,1)S(1)} %get-tuple-element.63), channel_id=1, source_target_pairs={{0,3},{1,2},{2,1},{3,0},{4,7},{5,6},{6,5},{7,4},{8,11},{9,10},{10,... | collective-permute-start | bytes 798728 | tf_op jit(solution)/shard_map/ppermute | solution.py:661
  6.7 1.3 %collective-permute-start.3 = (bf16[3,8,128]{2,1,0:T(8,128)(2,1)S(1)}, bf16[3,8,128]{2,1,0:T(8,128)(2,1)S(1)}, u32[]{:S(2)}, u32[]{:S(2)}) collective-permute-start(bf16[3,8,128]{2,1,0:T(8,128)(2,1)S(1)} %get-tuple-element.64), channel_id=1, source_target_pairs={{3,4},{11,12},{19,20},{27,28}} | collective-permute-start | bytes 18440 | tf_op jit(solution)/shard_map/ppermute | solution.py:714
  7.3 1.4 %collective-permute-start.4 = (bf16[3,8,128]{2,1,0:T(8,128)(2,1)S(1)}, bf16[3,8,128]{2,1,0:T(8,128)(2,1)S(1)}, u32[]{:S(2)}, u32[]{:S(2)}) collective-permute-start(bf16[3,8,128]{2,1,0:T(8,128)(2,1)S(1)} %get-tuple-element.65), channel_id=1, source_target_pairs={{3,5},{11,13},{19,21},{27,29}} | collective-permute-start | bytes 18440 | tf_op jit(solution)/shard_map/ppermute | solution.py:714
  8.0 1.4 %collective-permute-start.5 = (bf16[3,8,128]{2,1,0:T(8,128)(2,1)S(1)}, bf16[3,8,128]{2,1,0:T(8,128)(2,1)S(1)}, u32[]{:S(2)}, u32[]{:S(2)}) collective-permute-start(bf16[3,8,128]{2,1,0:T(8,128)(2,1)S(1)} %get-tuple-element.66), channel_id=1, source_target_pairs={{3,6},{11,14},{19,22},{27,30}} | collective-permute-start | bytes 18440 | tf_op jit(solution)/shard_map/ppermute | solution.py:714
  8.7 0.7 %collective-permute-start.6 = (bf16[3,8,128]{2,1,0:T(8,128)(2,1)S(1)}, bf16[3,8,128]{2,1,0:T(8,128)(2,1)S(1)}, u32[]{:S(2)}, u32[]{:S(2)}) collective-permute-start(bf16[3,8,128]{2,1,0:T(8,128)(2,1)S(1)} %get-tuple-element.67), channel_id=1, source_target_pairs={{3,7},{11,15},{19,23},{27,31}} | collective-permute-start | bytes 18440 | tf_op jit(solution)/shard_map/ppermute | solution.py:714
  26.3 5.2 %collective-permute-start.7 = (f32[128,128]{1,0:T(8,128)S(1)}, f32[128,128]{1,0:T(8,128)S(1)}, u32[]{:S(2)}, u32[]{:S(2)}) collective-permute-start(f32[128,128]{1,0:T(8,128)S(1)} %get-tuple-element.81), channel_id=1, source_target_pairs={{0,4},{1,5},{2,6},{3,7},{4,0},{5,1},{6,2},{7,3},{8,12},{9,13},{10,... | collective-permute-start | bytes 196616 | tf_op jit(solution)/shard_map/ppermute | solution.py:724
  33.5 7.8 %collective-permute-start.9 = (f32[3,8,128]{2,1,0:T(8,128)S(1)}, f32[3,8,128]{2,1,0:T(8,128)S(1)}, u32[]{:S(2)}, u32[]{:S(2)}) collective-permute-start(f32[3,8,128]{2,1,0:T(8,128)S(1)} %get-tuple-element.88), channel_id=1, source_target_pairs={{4,0},{5,1},{6,2},{7,3},{12,8},{13,9},{14,10},{15,11},{20,16},{21,... | collective-permute-start | bytes 36872 | tf_op jit(solution)/shard_map/ppermute | solution.py:674
  39.6 4.2 %collective-permute-start.8 = (f32[16,512]{1,0:T(8,128)S(1)}, f32[16,512]{1,0:T(8,128)S(1)}, u32[]{:S(2)}, u32[]{:S(2)}) collective-permute-start(f32[16,512]{1,0:T(8,128)S(1)} %get-tuple-element.85), channel_id=1, source_target_pairs={{0,1},{1,0},{2,3},{3,2},{4,5},{5,4},{6,7},{7,6},{8,9},{9,8},{10,11... | collective-permute-start | bytes 98312 | tf_op jit(solution)/shard_map/ppermute | solution.py:693
  43.9 8.7 %collective-permute-start.12 = (bf16[1040,128]{1,0:T(8,128)(2,1)S(1)}, bf16[1040,128]{1,0:T(8,128)(2,1)S(1)}, u32[]{:S(2)}, u32[]{:S(2)}) collective-permute-start(bf16[1040,128]{1,0:T(8,128)(2,1)S(1)} %get-tuple-element.99), channel_id=1, source_target_pairs={{0,1},{1,0},{2,3},{3,2},{4,5},{5,4},{6,7},{7,6},{8,9},{9,8},{10,11... | collective-permute-start | bytes 798728 | tf_op jit(solution)/shard_map/ppermute | solution.py:661
  45.5 7.1 %collective-permute-start.13 = (bf16[1040,128]{1,0:T(8,128)(2,1)S(1)}, bf16[1040,128]{1,0:T(8,128)(2,1)S(1)}, u32[]{:S(2)}, u32[]{:S(2)}) collective-permute-start(bf16[1040,128]{1,0:T(8,128)(2,1)S(1)} %get-tuple-element.100), channel_id=1, source_target_pairs={{0,2},{1,3},{2,0},{3,1},{4,6},{5,7},{6,4},{7,5},{8,10},{9,11},{10,... | collective-permute-start | bytes 798728 | tf_op jit(solution)/shard_map/ppermute | solution.py:661
  47.1 10.9 %collective-permute-start.14 = (bf16[1040,128]{1,0:T(8,128)(2,1)S(1)}, bf16[1040,128]{1,0:T(8,128)(2,1)S(1)}, u32[]{:S(2)}, u32[]{:S(2)}) collective-permute-start(bf16[1040,128]{1,0:T(8,128)(2,1)S(1)} %get-tuple-element.103), channel_id=1, source_target_pairs={{0,3},{1,2},{2,1},{3,0},{4,7},{5,6},{6,5},{7,4},{8,11},{9,10},{10,... | collective-permute-start | bytes 798728 | tf_op jit(solution)/shard_map/ppermute | solution.py:661
  47.3 1.2 %collective-permute-start.10 = (f32[16,512]{1,0:T(8,128)S(1)}, f32[16,512]{1,0:T(8,128)S(1)}, u32[]{:S(2)}, u32[]{:S(2)}) collective-permute-start(f32[16,512]{1,0:T(8,128)S(1)} %add.18), channel_id=1, source_target_pairs={{0,8},{1,9},{2,10},{3,11},{4,12},{5,13},{6,14},{7,15},{8,0},{9,1},... | collective-permute-start | bytes 98312 | tf_op jit(solution)/shard_map/ppermute | solution.py:693
  48.6 3.9 %collective-permute-start.11 = (f32[16,512]{1,0:T(8,128)S(1)}, f32[16,512]{1,0:T(8,128)S(1)}, u32[]{:S(2)}, u32[]{:S(2)}) collective-permute-start(f32[16,512]{1,0:T(8,128)S(1)} %add.19), channel_id=1, source_target_pairs={{0,16},{1,17},{2,18},{3,19},{4,20},{5,21},{6,22},{7,23},{8,24},{9,... | collective-permute-start | bytes 98312 | tf_op jit(solution)/shard_map/ppermute | solution.py:693
  52.6 6.8 %collective-permute-start.17 = (f32[16,512]{1,0:T(8,128)S(1)}, f32[16,512]{1,0:T(8,128)S(1)}, u32[]{:S(2)}, u32[]{:S(2)}) collective-permute-start(f32[16,512]{1,0:T(8,128)S(1)} %add.20), channel_id=1, source_target_pairs={{0,6},{1,7},{2,4},{3,5},{4,2},{5,3},{6,0},{7,1},{8,14},{9,15},{10,... | collective-permute-start | bytes 98312 | tf_op jit(solution)/shard_map/ppermute | solution.py:693
  57.3 4.8 %collective-permute-start.16 = (f32[16,512]{1,0:T(8,128)S(1)}, f32[16,512]{1,0:T(8,128)S(1)}, u32[]{:S(2)}, u32[]{:S(2)}) collective-permute-start(f32[16,512]{1,0:T(8,128)S(1)} %add.20), channel_id=1, source_target_pairs={{0,4},{1,5},{2,6},{3,7},{4,0},{5,1},{6,2},{7,3},{8,12},{9,13},{10,... | collective-permute-start | bytes 98312 | tf_op jit(solution)/shard_map/ppermute | solution.py:693
  57.4 4.8 %collective-permute-start.15 = (f32[16,512]{1,0:T(8,128)S(1)}, f32[16,512]{1,0:T(8,128)S(1)}, u32[]{:S(2)}, u32[]{:S(2)}) collective-permute-start(f32[16,512]{1,0:T(8,128)S(1)} %add.20), channel_id=1, source_target_pairs={{0,2},{1,3},{2,0},{3,1},{4,6},{5,7},{6,4},{7,5},{8,10},{9,11},{10,... | collective-permute-start | bytes 98312 | tf_op jit(solution)/shard_map/ppermute | solution.py:693

commit v6 on v5

--- a/solution.py
+++ b/solution.py
@@ -451,10 +451,38 @@
     return u_value, x_value, mixed.astype(BF16), kept_row
 
 
+def chains_kernel(mt_in, bt_in, ct_in, ahead, ahead_add, behind, behind_add):
+    count, width = mt_in.shape[:2]
+    ahead[0], ahead_add[0] = mt_in[0], bt_in[0]
+    behind[count - 1], behind_add[count - 1] = mt_in[count - 1].T, ct_in[count - 1]
+    behind[0], behind_add[0] = jnp.zeros((width, width), F32), jnp.zeros((width, width), F32)
+    for c in range(1, count):
+        other = count - 1 - c
+        joined = nn(split(mt_in[c]), columns_of(split(ahead[c - 1]), split(ahead_add[c - 1])))
+        ahead[c], ahead_add[c] = joined[:, :width], joined[:, width:] + bt_in[c]
+        if other > 0:
+            joined = nn(
+                split(mt_in[other].T), columns_of(split(behind[other + 1]), split(behind_add[other + 1]))
+            )
+            behind[other], behind_add[other] = joined[:, :width], joined[:, width:] + ct_in[other]
+
+
+def chains_part(mt, bt, ct):
+    return pl.pallas_call(
+        chains_kernel,
+        out_shape=[pltpu.VMEM(mt.shape, F32)] * 4,
+        in_specs=[VMEM] * 3,
+        out_specs=[VMEM] * 4,
+        compiler_params=params(),
+        cost_estimate=cost(2),
+        name="chains_part",
+    )(mt, bt, ct)
+
+
 def state_kernel(heads, axis, *refs):
     raw, tails, refs = refs[0], refs[1 : 1 + heads], refs[1 + heads :]
     (rate, q_in, k_in, v_in, p_in, u_in, w_in, x_in, y_in), refs = refs[:9], refs[9:]
-    tap_refs, (mt_in, bt_in, ct_in, state_in, back_in), refs = refs[:3], refs[3:8], refs[8:]
+    tap_refs, (ahead, ahead_add, behind, behind_add, state_in, back_in), refs = refs[:3], refs[3:9], refs[9:]
     states, backs, conv_out, rate_grad, tap_out, rim_out, mixed_out, padded = refs
     me, group = place_in_group(axis, heads)
     length, width = q_in.shape
@@ -465,12 +493,12 @@
     back = jnp.where(group < lax.axis_size(axis) // heads - 1, back_in[...], 0.0)
     states[0] = state
     backs[chunk_count] = back
+    s_pair, d_pair = split(state), split(back)
     for c in range(chunk_count):
-        other = chunk_count - 1 - c
-        state = nn(split(mt_in[c]), split(state)) + bt_in[c]
-        back = nn(split(mt_in[other].T), split(back)) + ct_in[other]
-        states[c + 1] = state
-        backs[other] = back
+        states[c + 1] = nn(split(ahead[c]), s_pair) + ahead_add[c]
+        if c > 0:
+            backs[c] = nn(split(behind[c]), d_pair) + behind_add[c]
+    backs[0] = jnp.zeros_like(back)
 
     for place in range(3):
         padded[place, 0:8, :] = tail_of(tails, place)
@@ -720,6 +748,7 @@
     tap_args = (k_taps, v_taps, q_taps)
     parts = local_part(heads, axis, q.shape[0], blocks, tails, tap_args)
     raw, rate, keys, queries, values, p, u, w, x, y, mt, bt, ct, state, back = parts
+    chains = chains_part(mt, bt, ct)
     if groups == 2:
         arriving = returning = lax.ppermute(
             state, axis, [(d, (d + heads) % count) for d in range(count)]
@@ -738,7 +767,7 @@
                     back = jnp.dot(mt[other].T, back, precision=exact) + ct[other]
     shared = (raw, *tails, rate, queries, keys, values, p, u, w, x, y, *tap_args)
     states, backs, conv, rate_grad, taps, rim, mixed = state_part(
-        heads, axis, shared, (mt, bt, ct, on_chip(arriving), on_chip(returning))
+        heads, axis, shared, (*chains, on_chip(arriving), on_chip(returning))
     )
     rim = along(rim, axis, -heads)
     args = (raw, rate, queries, keys, values, p, u, w, x, y, states, backs, taps, *tap_args)

time: 63 us -> 62.2 us (0.987)
  waiting for transfers between devices: 20.1 us -> 18.8 us
    ppermute x1, waiting for transfers between devices: 2.41 us -> 1.01 us  [body(): lax.ppermute(state, axis, [(d, (d + heads) % count) for d in range(count)])]
    pallas_call x0 -> x1, Pallas kernels: none -> 1.39 us  [chains_part(): pl.pallas_call(chains_kernel, out_shape=[pltpu.VMEM(mt.shape, F32)] * 4,...]
    pallas_call x1, Pallas kernels: 2.04 us -> 1.24 us  [state_part(): pl.pallas_call(functools.partial(state_kernel, heads, axis), out_shape=ou...]
  transfers between devices with their start and end apart: 18 -> 18, of which waited for: 10 -> 11; matrix products, arithmetic and copies ran while one was open for 0% -> 0% of each run, Pallas kernels for 10% -> 12%
where the time goes in v6:
time: 62.2 us; the launch traced here: 62 us
  starting transfers between devices  23.7 us (38%)
  waiting for transfers between devices  18.8 us (30%)
  Pallas kernels  18.1 us (29%)
  between operations  0.79 us (1%)
    ppermute x6, waiting for transfers between devices, trade_one(): return lax.ppermute(value, axis, pairs)  9.26 us
    ppermute x6, starting transfers between devices, swapped(): return lax.ppermute(value, axes, [(d, d ^ mask) for d in range(count)])  8.78 us
    ppermute x6, waiting for transfers between devices, swapped(): return lax.ppermute(value, axes, [(d, d ^ mask) for d in range(count)])  8.47 us
    ppermute x6, starting transfers between devices, trade_one(): return lax.ppermute(value, axis, pairs)  8.06 us
    pallas_call x1, Pallas kernels, local_part(): pl.pallas_call(functools.partial(local_kernel, heads, axis), out_shape=ou...  7.8 us
    pallas_call x1, Pallas kernels, final_part(): pl.pallas_call(functools.partial(final_kernel, heads, axis), out_shape=ou...  4.63 us
    ppermute x1, starting transfers between devices, body(): lax.ppermute(state, axis, [(d, (d + heads) % count) for d in range(count)])  2.76 us
    ppermute x4, starting transfers between devices, body(): lax.ppermute(tails[head], axis, [(g * heads - 1, g * heads + head) for g...  2.63 us
  transfers between devices with their start and end apart: 18, of which 11 were waited for; matrix products, arithmetic and copies ran while one was open for 0% of the time, Pallas kernels for 12%

profile of v6, /device:TPU:0, one launch (start us, length us, event | category | flops | bytes accessed | tf_op | source)
XLA Modules:
  0.0 62.0 jit_solution(4691109693878926749)
XLA Ops:
  0.7 1.4 %pack.1 = (bf16[1040,128]{1,0:T(8,128)(2,1)S(1)}, bf16[1040,128]{1,0:T(8,128)(2,1)S(1)}, bf16[1040,128]{1,0:T(8,128)(2,1)S(1)}, bf16[1040,128]{1,0:T(8,128)(2,1)...) custom-call(bf16[256,512]{1,0:T(8,128)(2,1)} %bitcast.20, ...), custom_call_target="tpu_custom_call" | custom-call | flops 2000000000 | bytes 6000000 | tf_op jit(solution)/shard_map/pack/pallas_call | solution.py:142
  2.1 3.0 %collective-permute-start = (bf16[1040,128]{1,0:T(8,128)(2,1)S(1)}, bf16[1040,128]{1,0:T(8,128)(2,1)S(1)}, u32[]{:S(2)}, u32[]{:S(2)}) collective-permute-start(bf16[1040,128]{1,0:T(8,128)(2,1)S(1)} %get-tuple-element.65), channel_id=1, source_target_pairs={{0,1},{1,0},{2,3},{3,2},{4,5},{5,4},{6,7},{7,6},{8,9},{9,8},{10,11... | collective-permute-start | bytes 798728 | tf_op jit(solution)/shard_map/ppermute | solution.py:689
  5.1 1.6 %collective-permute-start.1 = (bf16[1040,128]{1,0:T(8,128)(2,1)S(1)}, bf16[1040,128]{1,0:T(8,128)(2,1)S(1)}, u32[]{:S(2)}, u32[]{:S(2)}) collective-permute-start(bf16[1040,128]{1,0:T(8,128)(2,1)S(1)} %get-tuple-element.66), channel_id=1, source_target_pairs={{0,2},{1,3},{2,0},{3,1},{4,6},{5,7},{6,4},{7,5},{8,10},{9,11},{10,... | collective-permute-start | bytes 798728 | tf_op jit(solution)/shard_map/ppermute | solution.py:689
  6.7 0.7 %collective-permute-start.3 = (bf16[3,8,128]{2,1,0:T(8,128)(2,1)S(1)}, bf16[3,8,128]{2,1,0:T(8,128)(2,1)S(1)}, u32[]{:S(2)}, u32[]{:S(2)}) collective-permute-start(bf16[3,8,128]{2,1,0:T(8,128)(2,1)S(1)} %get-tuple-element.68), channel_id=1, source_target_pairs={{3,4},{11,12},{19,20},{27,28}} | collective-permute-start | bytes 18440 | tf_op jit(solution)/shard_map/ppermute | solution.py:742
  7.3 0.7 %collective-permute-start.4 = (bf16[3,8,128]{2,1,0:T(8,128)(2,1)S(1)}, bf16[3,8,128]{2,1,0:T(8,128)(2,1)S(1)}, u32[]{:S(2)}, u32[]{:S(2)}) collective-permute-start(bf16[3,8,128]{2,1,0:T(8,128)(2,1)S(1)} %get-tuple-element.69), channel_id=1, source_target_pairs={{3,5},{11,13},{19,21},{27,29}} | collective-permute-start | bytes 18440 | tf_op jit(solution)/shard_map/ppermute | solution.py:742
  8.0 0.7 %collective-permute-start.5 = (bf16[3,8,128]{2,1,0:T(8,128)(2,1)S(1)}, bf16[3,8,128]{2,1,0:T(8,128)(2,1)S(1)}, u32[]{:S(2)}, u32[]{:S(2)}) collective-permute-start(bf16[3,8,128]{2,1,0:T(8,128)(2,1)S(1)} %get-tuple-element.70), channel_id=1, source_target_pairs={{3,6},{11,14},{19,22},{27,30}} | collective-permute-start | bytes 18440 | tf_op jit(solution)/shard_map/ppermute | solution.py:742
  8.7 0.7 %collective-permute-start.6 = (bf16[3,8,128]{2,1,0:T(8,128)(2,1)S(1)}, bf16[3,8,128]{2,1,0:T(8,128)(2,1)S(1)}, u32[]{:S(2)}, u32[]{:S(2)}) collective-permute-start(bf16[3,8,128]{2,1,0:T(8,128)(2,1)S(1)} %get-tuple-element.71), channel_id=1, source_target_pairs={{3,7},{11,15},{19,23},{27,31}} | collective-permute-start | bytes 18440 | tf_op jit(solution)/shard_map/ppermute | solution.py:742
  9.4 2.1 %collective-permute-done.refs_1_ = bf16[1040,128]{1,0:T(8,128)(2,1)S(1)} collective-permute-done((bf16[1040,128]{1,0:T(8,128)(2,1)S(1)}, bf16[1040,128]{1,0:T(8,128)(2,1)S(1)}, u32[]{:S(2)}, u32[]{:S(2)}) %collective-permute-start) | collective-permute-done | bytes 266272 | tf_op jit(solution)/shard_map/ppermute | solution.py:689
  11.5 2.9 %collective-permute-done.1.refs_2_ = bf16[1040,128]{1,0:T(8,128)(2,1)S(1)} collective-permute-done((bf16[1040,128]{1,0:T(8,128)(2,1)S(1)}, bf16[1040,128]{1,0:T(8,128)(2,1)S(1)}, u32[]{:S(2)}, u32[]{:S(2)}) %collective-permute-start.1) | collective-permute-done | bytes 266272 | tf_op jit(solution)/shard_map/ppermute | solution.py:689
  14.4 4.0 %collective-permute-done.2.refs_3_ = bf16[1040,128]{1,0:T(8,128)(2,1)S(1)} collective-permute-done((bf16[1040,128]{1,0:T(8,128)(2,1)S(1)}, bf16[1040,128]{1,0:T(8,128)(2,1)S(1)}, u32[]{:S(2)}, u32[]{:S(2)}) %collective-permute-start.2) | collective-permute-done | bytes 266272 | tf_op jit(solution)/shard_map/ppermute | solution.py:689
  18.5 7.8 %local_part.1 = (bf16[4,1024,128]{2,1,0:T(8,128)(2,1)S(1)}, f32[2,8,128]{2,1,0:T(8,128)S(1)}, f32[1024,128]{1,0:T(8,128)S(1)}, f32[1024,128]{1,0:T(8,128)S(1)}, ...) custom-call(bf16[1040,128]{1,0:T(8,128)(2,1)S(1)} %get-tuple-element, ...), custom_call_target="tpu_custom_call" | custom-call | flops 10000000000 | bytes 30000000 | tf_op jit(solution)/shard_map/local_part/pallas_call | solution.py:361
  26.3 2.8 %collective-permute-start.7 = (f32[128,128]{1,0:T(8,128)S(1)}, f32[128,128]{1,0:T(8,128)S(1)}, u32[]{:S(2)}, u32[]{:S(2)}) collective-permute-start(f32[128,128]{1,0:T(8,128)S(1)} %get-tuple-element.89), channel_id=1, source_target_pairs={{0,4},{1,5},{2,6},{3,7},{4,0},{5,1},{6,2},{7,3},{8,12},{9,13},{10,... | collective-permute-start | bytes 196616 | tf_op jit(solution)/shard_map/ppermute | solution.py:753
  29.0 1.4 %chains_part.1 = (f32[8,128,128]{2,1,0:T(8,128)S(1)}, f32[8,128,128]{2,1,0:T(8,128)S(1)}, f32[8,128,128]{2,1,0:T(8,128)S(1)}, f32[8,128,128]{2,1,0:T(8,128)S(1)}) custom-call(f32[8,128,128]{2,1,0:T(8,128)S(1)} %get-tuple-element.82.mt_in, f32[8,128,128]{2,1,0:T(8,128)S(1)} %get-tuple-element.83.bt_in, f32[8,128,128]{2,1,0:T(8,128)S(1)} %get-tuple-element.84.ct_in), custom_call_target="tpu_custom_call" | custom-call | flops 2000000000 | bytes 6000000 | tf_op jit(solution)/shard_map/chains_part/pallas_call | solution.py:471
  30.4 1.0 %collective-permute-done.7.refs_21_.refs_22_ = f32[128,128]{1,0:T(8,128)S(1)} collective-permute-done((f32[128,128]{1,0:T(8,128)S(1)}, f32[128,128]{1,0:T(8,128)S(1)}, u32[]{:S(2)}, u32[]{:S(2)}) %collective-permute-start.7) | collective-permute-done | bytes 65568 | tf_op jit(solution)/shard_map/ppermute | solution.py:753
  31.4 1.2 %state_part.1 = (f32[9,128,128]{2,1,0:T(8,128)S(1)}, f32[9,128,128]{2,1,0:T(8,128)S(1)}, f32[3,128,128]{2,1,0:T(8,128)S(1)}, f32[2,1,128]{2,1,0:T(1,128)S(1)}, f...) custom-call(bf16[4,1024,128]{2,1,0:T(8,128)(2,1)S(1)} %get-tuple-element.72.refs_0_, ...), custom_call_target="tpu_custom_call" | custom-call | flops 7000000000 | bytes 21000000 | tf_op jit(solution)/shard_map/state_part/pallas_call | solution.py:543
  32.7 1.5 %collective-permute-start.9 = (f32[3,8,128]{2,1,0:T(8,128)S(1)}, f32[3,8,128]{2,1,0:T(8,128)S(1)}, u32[]{:S(2)}, u32[]{:S(2)}) collective-permute-start(f32[3,8,128]{2,1,0:T(8,128)S(1)} %get-tuple-element.96), channel_id=1, source_target_pairs={{4,0},{5,1},{6,2},{7,3},{12,8},{13,9},{14,10},{15,11},{20,16},{21,... | collective-permute-start | bytes 36872 | tf_op jit(solution)/shard_map/ppermute | solution.py:702
  34.2 4.6 %final_part.1 = (f32[3,896,128]{2,1,0:T(8,128)S(1)}, f32[2,7,128]{2,1,0:T(8,128)S(1)}, f32[16,512]{1,0:T(8,128)S(1)}, bf16[896,128]{1,0:T(8,128)(2,1)S(1)}) custom-call(bf16[4,1024,128]{2,1,0:T(8,128)(2,1)S(1)} %get-tuple-element.72.refs_0_, f32[2,8,128]{2,1,0:T(8,128)S(1)} %get-tuple-element.73.refs_5_.refs_1_, ...), custom_call_target="tpu_custom_call" | custom-call | flops 8000000000 | bytes 24000000 | tf_op jit(solution)/shard_map/final_part/pallas_call | solution.py:605
  38.8 1.7 %collective-permute-start.8 = (f32[16,512]{1,0:T(8,128)S(1)}, f32[16,512]{1,0:T(8,128)S(1)}, u32[]{:S(2)}, u32[]{:S(2)}) collective-permute-start(f32[16,512]{1,0:T(8,128)S(1)} %get-tuple-element.93), channel_id=1, source_target_pairs={{0,1},{1,0},{2,3},{3,2},{4,5},{5,4},{6,7},{7,6},{8,9},{9,8},{10,11... | collective-permute-start | bytes 98312 | tf_op jit(solution)/shard_map/ppermute | solution.py:721
  40.5 0.6 input_part.1
  41.1 1.9 %collective-permute-done.8 = f32[16,512]{1,0:T(8,128)S(1)} collective-permute-done((f32[16,512]{1,0:T(8,128)S(1)}, f32[16,512]{1,0:T(8,128)S(1)}, u32[]{:S(2)}, u32[]{:S(2)}) %collective-permute-start.8) | collective-permute-done | bytes 32800 | tf_op jit(solution)/shard_map/ppermute | solution.py:721
  43.1 1.7 %collective-permute-start.12 = (bf16[1040,128]{1,0:T(8,128)(2,1)S(1)}, bf16[1040,128]{1,0:T(8,128)(2,1)S(1)}, u32[]{:S(2)}, u32[]{:S(2)}) collective-permute-start(bf16[1040,128]{1,0:T(8,128)(2,1)S(1)} %get-tuple-element.107), channel_id=1, source_target_pairs={{0,1},{1,0},{2,3},{3,2},{4,5},{5,4},{6,7},{7,6},{8,9},{9,8},{10,11... | collective-permute-start | bytes 798728 | tf_op jit(solution)/shard_map/ppermute | solution.py:689
  44.7 1.6 %collective-permute-start.13 = (bf16[1040,128]{1,0:T(8,128)(2,1)S(1)}, bf16[1040,128]{1,0:T(8,128)(2,1)S(1)}, u32[]{:S(2)}, u32[]{:S(2)}) collective-permute-start(bf16[1040,128]{1,0:T(8,128)(2,1)S(1)} %get-tuple-element.108), channel_id=1, source_target_pairs={{0,2},{1,3},{2,0},{3,1},{4,6},{5,7},{6,4},{7,5},{8,10},{9,11},{10,... | collective-permute-start | bytes 798728 | tf_op jit(solution)/shard_map/ppermute | solution.py:689
  46.3 0.2 collective-permute-start.14
  46.5 1.2 %collective-permute-done.10 = f32[16,512]{1,0:T(8,128)S(1)} collective-permute-done((f32[16,512]{1,0:T(8,128)S(1)}, f32[16,512]{1,0:T(8,128)S(1)}, u32[]{:S(2)}, u32[]{:S(2)}) %collective-permute-start.10) | collective-permute-done | bytes 32800 | tf_op jit(solution)/shard_map/ppermute | solution.py:721
  47.8 1.7 %collective-permute-start.11 = (f32[16,512]{1,0:T(8,128)S(1)}, f32[16,512]{1,0:T(8,128)S(1)}, u32[]{:S(2)}, u32[]{:S(2)}) collective-permute-start(f32[16,512]{1,0:T(8,128)S(1)} %add.19), channel_id=1, source_target_pairs={{0,16},{1,17},{2,18},{3,19},{4,20},{5,21},{6,22},{7,23},{8,24},{9,... | collective-permute-start | bytes 98312 | tf_op jit(solution)/shard_map/ppermute | solution.py:721
  49.5 2.2 %collective-permute-done.11 = f32[16,512]{1,0:T(8,128)S(1)} collective-permute-done((f32[16,512]{1,0:T(8,128)S(1)}, f32[16,512]{1,0:T(8,128)S(1)}, u32[]{:S(2)}, u32[]{:S(2)}) %collective-permute-start.11) | collective-permute-done | bytes 32800 | tf_op jit(solution)/shard_map/ppermute | solution.py:721
  51.9 4.7 %collective-permute-start.17 = (f32[16,512]{1,0:T(8,128)S(1)}, f32[16,512]{1,0:T(8,128)S(1)}, u32[]{:S(2)}, u32[]{:S(2)}) collective-permute-start(f32[16,512]{1,0:T(8,128)S(1)} %add.20), channel_id=1, source_target_pairs={{0,6},{1,7},{2,4},{3,5},{4,2},{5,3},{6,0},{7,1},{8,14},{9,15},{10,... | collective-permute-start | bytes 98312 | tf_op jit(solution)/shard_map/ppermute | solution.py:721
  56.6 0.6 %collective-permute-start.15 = (f32[16,512]{1,0:T(8,128)S(1)}, f32[16,512]{1,0:T(8,128)S(1)}, u32[]{:S(2)}, u32[]{:S(2)}) collective-permute-start(f32[16,512]{1,0:T(8,128)S(1)} %add.20), channel_id=1, source_target_pairs={{0,2},{1,3},{2,0},{3,1},{4,6},{5,7},{6,4},{7,5},{8,10},{9,11},{10,... | collective-permute-start | bytes 98312 | tf_op jit(solution)/shard_map/ppermute | solution.py:721
  57.2 1.0 %unpack.1 = (bf16[256,512]{1,0:T(8,128)(2,1)}, bf16[256,512]{1,0:T(8,128)(2,1)}, bf16[256,512]{1,0:T(8,128)(2,1)}, bf16[256,512]{1,0:T(8,128)(2,1)}, f32[4,256]{1,0:T(4,128)}, /*index=5*/f32[4,256]{1,0:T(4,128)}) custom-call(bf16[1040,128]{1,0:T(8,128)(2,1)S(1)} %get-tuple-element.105.refs_0_, bf16[1040,128]{1,0:T(8,128)(2,1)S(1)} %collective-permute-done.12.refs_1_, ...), custom_call_target="tpu_custom_call" | custom-call | flops 2000000000 | bytes 6000000 | tf_op jit(solution)/shard_map/unpack/pallas_call | solution.py:184
  58.2 0.4 collective-permute-done.17
  58.7 2.7 %collective-permute-done.16 = f32[16,512]{1,0:T(8,128)S(1)} collective-permute-done((f32[16,512]{1,0:T(8,128)S(1)}, f32[16,512]{1,0:T(8,128)S(1)}, u32[]{:S(2)}, u32[]{:S(2)}) %collective-permute-start.16) | collective-permute-done | bytes 32800 | tf_op jit(solution)/shard_map/ppermute | solution.py:721
  61.4 0.6 fusion
  (22 shorter events, 0.3 us)
Async XLA Ops:
  0.6 17.8 %copy-start = (f32[4,512]{1,0:T(4,128)S(1)}, f32[4,512]{1,0:T(4,128)}, u32[]{:S(2)}) copy-start(f32[4,512]{1,0:T(4,128)} %refs_5_.1) | copy-start | bytes 24580
  0.7 17.8 %copy-start.1 = (f32[4,512]{1,0:T(4,128)S(1)}, f32[4,512]{1,0:T(4,128)}, u32[]{:S(2)}) copy-start(f32[4,512]{1,0:T(4,128)} %refs_6_.1) | copy-start | bytes 24580
  0.7 17.8 %copy-start.2 = (f32[4,512]{1,0:T(4,128)S(1)}, f32[4,512]{1,0:T(4,128)}, u32[]{:S(2)}) copy-start(f32[4,512]{1,0:T(4,128)} %refs_7_.1) | copy-start | bytes 24580
  2.1 9.4 %collective-permute-start = (bf16[1040,128]{1,0:T(8,128)(2,1)S(1)}, bf16[1040,128]{1,0:T(8,128)(2,1)S(1)}, u32[]{:S(2)}, u32[]{:S(2)}) collective-permute-start(bf16[1040,128]{1,0:T(8,128)(2,1)S(1)} %get-tuple-element.65), channel_id=1, source_target_pairs={{0,1},{1,0},{2,3},{3,2},{4,5},{5,4},{6,7},{7,6},{8,9},{9,8},{10,11... | collective-permute-start | bytes 798728 | tf_op jit(solution)/shard_map/ppermute | solution.py:689
  5.1 9.3 %collective-permute-start.1 = (bf16[1040,128]{1,0:T(8,128)(2,1)S(1)}, bf16[1040,128]{1,0:T(8,128)(2,1)S(1)}, u32[]{:S(2)}, u32[]{:S(2)}) collective-permute-start(bf16[1040,128]{1,0:T(8,128)(2,1)S(1)} %get-tuple-element.66), channel_id=1, source_target_pairs={{0,2},{1,3},{2,0},{3,1},{4,6},{5,7},{6,4},{7,5},{8,10},{9,11},{10,... | collective-permute-start | bytes 798728 | tf_op jit(solution)/shard_map/ppermute | solution.py:689
  6.7 11.8 %collective-permute-start.2 = (bf16[1040,128]{1,0:T(8,128)(2,1)S(1)}, bf16[1040,128]{1,0:T(8,128)(2,1)S(1)}, u32[]{:S(2)}, u32[]{:S(2)}) collective-permute-start(bf16[1040,128]{1,0:T(8,128)(2,1)S(1)} %get-tuple-element.67), channel_id=1, source_target_pairs={{0,3},{1,2},{2,1},{3,0},{4,7},{5,6},{6,5},{7,4},{8,11},{9,10},{10,... | collective-permute-start | bytes 798728 | tf_op jit(solution)/shard_map/ppermute | solution.py:689
  6.7 1.3 %collective-permute-start.3 = (bf16[3,8,128]{2,1,0:T(8,128)(2,1)S(1)}, bf16[3,8,128]{2,1,0:T(8,128)(2,1)S(1)}, u32[]{:S(2)}, u32[]{:S(2)}) collective-permute-start(bf16[3,8,128]{2,1,0:T(8,128)(2,1)S(1)} %get-tuple-element.68), channel_id=1, source_target_pairs={{3,4},{11,12},{19,20},{27,28}} | collective-permute-start | bytes 18440 | tf_op jit(solution)/shard_map/ppermute | solution.py:742
  7.3 1.4 %collective-permute-start.4 = (bf16[3,8,128]{2,1,0:T(8,128)(2,1)S(1)}, bf16[3,8,128]{2,1,0:T(8,128)(2,1)S(1)}, u32[]{:S(2)}, u32[]{:S(2)}) collective-permute-start(bf16[3,8,128]{2,1,0:T(8,128)(2,1)S(1)} %get-tuple-element.69), channel_id=1, source_target_pairs={{3,5},{11,13},{19,21},{27,29}} | collective-permute-start | bytes 18440 | tf_op jit(solution)/shard_map/ppermute | solution.py:742
  8.0 1.4 %collective-permute-start.5 = (bf16[3,8,128]{2,1,0:T(8,128)(2,1)S(1)}, bf16[3,8,128]{2,1,0:T(8,128)(2,1)S(1)}, u32[]{:S(2)}, u32[]{:S(2)}) collective-permute-start(bf16[3,8,128]{2,1,0:T(8,128)(2,1)S(1)} %get-tuple-element.70), channel_id=1, source_target_pairs={{3,6},{11,14},{19,22},{27,30}} | collective-permute-start | bytes 18440 | tf_op jit(solution)/shard_map/ppermute | solution.py:742
  8.7 0.7 %collective-permute-start.6 = (bf16[3,8,128]{2,1,0:T(8,128)(2,1)S(1)}, bf16[3,8,128]{2,1,0:T(8,128)(2,1)S(1)}, u32[]{:S(2)}, u32[]{:S(2)}) collective-permute-start(bf16[3,8,128]{2,1,0:T(8,128)(2,1)S(1)} %get-tuple-element.71), channel_id=1, source_target_pairs={{3,7},{11,15},{19,23},{27,31}} | collective-permute-start | bytes 18440 | tf_op jit(solution)/shard_map/ppermute | solution.py:742
  26.3 5.2 %collective-permute-start.7 = (f32[128,128]{1,0:T(8,128)S(1)}, f32[128,128]{1,0:T(8,128)S(1)}, u32[]{:S(2)}, u32[]{:S(2)}) collective-permute-start(f32[128,128]{1,0:T(8,128)S(1)} %get-tuple-element.89), channel_id=1, source_target_pairs={{0,4},{1,5},{2,6},{3,7},{4,0},{5,1},{6,2},{7,3},{8,12},{9,13},{10,... | collective-permute-start | bytes 196616 | tf_op jit(solution)/shard_map/ppermute | solution.py:753
  32.7 7.9 %collective-permute-start.9 = (f32[3,8,128]{2,1,0:T(8,128)S(1)}, f32[3,8,128]{2,1,0:T(8,128)S(1)}, u32[]{:S(2)}, u32[]{:S(2)}) collective-permute-start(f32[3,8,128]{2,1,0:T(8,128)S(1)} %get-tuple-element.96), channel_id=1, source_target_pairs={{4,0},{5,1},{6,2},{7,3},{12,8},{13,9},{14,10},{15,11},{20,16},{21,... | collective-permute-start | bytes 36872 | tf_op jit(solution)/shard_map/ppermute | solution.py:702
  38.8 4.2 %collective-permute-start.8 = (f32[16,512]{1,0:T(8,128)S(1)}, f32[16,512]{1,0:T(8,128)S(1)}, u32[]{:S(2)}, u32[]{:S(2)}) collective-permute-start(f32[16,512]{1,0:T(8,128)S(1)} %get-tuple-element.93), channel_id=1, source_target_pairs={{0,1},{1,0},{2,3},{3,2},{4,5},{5,4},{6,7},{7,6},{8,9},{9,8},{10,11... | collective-permute-start | bytes 98312 | tf_op jit(solution)/shard_map/ppermute | solution.py:721
  43.1 8.7 %collective-permute-start.12 = (bf16[1040,128]{1,0:T(8,128)(2,1)S(1)}, bf16[1040,128]{1,0:T(8,128)(2,1)S(1)}, u32[]{:S(2)}, u32[]{:S(2)}) collective-permute-start(bf16[1040,128]{1,0:T(8,128)(2,1)S(1)} %get-tuple-element.107), channel_id=1, source_target_pairs={{0,1},{1,0},{2,3},{3,2},{4,5},{5,4},{6,7},{7,6},{8,9},{9,8},{10,11... | collective-permute-start | bytes 798728 | tf_op jit(solution)/shard_map/ppermute | solution.py:689
  44.7 7.1 %collective-permute-start.13 = (bf16[1040,128]{1,0:T(8,128)(2,1)S(1)}, bf16[1040,128]{1,0:T(8,128)(2,1)S(1)}, u32[]{:S(2)}, u32[]{:S(2)}) collective-permute-start(bf16[1040,128]{1,0:T(8,128)(2,1)S(1)} %get-tuple-element.108), channel_id=1, source_target_pairs={{0,2},{1,3},{2,0},{3,1},{4,6},{5,7},{6,4},{7,5},{8,10},{9,11},{10,... | collective-permute-start | bytes 798728 | tf_op jit(solution)/shard_map/ppermute | solution.py:689
  46.3 10.9 %collective-permute-start.14 = (bf16[1040,128]{1,0:T(8,128)(2,1)S(1)}, bf16[1040,128]{1,0:T(8,128)(2,1)S(1)}, u32[]{:S(2)}, u32[]{:S(2)}) collective-permute-start(bf16[1040,128]{1,0:T(8,128)(2,1)S(1)} %get-tuple-element.111), channel_id=1, source_target_pairs={{0,3},{1,2},{2,1},{3,0},{4,7},{5,6},{6,5},{7,4},{8,11},{9,10},{10,... | collective-permute-start | bytes 798728 | tf_op jit(solution)/shard_map/ppermute | solution.py:689
  46.5 1.2 %collective-permute-start.10 = (f32[16,512]{1,0:T(8,128)S(1)}, f32[16,512]{1,0:T(8,128)S(1)}, u32[]{:S(2)}, u32[]{:S(2)}) collective-permute-start(f32[16,512]{1,0:T(8,128)S(1)} %add.18), channel_id=1, source_target_pairs={{0,8},{1,9},{2,10},{3,11},{4,12},{5,13},{6,14},{7,15},{8,0},{9,1},... | collective-permute-start | bytes 98312 | tf_op jit(solution)/shard_map/ppermute | solution.py:721
  47.8 3.9 %collective-permute-start.11 = (f32[16,512]{1,0:T(8,128)S(1)}, f32[16,512]{1,0:T(8,128)S(1)}, u32[]{:S(2)}, u32[]{:S(2)}) collective-permute-start(f32[16,512]{1,0:T(8,128)S(1)} %add.19), channel_id=1, source_target_pairs={{0,16},{1,17},{2,18},{3,19},{4,20},{5,21},{6,22},{7,23},{8,24},{9,... | collective-permute-start | bytes 98312 | tf_op jit(solution)/shard_map/ppermute | solution.py:721
  51.9 6.8 %collective-permute-start.17 = (f32[16,512]{1,0:T(8,128)S(1)}, f32[16,512]{1,0:T(8,128)S(1)}, u32[]{:S(2)}, u32[]{:S(2)}) collective-permute-start(f32[16,512]{1,0:T(8,128)S(1)} %add.20), channel_id=1, source_target_pairs={{0,6},{1,7},{2,4},{3,5},{4,2},{5,3},{6,0},{7,1},{8,14},{9,15},{10,... | collective-permute-start | bytes 98312 | tf_op jit(solution)/shard_map/ppermute | solution.py:721
  56.6 4.8 %collective-permute-start.16 = (f32[16,512]{1,0:T(8,128)S(1)}, f32[16,512]{1,0:T(8,128)S(1)}, u32[]{:S(2)}, u32[]{:S(2)}) collective-permute-start(f32[16,512]{1,0:T(8,128)S(1)} %add.20), channel_id=1, source_target_pairs={{0,4},{1,5},{2,6},{3,7},{4,0},{5,1},{6,2},{7,3},{8,12},{9,13},{10,... | collective-permute-start | bytes 98312 | tf_op jit(solution)/shard_map/ppermute | solution.py:721
  56.6 4.8 %collective-permute-start.15 = (f32[16,512]{1,0:T(8,128)S(1)}, f32[16,512]{1,0:T(8,128)S(1)}, u32[]{:S(2)}, u32[]{:S(2)}) collective-permute-start(f32[16,512]{1,0:T(8,128)S(1)} %add.20), channel_id=1, source_target_pairs={{0,2},{1,3},{2,0},{3,1},{4,6},{5,7},{6,4},{7,5},{8,10},{9,11},{10,... | collective-permute-start | bytes 98312 | tf_op jit(solution)/shard_map/ppermute | solution.py:721

commit v7 on v6

--- a/solution.py
+++ b/solution.py
@@ -208,10 +208,13 @@
 
 
 def activated(c_value, unit):
-    y = c_value * jax.nn.sigmoid(c_value)
+    gate = jax.nn.sigmoid(c_value)
+    y = c_value * gate
+    factor = gate * (1.0 + c_value * (1.0 - gate))
     if unit:
-        y = y * lax.rsqrt(jnp.sum(y * y, axis=1, keepdims=True) + 1e-06)
-    return y
+        scale = lax.rsqrt(jnp.sum(y * y, axis=1, keepdims=True) + 1e-06)
+        return y * scale, factor * scale
+    return y, factor
 
 
 def ratio_forms(g_column, g_row, rows, columns):
@@ -224,8 +227,8 @@
 def local_kernel(heads, axis, *refs):
     received, tails, tap_refs, refs = refs[:heads], refs[heads : 2 * heads], refs[2 * heads : 2 * heads + 3], refs[2 * heads + 3 :]
     (raw, rate_out, k_out, q_out, v_out, p_out, u_out, w_out, x_out, y_out) = refs[:10]
-    (mt_out, bt_out, ct_out, state_out, back_out) = refs[10:15]
-    inverse, padded, lower_high, lower_low = refs[15:]
+    (mt_out, bt_out, ct_out, gates, state_out, back_out) = refs[10:16]
+    inverse, padded, lower_high, lower_low = refs[16:]
     me, group = place_in_group(axis, heads)
     length, width = k_out.shape
     frames = length // heads
@@ -262,7 +265,7 @@
         at = pl.ds(c * CHUNK, CHUNK)
         g_column, g_row, g_last = decay_forms(rate_out[0, c : c + 1, :], rows, columns)
         beta_column = as_column(rate_out[1, c : c + 1, :], rows, columns)
-        keys = activated(convolve(padded, 0, c * CHUNK, taps[0]), True)
+        keys, gates[0, at, :] = activated(convolve(padded, 0, c * CHUNK, taps[0]), True)
         k_out[at, :] = keys
         k_pair = split(keys)
         below = columns < rows
@@ -293,8 +296,8 @@
         ratio, ratio_t = ratio_forms(g_column, g_row, rows, columns)
         start_column, start_row = jnp.exp(g_column), jnp.exp(g_row)
         tail_column, tail_row = jnp.exp(g_last - g_column), jnp.exp(g_last - g_row)
-        values = activated(convolve(padded, 1, c * CHUNK, taps[1]), False)
-        queries = activated(convolve(padded, 2, c * CHUNK, taps[2]), True)
+        values, gates[1, at, :] = activated(convolve(padded, 1, c * CHUNK, taps[1]), False)
+        queries, gates[2, at, :] = activated(convolve(padded, 2, c * CHUNK, taps[2]), True)
         q_out[at, :], v_out[at, :] = queries, values
         yield True
         keys = k_out[at, :]
@@ -357,7 +360,7 @@
     square = pltpu.VMEM((chunk_count, width, width), F32)
     one = jax.ShapeDtypeStruct((width, width), F32)
     out_shape = [pltpu.VMEM((4, length, width), BF16), pltpu.VMEM((2, chunk_count, CHUNK), F32)]
-    out_shape += [tall] * 8 + [square] * 3 + [one] * 2
+    out_shape += [tall] * 8 + [square] * 3 + [pltpu.VMEM((3, length, width), F32)] + [one] * 2
     return pl.pallas_call(
         functools.partial(local_kernel, heads, axis),
         out_shape=out_shape,
@@ -381,7 +384,7 @@
     return g_column, g_row, g_last, beta_row, as_column(beta_row, rows, columns)
 
 
-def chunk_back(c, forms, given, ids, padded, taps, sums):
+def chunk_back(c, forms, given, ids, padded, gates, sums):
     g_column, g_row, g_last, beta_row, beta_column = forms
     keys, queries, values, u_value, x_value, state, back, cotangent, kept_row = given
     rows, columns = ids
@@ -419,15 +422,9 @@
     for place, (grad, unit) in enumerate(((d_keys, keys), (d_values, None), (d_queries, queries))):
         at = c * CHUNK + 5
         shifted = [padded[place, at + i : at + i + CHUNK, :] for i in range(4)]
-        c_value = taps[place][0:1] * shifted[0]
-        for offset in range(1, 4):
-            c_value = c_value + taps[place][offset : offset + 1] * shifted[offset]
-        gate = jax.nn.sigmoid(c_value)
         if unit is not None:
-            y = c_value * gate
-            scale = lax.rsqrt(jnp.sum(y * y, axis=1, keepdims=True) + 1e-06)
-            grad = scale * (grad - unit * jnp.sum(unit * grad, axis=1, keepdims=True))
-        grad = grad * (gate * (1.0 + c_value * (1.0 - gate)))
+            grad = grad - unit * jnp.sum(unit * grad, axis=1, keepdims=True)
+        grad = grad * gates[place, c * CHUNK : (c + 1) * CHUNK, :]
         made.append(grad)
         yield True
         for offset in range(4):
@@ -482,7 +479,8 @@
 def state_kernel(heads, axis, *refs):
     raw, tails, refs = refs[0], refs[1 : 1 + heads], refs[1 + heads :]
     (rate, q_in, k_in, v_in, p_in, u_in, w_in, x_in, y_in), refs = refs[:9], refs[9:]
-    tap_refs, (ahead, ahead_add, behind, behind_add, state_in, back_in), refs = refs[:3], refs[3:9], refs[9:]
+    gates, refs = refs[0], refs[1:]
+    (ahead, ahead_add, behind, behind_add, state_in, back_in), refs = refs[:6], refs[6:]
     states, backs, conv_out, rate_grad, tap_out, rim_out, mixed_out, padded = refs
     me, group = place_in_group(axis, heads)
     length, width = q_in.shape
@@ -503,7 +501,6 @@
     for place in range(3):
         padded[place, 0:8, :] = tail_of(tails, place)
         padded[place, 8:, :] = raw[place, 0:CHUNK, :].astype(F32)
-    taps = [ref[:, aligned(me, width)] for ref in tap_refs]
     sums = [[jnp.zeros((8, width), F32) for _ in range(4)] for _ in range(3)]
     at = pl.ds(0, CHUNK)
     forms = chunk_forms(rate, 0, rows, columns)
@@ -516,7 +513,7 @@
     given = (k_in[at, :], q_in[at, :], v_in[at, :], u_value, x_value)
     given += (states[0], backs[1], raw[3, at, :], kept_row)
     made, decay_row, beta_row = whole(
-        chunk_back(0, forms, given, (rows, columns), padded, taps, sums)
+        chunk_back(0, forms, given, (rows, columns), padded, gates, sums)
     )
     rate_grad[0], rate_grad[1] = decay_row, beta_row
     for place in range(3):
@@ -556,13 +553,12 @@
 
 def final_kernel(heads, axis, *refs):
     raw, rate, q_in, k_in, v_in, p_in, u_in, w_in, x_in, y_in, states, backs, tap_before = refs[:13]
-    tap_refs, (conv_out, rate_grad, tap_out, mixed_out, padded) = refs[13:16], refs[16:]
+    (gates,), (conv_out, rate_grad, tap_out, mixed_out, padded) = refs[13:14], refs[14:]
     me, _ = place_in_group(axis, heads)
     length, width = q_in.shape
     rows, columns = grid_ids()
     for place in range(3):
         padded[place, CHUNK - 8 :, :] = raw[place, CHUNK - 16 :, :].astype(F32)
-    taps = [ref[:, aligned(me, width)] for ref in tap_refs]
     sums = [[tap_before[4 * place + offset] for offset in range(4)] for place in range(3)]
     def chunk(c):
         at = pl.ds(c * CHUNK, CHUNK)
@@ -577,7 +573,7 @@
         given = (k_in[at, :], q_in[at, :], v_in[at, :], u_value, x_value, *around)
         given += (raw[3, at, :], kept_row)
         made, decay_row, beta_row = yield from chunk_back(
-            c, forms, given, (rows, columns), padded, taps, sums
+            c, forms, given, (rows, columns), padded, gates, sums
         )
         rate_grad[0, c - 1 : c, :] = decay_row
         rate_grad[1, c - 1 : c, :] = beta_row
@@ -747,7 +743,7 @@
     ]
     tap_args = (k_taps, v_taps, q_taps)
     parts = local_part(heads, axis, q.shape[0], blocks, tails, tap_args)
-    raw, rate, keys, queries, values, p, u, w, x, y, mt, bt, ct, state, back = parts
+    raw, rate, keys, queries, values, p, u, w, x, y, mt, bt, ct, gates, state, back = parts
     chains = chains_part(mt, bt, ct)
     if groups == 2:
         arriving = returning = lax.ppermute(
@@ -765,12 +761,12 @@
                     other = mt.shape[0] - 1 - c
                     state = jnp.dot(mt[c], state, precision=exact) + bt[c]
                     back = jnp.dot(mt[other].T, back, precision=exact) + ct[other]
-    shared = (raw, *tails, rate, queries, keys, values, p, u, w, x, y, *tap_args)
+    shared = (raw, *tails, rate, queries, keys, values, p, u, w, x, y, gates)
     states, backs, conv, rate_grad, taps, rim, mixed = state_part(
         heads, axis, shared, (*chains, on_chip(arriving), on_chip(returning))
     )
     rim = along(rim, axis, -heads)
-    args = (raw, rate, queries, keys, values, p, u, w, x, y, states, backs, taps, *tap_args)
+    args = (raw, rate, queries, keys, values, p, u, w, x, y, states, backs, taps, gates)
     more_conv, more_rate, taps, more_mixed = final_part(heads, axis, args)
     axes = ("dp", axis)
     rounds = sum_rounds(axes)

time: 62.2 us -> 61.3 us (0.986)
  Pallas kernels: 18.1 us -> 17.3 us
    pallas_call x1, Pallas kernels: 4.63 us -> 3.58 us  [final_part(): pl.pallas_call(functools.partial(final_kernel, heads, axis), out_shape=ou...]
  transfers between devices with their start and end apart: 18 -> 18, of which waited for: 11 -> 10; matrix products, arithmetic and copies ran while one was open for 0% -> 0% of each run, Pallas kernels for 12% -> 11%
where the time goes in v7:
time: 61.3 us; the launch traced here: 61.1 us
  starting transfers between devices  23.8 us (39%)
  waiting for transfers between devices  18.6 us (30%)
  Pallas kernels  17.3 us (28%)
  between operations  0.79 us (1%)
  local copies, waits for them, and re-layouts  0.62 us (1%)
    ppermute x6, waiting for transfers between devices, trade_one(): return lax.ppermute(value, axis, pairs)  9.2 us
    ppermute x6, starting transfers between devices, swapped(): return lax.ppermute(value, axes, [(d, d ^ mask) for d in range(count)])  8.84 us
    ppermute x6, waiting for transfers between devices, swapped(): return lax.ppermute(value, axes, [(d, d ^ mask) for d in range(count)])  8.43 us
    ppermute x6, starting transfers between devices, trade_one(): return lax.ppermute(value, axis, pairs)  8.06 us
    pallas_call x1, Pallas kernels, local_part(): pl.pallas_call(functools.partial(local_kernel, heads, axis), out_shape=ou...  8.04 us
    pallas_call x1, Pallas kernels, final_part(): pl.pallas_call(functools.partial(final_kernel, heads, axis), out_shape=ou...  3.58 us
    ppermute x1, starting transfers between devices, body(): lax.ppermute(state, axis, [(d, (d + heads) % count) for d in range(count)])  2.76 us
    ppermute x4, starting transfers between devices, body(): lax.ppermute(tails[head], axis, [(g * heads - 1, g * heads + head) for g...  2.63 us
  transfers between devices with their start and end apart: 18, of which 10 were waited for; matrix products, arithmetic and copies ran while one was open for 0% of the time, Pallas kernels for 11%

profile of v7, /device:TPU:0, one launch (start us, length us, event | category | flops | bytes accessed | tf_op | source)
XLA Modules:
  0.0 61.1 jit_solution(12977316513977604973)
XLA Ops:
  0.7 1.4 %pack.1 = (bf16[1040,128]{1,0:T(8,128)(2,1)S(1)}, bf16[1040,128]{1,0:T(8,128)(2,1)S(1)}, bf16[1040,128]{1,0:T(8,128)(2,1)S(1)}, bf16[1040,128]{1,0:T(8,128)(2,1)...) custom-call(bf16[256,512]{1,0:T(8,128)(2,1)} %bitcast.20, ...), custom_call_target="tpu_custom_call" | custom-call | flops 2000000000 | bytes 6000000 | tf_op jit(solution)/shard_map/pack/pallas_call | solution.py:142
  2.1 3.0 %collective-permute-start = (bf16[1040,128]{1,0:T(8,128)(2,1)S(1)}, bf16[1040,128]{1,0:T(8,128)(2,1)S(1)}, u32[]{:S(2)}, u32[]{:S(2)}) collective-permute-start(bf16[1040,128]{1,0:T(8,128)(2,1)S(1)} %get-tuple-element.66), channel_id=1, source_target_pairs={{0,1},{1,0},{2,3},{3,2},{4,5},{5,4},{6,7},{7,6},{8,9},{9,8},{10,11... | collective-permute-start | bytes 798728 | tf_op jit(solution)/shard_map/ppermute | solution.py:685
  5.1 1.6 %collective-permute-start.1 = (bf16[1040,128]{1,0:T(8,128)(2,1)S(1)}, bf16[1040,128]{1,0:T(8,128)(2,1)S(1)}, u32[]{:S(2)}, u32[]{:S(2)}) collective-permute-start(bf16[1040,128]{1,0:T(8,128)(2,1)S(1)} %get-tuple-element.67), channel_id=1, source_target_pairs={{0,2},{1,3},{2,0},{3,1},{4,6},{5,7},{6,4},{7,5},{8,10},{9,11},{10,... | collective-permute-start | bytes 798728 | tf_op jit(solution)/shard_map/ppermute | solution.py:685
  6.7 0.7 %collective-permute-start.3 = (bf16[3,8,128]{2,1,0:T(8,128)(2,1)S(1)}, bf16[3,8,128]{2,1,0:T(8,128)(2,1)S(1)}, u32[]{:S(2)}, u32[]{:S(2)}) collective-permute-start(bf16[3,8,128]{2,1,0:T(8,128)(2,1)S(1)} %get-tuple-element.69), channel_id=1, source_target_pairs={{3,4},{11,12},{19,20},{27,28}} | collective-permute-start | bytes 18440 | tf_op jit(solution)/shard_map/ppermute | solution.py:738
  7.3 0.7 %collective-permute-start.4 = (bf16[3,8,128]{2,1,0:T(8,128)(2,1)S(1)}, bf16[3,8,128]{2,1,0:T(8,128)(2,1)S(1)}, u32[]{:S(2)}, u32[]{:S(2)}) collective-permute-start(bf16[3,8,128]{2,1,0:T(8,128)(2,1)S(1)} %get-tuple-element.70), channel_id=1, source_target_pairs={{3,5},{11,13},{19,21},{27,29}} | collective-permute-start | bytes 18440 | tf_op jit(solution)/shard_map/ppermute | solution.py:738
  8.0 0.7 %collective-permute-start.5 = (bf16[3,8,128]{2,1,0:T(8,128)(2,1)S(1)}, bf16[3,8,128]{2,1,0:T(8,128)(2,1)S(1)}, u32[]{:S(2)}, u32[]{:S(2)}) collective-permute-start(bf16[3,8,128]{2,1,0:T(8,128)(2,1)S(1)} %get-tuple-element.71), channel_id=1, source_target_pairs={{3,6},{11,14},{19,22},{27,30}} | collective-permute-start | bytes 18440 | tf_op jit(solution)/shard_map/ppermute | solution.py:738
  8.7 0.7 %collective-permute-start.6 = (bf16[3,8,128]{2,1,0:T(8,128)(2,1)S(1)}, bf16[3,8,128]{2,1,0:T(8,128)(2,1)S(1)}, u32[]{:S(2)}, u32[]{:S(2)}) collective-permute-start(bf16[3,8,128]{2,1,0:T(8,128)(2,1)S(1)} %get-tuple-element.72), channel_id=1, source_target_pairs={{3,7},{11,15},{19,23},{27,31}} | collective-permute-start | bytes 18440 | tf_op jit(solution)/shard_map/ppermute | solution.py:738
  9.4 2.1 %collective-permute-done.refs_1_ = bf16[1040,128]{1,0:T(8,128)(2,1)S(1)} collective-permute-done((bf16[1040,128]{1,0:T(8,128)(2,1)S(1)}, bf16[1040,128]{1,0:T(8,128)(2,1)S(1)}, u32[]{:S(2)}, u32[]{:S(2)}) %collective-permute-start) | collective-permute-done | bytes 266272 | tf_op jit(solution)/shard_map/ppermute | solution.py:685
  11.5 2.9 %collective-permute-done.1.refs_2_ = bf16[1040,128]{1,0:T(8,128)(2,1)S(1)} collective-permute-done((bf16[1040,128]{1,0:T(8,128)(2,1)S(1)}, bf16[1040,128]{1,0:T(8,128)(2,1)S(1)}, u32[]{:S(2)}, u32[]{:S(2)}) %collective-permute-start.1) | collective-permute-done | bytes 266272 | tf_op jit(solution)/shard_map/ppermute | solution.py:685
  14.4 4.0 %collective-permute-done.2.refs_3_ = bf16[1040,128]{1,0:T(8,128)(2,1)S(1)} collective-permute-done((bf16[1040,128]{1,0:T(8,128)(2,1)S(1)}, bf16[1040,128]{1,0:T(8,128)(2,1)S(1)}, u32[]{:S(2)}, u32[]{:S(2)}) %collective-permute-start.2) | collective-permute-done | bytes 266272 | tf_op jit(solution)/shard_map/ppermute | solution.py:685
  18.5 8.0 %local_part.1 = (bf16[4,1024,128]{2,1,0:T(8,128)(2,1)S(1)}, f32[2,8,128]{2,1,0:T(8,128)S(1)}, f32[1024,128]{1,0:T(8,128)S(1)}, f32[1024,128]{1,0:T(8,128)S(1)}, ...) custom-call(bf16[1040,128]{1,0:T(8,128)(2,1)S(1)} %get-tuple-element, ...), custom_call_target="tpu_custom_call" | custom-call | flops 10000000000 | bytes 30000000 | tf_op jit(solution)/shard_map/local_part/pallas_call | solution.py:364
  26.5 2.8 %collective-permute-start.7 = (f32[128,128]{1,0:T(8,128)S(1)}, f32[128,128]{1,0:T(8,128)S(1)}, u32[]{:S(2)}, u32[]{:S(2)}) collective-permute-start(f32[128,128]{1,0:T(8,128)S(1)} %get-tuple-element.91), channel_id=1, source_target_pairs={{0,4},{1,5},{2,6},{3,7},{4,0},{5,1},{6,2},{7,3},{8,12},{9,13},{10,... | collective-permute-start | bytes 196616 | tf_op jit(solution)/shard_map/ppermute | solution.py:749
  29.3 1.4 %chains_part.1 = (f32[8,128,128]{2,1,0:T(8,128)S(1)}, f32[8,128,128]{2,1,0:T(8,128)S(1)}, f32[8,128,128]{2,1,0:T(8,128)S(1)}, f32[8,128,128]{2,1,0:T(8,128)S(1)}) custom-call(f32[8,128,128]{2,1,0:T(8,128)S(1)} %get-tuple-element.84.mt_in, f32[8,128,128]{2,1,0:T(8,128)S(1)} %get-tuple-element.85.bt_in, f32[8,128,128]{2,1,0:T(8,128)S(1)} %get-tuple-element.86.ct_in), custom_call_target="tpu_custom_call" | custom-call | flops 2000000000 | bytes 6000000 | tf_op jit(solution)/shard_map/chains_part/pallas_call | solution.py:468
  30.7 1.0 %collective-permute-done.7.refs_19_.refs_20_ = f32[128,128]{1,0:T(8,128)S(1)} collective-permute-done((f32[128,128]{1,0:T(8,128)S(1)}, f32[128,128]{1,0:T(8,128)S(1)}, u32[]{:S(2)}, u32[]{:S(2)}) %collective-permute-start.7) | collective-permute-done | bytes 65568 | tf_op jit(solution)/shard_map/ppermute | solution.py:749
  31.7 1.2 %state_part.1 = (f32[9,128,128]{2,1,0:T(8,128)S(1)}, f32[9,128,128]{2,1,0:T(8,128)S(1)}, f32[3,128,128]{2,1,0:T(8,128)S(1)}, f32[2,1,128]{2,1,0:T(1,128)S(1)}, f...) custom-call(bf16[4,1024,128]{2,1,0:T(8,128)(2,1)S(1)} %get-tuple-element.73.refs_0_, ...), custom_call_target="tpu_custom_call" | custom-call | flops 7000000000 | bytes 21000000 | tf_op jit(solution)/shard_map/state_part/pallas_call | solution.py:540
  32.9 1.5 %collective-permute-start.9 = (f32[3,8,128]{2,1,0:T(8,128)S(1)}, f32[3,8,128]{2,1,0:T(8,128)S(1)}, u32[]{:S(2)}, u32[]{:S(2)}) collective-permute-start(f32[3,8,128]{2,1,0:T(8,128)S(1)} %get-tuple-element.98), channel_id=1, source_target_pairs={{4,0},{5,1},{6,2},{7,3},{12,8},{13,9},{14,10},{15,11},{20,16},{21,... | collective-permute-start | bytes 36872 | tf_op jit(solution)/shard_map/ppermute | solution.py:698
  34.4 3.6 %final_part.1 = (f32[3,896,128]{2,1,0:T(8,128)S(1)}, f32[2,7,128]{2,1,0:T(8,128)S(1)}, f32[16,512]{1,0:T(8,128)S(1)}, bf16[896,128]{1,0:T(8,128)(2,1)S(1)}) custom-call(bf16[4,1024,128]{2,1,0:T(8,128)(2,1)S(1)} %get-tuple-element.73.refs_0_, f32[2,8,128]{2,1,0:T(8,128)S(1)} %get-tuple-element.74.refs_5_.refs_1_, ...), custom_call_target="tpu_custom_call" | custom-call | flops 8000000000 | bytes 24000000 | tf_op jit(solution)/shard_map/final_part/pallas_call | solution.py:601
  37.9 1.7 %collective-permute-start.8 = (f32[16,512]{1,0:T(8,128)S(1)}, f32[16,512]{1,0:T(8,128)S(1)}, u32[]{:S(2)}, u32[]{:S(2)}) collective-permute-start(f32[16,512]{1,0:T(8,128)S(1)} %get-tuple-element.95), channel_id=1, source_target_pairs={{0,1},{1,0},{2,3},{3,2},{4,5},{5,4},{6,7},{7,6},{8,9},{9,8},{10,11... | collective-permute-start | bytes 98312 | tf_op jit(solution)/shard_map/ppermute | solution.py:717
  39.7 0.6 input_part.1
  40.3 1.9 %collective-permute-done.8 = f32[16,512]{1,0:T(8,128)S(1)} collective-permute-done((f32[16,512]{1,0:T(8,128)S(1)}, f32[16,512]{1,0:T(8,128)S(1)}, u32[]{:S(2)}, u32[]{:S(2)}) %collective-permute-start.8) | collective-permute-done | bytes 32800 | tf_op jit(solution)/shard_map/ppermute | solution.py:717
  42.2 1.7 %collective-permute-start.12 = (bf16[1040,128]{1,0:T(8,128)(2,1)S(1)}, bf16[1040,128]{1,0:T(8,128)(2,1)S(1)}, u32[]{:S(2)}, u32[]{:S(2)}) collective-permute-start(bf16[1040,128]{1,0:T(8,128)(2,1)S(1)} %get-tuple-element.109), channel_id=1, source_target_pairs={{0,1},{1,0},{2,3},{3,2},{4,5},{5,4},{6,7},{7,6},{8,9},{9,8},{10,11... | collective-permute-start | bytes 798728 | tf_op jit(solution)/shard_map/ppermute | solution.py:685
  43.9 1.6 %collective-permute-start.13 = (bf16[1040,128]{1,0:T(8,128)(2,1)S(1)}, bf16[1040,128]{1,0:T(8,128)(2,1)S(1)}, u32[]{:S(2)}, u32[]{:S(2)}) collective-permute-start(bf16[1040,128]{1,0:T(8,128)(2,1)S(1)} %get-tuple-element.110), channel_id=1, source_target_pairs={{0,2},{1,3},{2,0},{3,1},{4,6},{5,7},{6,4},{7,5},{8,10},{9,11},{10,... | collective-permute-start | bytes 798728 | tf_op jit(solution)/shard_map/ppermute | solution.py:685
  45.5 0.2 collective-permute-start.14
  45.7 1.2 %collective-permute-done.10 = f32[16,512]{1,0:T(8,128)S(1)} collective-permute-done((f32[16,512]{1,0:T(8,128)S(1)}, f32[16,512]{1,0:T(8,128)S(1)}, u32[]{:S(2)}, u32[]{:S(2)}) %collective-permute-start.10) | collective-permute-done | bytes 32800 | tf_op jit(solution)/shard_map/ppermute | solution.py:717
  46.9 1.7 %collective-permute-start.11 = (f32[16,512]{1,0:T(8,128)S(1)}, f32[16,512]{1,0:T(8,128)S(1)}, u32[]{:S(2)}, u32[]{:S(2)}) collective-permute-start(f32[16,512]{1,0:T(8,128)S(1)} %add.19), channel_id=1, source_target_pairs={{0,16},{1,17},{2,18},{3,19},{4,20},{5,21},{6,22},{7,23},{8,24},{9,... | collective-permute-start | bytes 98312 | tf_op jit(solution)/shard_map/ppermute | solution.py:717
  48.6 2.2 %collective-permute-done.11 = f32[16,512]{1,0:T(8,128)S(1)} collective-permute-done((f32[16,512]{1,0:T(8,128)S(1)}, f32[16,512]{1,0:T(8,128)S(1)}, u32[]{:S(2)}, u32[]{:S(2)}) %collective-permute-start.11) | collective-permute-done | bytes 32800 | tf_op jit(solution)/shard_map/ppermute | solution.py:717
  50.9 4.7 %collective-permute-start.17 = (f32[16,512]{1,0:T(8,128)S(1)}, f32[16,512]{1,0:T(8,128)S(1)}, u32[]{:S(2)}, u32[]{:S(2)}) collective-permute-start(f32[16,512]{1,0:T(8,128)S(1)} %add.20), channel_id=1, source_target_pairs={{0,6},{1,7},{2,4},{3,5},{4,2},{5,3},{6,0},{7,1},{8,14},{9,15},{10,... | collective-permute-start | bytes 98312 | tf_op jit(solution)/shard_map/ppermute | solution.py:717
  55.7 0.6 %collective-permute-start.15 = (f32[16,512]{1,0:T(8,128)S(1)}, f32[16,512]{1,0:T(8,128)S(1)}, u32[]{:S(2)}, u32[]{:S(2)}) collective-permute-start(f32[16,512]{1,0:T(8,128)S(1)} %add.20), channel_id=1, source_target_pairs={{0,2},{1,3},{2,0},{3,1},{4,6},{5,7},{6,4},{7,5},{8,10},{9,11},{10,... | collective-permute-start | bytes 98312 | tf_op jit(solution)/shard_map/ppermute | solution.py:717
  56.3 1.0 %unpack.1 = (bf16[256,512]{1,0:T(8,128)(2,1)}, bf16[256,512]{1,0:T(8,128)(2,1)}, bf16[256,512]{1,0:T(8,128)(2,1)}, bf16[256,512]{1,0:T(8,128)(2,1)}, f32[4,256]{1,0:T(4,128)}, /*index=5*/f32[4,256]{1,0:T(4,128)}) custom-call(bf16[1040,128]{1,0:T(8,128)(2,1)S(1)} %get-tuple-element.107.refs_0_, bf16[1040,128]{1,0:T(8,128)(2,1)S(1)} %collective-permute-done.12.refs_1_, ...), custom_call_target="tpu_custom_call" | custom-call | flops 2000000000 | bytes 6000000 | tf_op jit(solution)/shard_map/unpack/pallas_call | solution.py:184
  57.4 0.5 collective-permute-done.17
  57.8 2.7 %collective-permute-done.16 = f32[16,512]{1,0:T(8,128)S(1)} collective-permute-done((f32[16,512]{1,0:T(8,128)S(1)}, f32[16,512]{1,0:T(8,128)S(1)}, u32[]{:S(2)}, u32[]{:S(2)}) %collective-permute-start.16) | collective-permute-done | bytes 32800 | tf_op jit(solution)/shard_map/ppermute | solution.py:717
  60.5 0.6 %fusion = (f32[4,512]{1,0:T(4,128)}, f32[4,512]{1,0:T(4,128)}, f32[4,512]{1,0:T(4,128)}) fusion(f32[16,512]{1,0:T(8,128)S(1)} %add_add_fusion), kind=kLoop, calls=%fused_computation.1 | loop fusion | bytes 49152 | tf_op jit(solution)/shard_map/slice | solution.py:804
  (22 shorter events, 0.2 us)
Async XLA Ops:
  0.6 17.8 %copy-start = (f32[4,512]{1,0:T(4,128)S(1)}, f32[4,512]{1,0:T(4,128)}, u32[]{:S(2)}) copy-start(f32[4,512]{1,0:T(4,128)} %refs_5_.1) | copy-start | bytes 24580
  0.7 17.8 %copy-start.1 = (f32[4,512]{1,0:T(4,128)S(1)}, f32[4,512]{1,0:T(4,128)}, u32[]{:S(2)}) copy-start(f32[4,512]{1,0:T(4,128)} %refs_6_.1) | copy-start | bytes 24580
  0.7 17.8 %copy-start.2 = (f32[4,512]{1,0:T(4,128)S(1)}, f32[4,512]{1,0:T(4,128)}, u32[]{:S(2)}) copy-start(f32[4,512]{1,0:T(4,128)} %refs_7_.1) | copy-start | bytes 24580
  2.1 9.4 %collective-permute-start = (bf16[1040,128]{1,0:T(8,128)(2,1)S(1)}, bf16[1040,128]{1,0:T(8,128)(2,1)S(1)}, u32[]{:S(2)}, u32[]{:S(2)}) collective-permute-start(bf16[1040,128]{1,0:T(8,128)(2,1)S(1)} %get-tuple-element.66), channel_id=1, source_target_pairs={{0,1},{1,0},{2,3},{3,2},{4,5},{5,4},{6,7},{7,6},{8,9},{9,8},{10,11... | collective-permute-start | bytes 798728 | tf_op jit(solution)/shard_map/ppermute | solution.py:685
  5.1 9.3 %collective-permute-start.1 = (bf16[1040,128]{1,0:T(8,128)(2,1)S(1)}, bf16[1040,128]{1,0:T(8,128)(2,1)S(1)}, u32[]{:S(2)}, u32[]{:S(2)}) collective-permute-start(bf16[1040,128]{1,0:T(8,128)(2,1)S(1)} %get-tuple-element.67), channel_id=1, source_target_pairs={{0,2},{1,3},{2,0},{3,1},{4,6},{5,7},{6,4},{7,5},{8,10},{9,11},{10,... | collective-permute-start | bytes 798728 | tf_op jit(solution)/shard_map/ppermute | solution.py:685
  6.7 11.8 %collective-permute-start.2 = (bf16[1040,128]{1,0:T(8,128)(2,1)S(1)}, bf16[1040,128]{1,0:T(8,128)(2,1)S(1)}, u32[]{:S(2)}, u32[]{:S(2)}) collective-permute-start(bf16[1040,128]{1,0:T(8,128)(2,1)S(1)} %get-tuple-element.68), channel_id=1, source_target_pairs={{0,3},{1,2},{2,1},{3,0},{4,7},{5,6},{6,5},{7,4},{8,11},{9,10},{10,... | collective-permute-start | bytes 798728 | tf_op jit(solution)/shard_map/ppermute | solution.py:685
  6.7 1.3 %collective-permute-start.3 = (bf16[3,8,128]{2,1,0:T(8,128)(2,1)S(1)}, bf16[3,8,128]{2,1,0:T(8,128)(2,1)S(1)}, u32[]{:S(2)}, u32[]{:S(2)}) collective-permute-start(bf16[3,8,128]{2,1,0:T(8,128)(2,1)S(1)} %get-tuple-element.69), channel_id=1, source_target_pairs={{3,4},{11,12},{19,20},{27,28}} | collective-permute-start | bytes 18440 | tf_op jit(solution)/shard_map/ppermute | solution.py:738
  7.3 1.4 %collective-permute-start.4 = (bf16[3,8,128]{2,1,0:T(8,128)(2,1)S(1)}, bf16[3,8,128]{2,1,0:T(8,128)(2,1)S(1)}, u32[]{:S(2)}, u32[]{:S(2)}) collective-permute-start(bf16[3,8,128]{2,1,0:T(8,128)(2,1)S(1)} %get-tuple-element.70), channel_id=1, source_target_pairs={{3,5},{11,13},{19,21},{27,29}} | collective-permute-start | bytes 18440 | tf_op jit(solution)/shard_map/ppermute | solution.py:738
  8.0 1.4 %collective-permute-start.5 = (bf16[3,8,128]{2,1,0:T(8,128)(2,1)S(1)}, bf16[3,8,128]{2,1,0:T(8,128)(2,1)S(1)}, u32[]{:S(2)}, u32[]{:S(2)}) collective-permute-start(bf16[3,8,128]{2,1,0:T(8,128)(2,1)S(1)} %get-tuple-element.71), channel_id=1, source_target_pairs={{3,6},{11,14},{19,22},{27,30}} | collective-permute-start | bytes 18440 | tf_op jit(solution)/shard_map/ppermute | solution.py:738
  8.7 0.7 %collective-permute-start.6 = (bf16[3,8,128]{2,1,0:T(8,128)(2,1)S(1)}, bf16[3,8,128]{2,1,0:T(8,128)(2,1)S(1)}, u32[]{:S(2)}, u32[]{:S(2)}) collective-permute-start(bf16[3,8,128]{2,1,0:T(8,128)(2,1)S(1)} %get-tuple-element.72), channel_id=1, source_target_pairs={{3,7},{11,15},{19,23},{27,31}} | collective-permute-start | bytes 18440 | tf_op jit(solution)/shard_map/ppermute | solution.py:738
  26.5 5.2 %collective-permute-start.7 = (f32[128,128]{1,0:T(8,128)S(1)}, f32[128,128]{1,0:T(8,128)S(1)}, u32[]{:S(2)}, u32[]{:S(2)}) collective-permute-start(f32[128,128]{1,0:T(8,128)S(1)} %get-tuple-element.91), channel_id=1, source_target_pairs={{0,4},{1,5},{2,6},{3,7},{4,0},{5,1},{6,2},{7,3},{8,12},{9,13},{10,... | collective-permute-start | bytes 196616 | tf_op jit(solution)/shard_map/ppermute | solution.py:749
  32.9 6.8 %collective-permute-start.9 = (f32[3,8,128]{2,1,0:T(8,128)S(1)}, f32[3,8,128]{2,1,0:T(8,128)S(1)}, u32[]{:S(2)}, u32[]{:S(2)}) collective-permute-start(f32[3,8,128]{2,1,0:T(8,128)S(1)} %get-tuple-element.98), channel_id=1, source_target_pairs={{4,0},{5,1},{6,2},{7,3},{12,8},{13,9},{14,10},{15,11},{20,16},{21,... | collective-permute-start | bytes 36872 | tf_op jit(solution)/shard_map/ppermute | solution.py:698
  37.9 4.2 %collective-permute-start.8 = (f32[16,512]{1,0:T(8,128)S(1)}, f32[16,512]{1,0:T(8,128)S(1)}, u32[]{:S(2)}, u32[]{:S(2)}) collective-permute-start(f32[16,512]{1,0:T(8,128)S(1)} %get-tuple-element.95), channel_id=1, source_target_pairs={{0,1},{1,0},{2,3},{3,2},{4,5},{5,4},{6,7},{7,6},{8,9},{9,8},{10,11... | collective-permute-start | bytes 98312 | tf_op jit(solution)/shard_map/ppermute | solution.py:717
  42.2 8.7 %collective-permute-start.12 = (bf16[1040,128]{1,0:T(8,128)(2,1)S(1)}, bf16[1040,128]{1,0:T(8,128)(2,1)S(1)}, u32[]{:S(2)}, u32[]{:S(2)}) collective-permute-start(bf16[1040,128]{1,0:T(8,128)(2,1)S(1)} %get-tuple-element.109), channel_id=1, source_target_pairs={{0,1},{1,0},{2,3},{3,2},{4,5},{5,4},{6,7},{7,6},{8,9},{9,8},{10,11... | collective-permute-start | bytes 798728 | tf_op jit(solution)/shard_map/ppermute | solution.py:685
  43.9 7.0 %collective-permute-start.13 = (bf16[1040,128]{1,0:T(8,128)(2,1)S(1)}, bf16[1040,128]{1,0:T(8,128)(2,1)S(1)}, u32[]{:S(2)}, u32[]{:S(2)}) collective-permute-start(bf16[1040,128]{1,0:T(8,128)(2,1)S(1)} %get-tuple-element.110), channel_id=1, source_target_pairs={{0,2},{1,3},{2,0},{3,1},{4,6},{5,7},{6,4},{7,5},{8,10},{9,11},{10,... | collective-permute-start | bytes 798728 | tf_op jit(solution)/shard_map/ppermute | solution.py:685
  45.5 10.8 %collective-permute-start.14 = (bf16[1040,128]{1,0:T(8,128)(2,1)S(1)}, bf16[1040,128]{1,0:T(8,128)(2,1)S(1)}, u32[]{:S(2)}, u32[]{:S(2)}) collective-permute-start(bf16[1040,128]{1,0:T(8,128)(2,1)S(1)} %get-tuple-element.113), channel_id=1, source_target_pairs={{0,3},{1,2},{2,1},{3,0},{4,7},{5,6},{6,5},{7,4},{8,11},{9,10},{10,... | collective-permute-start | bytes 798728 | tf_op jit(solution)/shard_map/ppermute | solution.py:685
  45.7 1.2 %collective-permute-start.10 = (f32[16,512]{1,0:T(8,128)S(1)}, f32[16,512]{1,0:T(8,128)S(1)}, u32[]{:S(2)}, u32[]{:S(2)}) collective-permute-start(f32[16,512]{1,0:T(8,128)S(1)} %add.18), channel_id=1, source_target_pairs={{0,8},{1,9},{2,10},{3,11},{4,12},{5,13},{6,14},{7,15},{8,0},{9,1},... | collective-permute-start | bytes 98312 | tf_op jit(solution)/shard_map/ppermute | solution.py:717
  46.9 3.9 %collective-permute-start.11 = (f32[16,512]{1,0:T(8,128)S(1)}, f32[16,512]{1,0:T(8,128)S(1)}, u32[]{:S(2)}, u32[]{:S(2)}) collective-permute-start(f32[16,512]{1,0:T(8,128)S(1)} %add.19), channel_id=1, source_target_pairs={{0,16},{1,17},{2,18},{3,19},{4,20},{5,21},{6,22},{7,23},{8,24},{9,... | collective-permute-start | bytes 98312 | tf_op jit(solution)/shard_map/ppermute | solution.py:717
  50.9 6.9 %collective-permute-start.17 = (f32[16,512]{1,0:T(8,128)S(1)}, f32[16,512]{1,0:T(8,128)S(1)}, u32[]{:S(2)}, u32[]{:S(2)}) collective-permute-start(f32[16,512]{1,0:T(8,128)S(1)} %add.20), channel_id=1, source_target_pairs={{0,6},{1,7},{2,4},{3,5},{4,2},{5,3},{6,0},{7,1},{8,14},{9,15},{10,... | collective-permute-start | bytes 98312 | tf_op jit(solution)/shard_map/ppermute | solution.py:717
  55.7 4.8 %collective-permute-start.16 = (f32[16,512]{1,0:T(8,128)S(1)}, f32[16,512]{1,0:T(8,128)S(1)}, u32[]{:S(2)}, u32[]{:S(2)}) collective-permute-start(f32[16,512]{1,0:T(8,128)S(1)} %add.20), channel_id=1, source_target_pairs={{0,4},{1,5},{2,6},{3,7},{4,0},{5,1},{6,2},{7,3},{8,12},{9,13},{10,... | collective-permute-start | bytes 98312 | tf_op jit(solution)/shard_map/ppermute | solution.py:717
  55.7 4.8 %collective-permute-start.15 = (f32[16,512]{1,0:T(8,128)S(1)}, f32[16,512]{1,0:T(8,128)S(1)}, u32[]{:S(2)}, u32[]{:S(2)}) collective-permute-start(f32[16,512]{1,0:T(8,128)S(1)} %add.20), channel_id=1, source_target_pairs={{0,2},{1,3},{2,0},{3,1},{4,6},{5,7},{6,4},{7,5},{8,10},{9,11},{10,... | collective-permute-start | bytes 98312 | tf_op jit(solution)/shard_map/ppermute | solution.py:717
